TPU v7x, 32 devices: a whole 2x2x4 slice. The times are simulated.
32 devices in a mesh: dp: 8 (over z, x), row: 2 (over y), col: 2 (over core).
Axes of the slice: x: 2, y: 2, z: 4, core: 2. Of those that a mesh axis runs over, the one named last changes fastest.
Arguments:
- tokens: bfloat16 [4096, 2048], P(('dp', 'col'), 'row'), may hold values from -30 to 30
- cotangent: bfloat16 [4096, 2048], P(('dp', 'col'), 'row'), may hold values from -6 to 6
- seq_lengths: int32 [8, 3], P('dp'), may hold values from 1 to 256, 512 in all within a row
- balance_order: int32 [8, 512], P('dp'), may hold values from 0 to 511, each once within a row
- attention_gain: bfloat16 [2048], P('row'), may hold values from 0.25 to 1.75
- query_weight: bfloat16 [2048, 2048], P('row', 'col'), may hold values from -0.125 to 0.125
- key_weight: bfloat16 [2048, 1024], P('row', 'col'), may hold values from -0.125 to 0.125
- value_projection: bfloat16 [2048, 1024], P('row', 'col'), may hold values from -0.125 to 0.125
- query_gain: bfloat16 [128], replicated, may hold values from 0.25 to 1.75
- key_norm_gain: bfloat16 [128], replicated, may hold values from 0.25 to 1.75
- output_weight: bfloat16 [2048, 2048], P('col', 'row'), may hold values from -1.5 to 1.5
- feedforward_gain: bfloat16 [2048], P('row'), may hold values from 0.25 to 1.75
- gate_weight: bfloat16 [2048, 6144], P('row', 'col'), may hold values from -0.125 to 0.125
- up_weight: bfloat16 [2048, 6144], P('row', 'col'), may hold values from -0.125 to 0.125
- down_weight: bfloat16 [6144, 2048], P('col', 'row'), may hold values from -0.109375 to 0.109375
Outputs:
- layer_out: float32 [4096, 2048], P(('dp', 'col'), 'row')
- input_grad: float32 [4096, 2048], P(('dp', 'col'), 'row')
- attention_gain_grad: float32 [2048], replicated
- query_weight_grad: float32 [2048, 2048], P(('row', 'dp'), 'col')
- key_weight_grad: float32 [2048, 1024], P(('row', 'dp'), 'col')
- value_weight_grad: float32 [2048, 1024], P(('row', 'dp'), 'col')
- query_gain_grad: float32 [128], replicated
- key_gain_grad: float32 [128], replicated
- output_weight_grad: float32 [2048, 2048], P(('col', 'dp'), 'row')
- feedforward_gain_grad: float32 [2048], replicated
- gate_weight_grad: float32 [2048, 6144], P(('row', 'dp'), 'col')
- up_weight_grad: float32 [2048, 6144], P(('row', 'dp'), 'col')
- down_weight_grad: float32 [6144, 2048], P(('col', 'dp'), 'row')
Inputs may be any that keep to these rules, and one draw needn't show every extreme that they name: `seq_lengths`: row d lists the lengths of the sequences of data group d in their order; each row sums to 512 and its largest entry is 256. `balance_order`: each row is a permutation of 0 to 511.
All inputs are finite; a program needn't handle non-finite values.
Results may differ from a plain program's by a relative error of at most 0.019.
Values may be sent and summed in bfloat16 or wider, within the bound.
No kernel may reach another device: no remote copies, remote signals or barrier semaphores. Data moves between devices by JAX's collectives and lax.ppermute only.
A program may use at most 192 MiB of HBM per device.

v0:
```python
import math

import jax
import jax.numpy as jnp
from jax import lax
from jax.sharding import PartitionSpec as P

D = 2048
HEAD_SIZE = 128


EPSILON = 1e-06
ROPE_BASE = 1000000.0
NEGATIVE = -1e30


def apply_rotary(values, token_position):
    half_width = values.shape[-1] // 2
    frequency = ROPE_BASE ** (-2.0 * jnp.arange(half_width, dtype=jnp.float32) / values.shape[-1])
    angles = token_position.astype(jnp.float32)[:, None] * frequency[None, :]
    cosine = jnp.cos(angles)[:, None, :]
    sine_part = jnp.sin(angles)[:, None, :]
    first_half = values[..., :half_width]
    second_half = values[..., half_width:]
    return jnp.concatenate(
        [
            first_half * cosine - second_half * sine_part,
            second_half * cosine + first_half * sine_part,
        ],
        axis=-1,
    )


def rotate_back(grads_in, token_position):
    half_width = grads_in.shape[-1] // 2
    frequency = ROPE_BASE ** (-2.0 * jnp.arange(half_width, dtype=jnp.float32) / grads_in.shape[-1])
    angles = token_position.astype(jnp.float32)[:, None] * frequency[None, :]
    cosine = jnp.cos(angles)[:, None, :]
    sine_part = jnp.sin(angles)[:, None, :]
    first_half = grads_in[..., :half_width]
    second_half = grads_in[..., half_width:]
    return jnp.concatenate(
        [
            first_half * cosine + second_half * sine_part,
            second_half * cosine - first_half * sine_part,
        ],
        axis=-1,
    )


def dot_plain(left_matrix, right_matrix):
    return jnp.dot(left_matrix, right_matrix, preferred_element_type=jnp.float32)


def dot_trans_right(left_matrix, right_matrix):
    return lax.dot_general(
        left_matrix, right_matrix, (((1,), (1,)), ((), ())), preferred_element_type=jnp.float32
    )


def dot_trans_left(left_matrix, right_matrix):
    return lax.dot_general(
        left_matrix, right_matrix, (((0,), (0,)), ((), ())), preferred_element_type=jnp.float32
    )


def feature_sum(values):
    return lax.psum(jnp.sum(values, axis=1), "row")


def col_rows(values):
    return lax.all_gather(values, "col", axis=0, tiled=True)


def row_rows(values):
    return lax.all_gather(values, "row", axis=0, tiled=True)


def row_sums(method, share_rows):
    return lax.psum_scatter(
        method(jnp.int32(0), lax.axis_size("row") * share_rows),
        "row",
        scatter_dimension=0,
        tiled=True,
    )


def col_sums(method, share_rows):
    return lax.psum_scatter(
        method(jnp.int32(0), lax.axis_size("col") * share_rows),
        "col",
        scatter_dimension=0,
        tiled=True,
    )


def head_norm(raw_values, head_count):
    shaped = raw_values.reshape(raw_values.shape[0], head_count, HEAD_SIZE)
    inverse = lax.rsqrt(jnp.mean(shaped * shaped, axis=-1, keepdims=True) + EPSILON)
    return (shaped * inverse, inverse)


def head_norm_back(grad_pre, unit_part, inverse, gain_vector):
    scaled_grad = grad_pre * gain_vector
    raw_grad = inverse * (
        scaled_grad - unit_part * jnp.mean(scaled_grad * unit_part, axis=-1, keepdims=True)
    )
    return (raw_grad.reshape(raw_grad.shape[0], -1), jnp.sum(grad_pre * unit_part, axis=(0, 1)))


def shards(
    tokens,
    cotangent,
    seq_lengths,
    balance_order,
    attention_gain,
    query_weight,
    key_weight,
    value_projection,
    query_gain,
    key_norm_gain,
    output_weight,
    feedforward_gain,
    gate_weight,
    up_weight,
    down_weight,
):
    row_count = lax.axis_size("row")
    col_count = lax.axis_size("col")
    row_index = lax.axis_index("row")
    half_rows = tokens.shape[0]
    group_members = half_rows * col_count
    row_share = group_members // row_count
    query_width = query_weight.shape[1]
    key_width = key_weight.shape[1]
    ff_width = gate_weight.shape[1]
    query_heads = query_width // HEAD_SIZE
    kv_heads = key_width // HEAD_SIZE
    repeat = query_heads // kv_heads
    scale_factor = 1.0 / math.sqrt(HEAD_SIZE)
    rows_per_block = min(512, row_share)
    block_count = row_share // rows_per_block
    moved_in, moved_grad = (
        lax.all_to_all(tokens, "dp", split_axis=0, concat_axis=0, tiled=True),
        lax.all_to_all(cotangent, "dp", split_axis=0, concat_axis=0, tiled=True),
    )
    slot_ids = jnp.arange(group_members, dtype=jnp.int32)
    picked = balance_order[0]
    returned = jnp.zeros((group_members,), jnp.int32).at[picked].set(slot_ids)
    lengths = seq_lengths[0]
    seq_ends = jnp.cumsum(lengths)
    starts = seq_ends - lengths
    segment = jnp.sum((slot_ids[:, None] >= seq_ends[None, :]).astype(jnp.int32), axis=1)
    seg_hits = segment[:, None] == jnp.arange(lengths.shape[0], dtype=jnp.int32)[None, :]
    token_position = slot_ids - jnp.sum(jnp.where(seg_hits, starts[None, :], 0), axis=1)
    seg_mine = lax.dynamic_slice_in_dim(segment, row_index * row_share, row_share)
    pos_mine = lax.dynamic_slice_in_dim(token_position, row_index * row_share, row_share)
    stream = moved_in.astype(jnp.float32)
    inverse_in = lax.rsqrt(feature_sum(stream * stream) / D + EPSILON)[:, None]
    unit_in = stream * inverse_in
    normed_layer_input = (unit_in * attention_gain).astype(jnp.bfloat16)
    normed_in_all = col_rows(normed_layer_input)
    normed_in_slots = normed_in_all[picked]

    def project_in(first_row, num_rows):
        return jnp.concatenate(
            [
                dot_plain(normed_in_slots, query_weight),
                dot_plain(normed_in_slots, key_weight),
                dot_plain(normed_in_slots, value_projection),
            ],
            axis=1,
        )

    projected = row_sums(project_in, row_share)
    query_unit, query_inverse = head_norm(projected[:, :query_width], query_heads)
    key_unit, key_inverse = head_norm(projected[:, query_width : query_width + key_width], kv_heads)
    value_mine = projected[:, query_width + key_width :].astype(jnp.bfloat16)
    query_rot = apply_rotary(query_unit * query_gain, pos_mine).astype(jnp.bfloat16)
    key_rot = (
        apply_rotary(key_unit * key_norm_gain, pos_mine)
        .astype(jnp.bfloat16)
        .reshape(row_share, key_width)
    )
    keys_all, values_all = (
        lax.all_gather(key_rot, "row", axis=0, tiled=True),
        lax.all_gather(value_mine, "row", axis=0, tiled=True),
    )
    keys_three = keys_all.reshape(group_members, kv_heads, HEAD_SIZE)
    values_three = values_all.reshape(group_members, kv_heads, HEAD_SIZE)
    query_blocks = query_rot.reshape(block_count, rows_per_block, query_width)
    seg_blocks = seg_mine.reshape(block_count, rows_per_block)
    pos_blocks = pos_mine.reshape(block_count, rows_per_block)
    block_ids = jnp.arange(block_count, dtype=jnp.int32)

    def masked_scores(query_row_block, seg_block, pos_block):
        grouped_heads = query_row_block.reshape(rows_per_block, kv_heads, repeat, HEAD_SIZE)
        scores = (
            jnp.einsum(
                "bkrd,tkd->krbt", grouped_heads, keys_three, preferred_element_type=jnp.float32
            )
            * scale_factor
        )
        allowed = (seg_block[:, None] == segment[None, :]) & (
            token_position[None, :] <= pos_block[:, None]
        )
        return (grouped_heads, jnp.where(allowed, scores, NEGATIVE))

    def attend(block_items):
        query_row_block, seg_block, pos_block, block_index = block_items
        grouped_heads, scores = masked_scores(query_row_block, seg_block, pos_block)
        row_top = jnp.max(scores, axis=-1, keepdims=True)
        exp_scores = jnp.exp(scores - row_top)
        row_total = jnp.sum(exp_scores, axis=-1, keepdims=True)
        prob_low = (exp_scores / row_total).astype(jnp.bfloat16)
        mixed_out = jnp.einsum(
            "krbt,tkd->bkrd", prob_low, values_three, preferred_element_type=jnp.float32
        )
        return (
            mixed_out.reshape(rows_per_block, query_width),
            (row_top + jnp.log(row_total))[..., 0],
        )

    mixed_all, log_totals = lax.map(attend, (query_blocks, seg_blocks, pos_blocks, block_ids))
    attention_mine = mixed_all.reshape(row_share, query_width).astype(jnp.bfloat16)
    attention_all = row_rows(attention_mine)
    attention_order = attention_all[returned]

    def project_out(first_row, num_rows):
        return dot_plain(attention_order, output_weight)

    stream_mid = stream + col_sums(project_out, half_rows)
    inverse_mid = lax.rsqrt(feature_sum(stream_mid * stream_mid) / D + EPSILON)[:, None]
    unit_mid = stream_mid * inverse_mid
    normed_mid = (unit_mid * feedforward_gain).astype(jnp.bfloat16)
    normed_mid_all = col_rows(normed_mid)

    def project_up(first_row, num_rows):
        return jnp.concatenate(
            [dot_plain(normed_mid_all, gate_weight), dot_plain(normed_mid_all, up_weight)], axis=1
        )

    gate_up = row_sums(project_up, row_share)
    gate_value = gate_up[:, :ff_width]
    up_value = gate_up[:, ff_width:]
    sigmoid_gate = jax.nn.sigmoid(gate_value)
    silu_gate = gate_value * sigmoid_gate
    activated = (silu_gate * up_value).astype(jnp.bfloat16)
    activated_all = row_rows(activated)

    def project_down(first_row, num_rows):
        return dot_plain(activated_all, down_weight)

    layer_out = stream_mid + col_sums(project_down, half_rows)
    upstream = moved_grad.astype(jnp.float32)
    upstream_all = col_rows(moved_grad)
    down_weight_grad = dot_trans_left(activated_all, upstream_all)

    def back_down(first_row, num_rows):
        return dot_trans_right(upstream_all, down_weight)

    act_grad = row_sums(back_down, row_share)
    gate_grad = (
        act_grad * up_value * sigmoid_gate * (1.0 + gate_value * (1.0 - sigmoid_gate))
    ).astype(jnp.bfloat16)
    up_grad = (act_grad * silu_gate).astype(jnp.bfloat16)
    gate_up_all = row_rows(jnp.concatenate([gate_grad, up_grad], axis=1))
    gate_weight_grad = dot_trans_left(normed_mid_all, gate_up_all[:, :ff_width])
    up_weight_grad = dot_trans_left(normed_mid_all, gate_up_all[:, ff_width:])

    def back_up(first_row, num_rows):
        return dot_trans_right(gate_up_all[:, :ff_width], gate_weight) + dot_trans_right(
            gate_up_all[:, ff_width:], up_weight
        )

    normed_mid_grad = col_sums(back_up, half_rows)
    weighted_mid = normed_mid_grad * feedforward_gain
    stream_mid_grad = upstream + inverse_mid * (
        weighted_mid - unit_mid * feature_sum(weighted_mid * unit_mid)[:, None] / D
    )
    feedforward_part = jnp.sum(normed_mid_grad * unit_mid, axis=0)
    branch_grad = stream_mid_grad.astype(jnp.bfloat16)
    branch_grad_all = col_rows(branch_grad)
    output_weight_grad = dot_trans_left(attention_order, branch_grad_all)
    branch_grad_slots = branch_grad_all[picked]

    def back_out(first_row, num_rows):
        return dot_trans_right(branch_grad_slots, output_weight)

    attention_grad = row_sums(back_out, row_share).astype(jnp.bfloat16)

    def attend_back(running, block_items):
        key_acc, value_acc = running
        query_row_block, seg_block, pos_block, total_block, grad_block, block_index = block_items
        grouped_heads, scores = masked_scores(query_row_block, seg_block, pos_block)
        prob_full = jnp.exp(scores - total_block[..., None])
        grad_out = grad_block.reshape(rows_per_block, kv_heads, repeat, HEAD_SIZE)
        prob_grad = jnp.einsum(
            "bkrd,tkd->krbt", grad_out, values_three, preferred_element_type=jnp.float32
        )
        centre = jnp.sum(prob_full * prob_grad, axis=-1, keepdims=True)
        score_grad = (prob_full * (prob_grad - centre)).astype(jnp.bfloat16)
        query_grad = (
            jnp.einsum("krbt,tkd->bkrd", score_grad, keys_three, preferred_element_type=jnp.float32)
            * scale_factor
        )
        key_acc = (
            key_acc
            + jnp.einsum(
                "krbt,bkrd->tkd", score_grad, grouped_heads, preferred_element_type=jnp.float32
            )
            * scale_factor
        )
        value_acc = value_acc + jnp.einsum(
            "krbt,bkrd->tkd",
            prob_full.astype(jnp.bfloat16),
            grad_out,
            preferred_element_type=jnp.float32,
        )
        return ((key_acc, value_acc), query_grad.reshape(rows_per_block, query_heads, HEAD_SIZE))

    zero_keys = jnp.zeros((group_members, kv_heads, HEAD_SIZE), jnp.float32)
    (key_acc, value_acc), query_rot_grad = lax.scan(
        attend_back,
        (zero_keys, zero_keys),
        (
            query_blocks,
            seg_blocks,
            pos_blocks,
            log_totals,
            attention_grad.reshape(block_count, rows_per_block, query_width),
            block_ids,
        ),
    )
    key_rot_grad, value_grad = (
        lax.psum_scatter(
            key_acc.reshape(group_members, key_width).astype(jnp.bfloat16),
            "row",
            scatter_dimension=0,
            tiled=True,
        ).astype(jnp.float32),
        lax.psum_scatter(
            value_acc.reshape(group_members, key_width).astype(jnp.bfloat16),
            "row",
            scatter_dimension=0,
            tiled=True,
        ).astype(jnp.float32),
    )
    query_pre_grad = rotate_back(
        query_rot_grad.reshape(row_share, query_heads, HEAD_SIZE), pos_mine
    )
    query_raw_grad, query_gain_part = head_norm_back(
        query_pre_grad, query_unit, query_inverse, query_gain
    )
    key_pre_grad = rotate_back(key_rot_grad.reshape(row_share, kv_heads, HEAD_SIZE), pos_mine)
    key_raw_grad, key_gain_part = head_norm_back(key_pre_grad, key_unit, key_inverse, key_norm_gain)
    projected_grad = jnp.concatenate(
        [
            query_raw_grad.astype(jnp.bfloat16),
            key_raw_grad.astype(jnp.bfloat16),
            value_grad.astype(jnp.bfloat16),
        ],
        axis=1,
    )
    projected_grad_all = row_rows(projected_grad)
    query_weight_grad = dot_trans_left(normed_in_slots, projected_grad_all[:, :query_width])
    key_weight_grad = dot_trans_left(
        normed_in_slots, projected_grad_all[:, query_width : query_width + key_width]
    )
    value_weight_grad = dot_trans_left(
        normed_in_slots, projected_grad_all[:, query_width + key_width :]
    )
    projected_grad_order = projected_grad_all[returned]

    def back_in(first_row, num_rows):
        return (
            dot_trans_right(projected_grad_order[:, :query_width], query_weight)
            + dot_trans_right(
                projected_grad_order[:, query_width : query_width + key_width], key_weight
            )
            + dot_trans_right(projected_grad_order[:, query_width + key_width :], value_projection)
        )

    normed_in_grad = col_sums(back_in, half_rows)
    weighted_in = normed_in_grad * attention_gain
    stream_grad = stream_mid_grad + inverse_in * (
        weighted_in - unit_in * feature_sum(weighted_in * unit_in)[:, None] / D
    )
    attention_part = jnp.sum(normed_in_grad * unit_in, axis=0)
    feature_start = row_index * attention_gain.shape[0]
    zero_vector = jnp.zeros((D,), jnp.float32)
    gain_totals = lax.psum(
        (
            lax.dynamic_update_slice_in_dim(zero_vector, attention_part, feature_start, 0),
            lax.dynamic_update_slice_in_dim(zero_vector, feedforward_part, feature_start, 0),
            query_gain_part,
            key_gain_part,
        ),
        ("dp", "row", "col"),
    )
    reduced = (
        lax.psum_scatter(
            query_weight_grad.astype(jnp.bfloat16), "dp", scatter_dimension=0, tiled=True
        ).astype(jnp.float32),
        lax.psum_scatter(
            key_weight_grad.astype(jnp.bfloat16), "dp", scatter_dimension=0, tiled=True
        ).astype(jnp.float32),
        lax.psum_scatter(
            value_weight_grad.astype(jnp.bfloat16), "dp", scatter_dimension=0, tiled=True
        ).astype(jnp.float32),
        lax.psum_scatter(
            output_weight_grad.astype(jnp.bfloat16), "dp", scatter_dimension=0, tiled=True
        ).astype(jnp.float32),
        lax.psum_scatter(
            gate_weight_grad.astype(jnp.bfloat16), "dp", scatter_dimension=0, tiled=True
        ).astype(jnp.float32),
        lax.psum_scatter(
            up_weight_grad.astype(jnp.bfloat16), "dp", scatter_dimension=0, tiled=True
        ).astype(jnp.float32),
        lax.psum_scatter(
            down_weight_grad.astype(jnp.bfloat16), "dp", scatter_dimension=0, tiled=True
        ).astype(jnp.float32),
    )
    out_back, grad_back = (
        lax.all_to_all(
            layer_out.astype(jnp.bfloat16), "dp", split_axis=0, concat_axis=0, tiled=True
        ).astype(layer_out.dtype),
        lax.all_to_all(
            stream_grad.astype(jnp.bfloat16), "dp", split_axis=0, concat_axis=0, tiled=True
        ).astype(stream_grad.dtype),
    )
    return (
        out_back,
        grad_back,
        gain_totals[0],
        reduced[0],
        reduced[1],
        reduced[2],
        gain_totals[2],
        gain_totals[3],
        reduced[3],
        gain_totals[1],
        reduced[4],
        reduced[5],
        reduced[6],
    )


def solution(mesh):
    placed = (
        P(("dp", "col"), "row"),
        P(("dp", "col"), "row"),
        P("dp", None),
        P("dp", None),
        P("row"),
        P("row", "col"),
        P("row", "col"),
        P("row", "col"),
        P(),
        P(),
        P("col", "row"),
        P("row"),
        P("row", "col"),
        P("row", "col"),
        P("col", "row"),
    )
    return jax.shard_map(
        shards,
        mesh=mesh,
        in_specs=placed,
        out_specs=(
            P(("dp", "col"), "row"),
            P(("dp", "col"), "row"),
            P(),
            P(("row", "dp"), "col"),
            P(("row", "dp"), "col"),
            P(("row", "dp"), "col"),
            P(),
            P(),
            P(("col", "dp"), "row"),
            P(),
            P(("row", "dp"), "col"),
            P(("row", "dp"), "col"),
            P(("col", "dp"), "row"),
        ),
        check_vma=False,
    )
```

profile of v0, /device:TPU:0, one launch (start us, length us, event | category | flops | bytes accessed | tf_op | source)
XLA Modules:
  0.0 1466.1 jit_solution(11175630094816987770)
XLA Ops:
  15.3 13.8 all-to-all-done
  59.2 53.1 %reduce-scatter.18.cloned.1.call-done = f32[256,2048]{1,0:T(8,128)} async-done(((f32[512,2048]{1,0:T(8,128)}), f32[256,2048]{1,0:T(8,128)}) %reduce-scatter.18.cloned.1.call-update) | async-done | bytes 2097168 | tf_op jit(solution)/shard_map/reduce_scatter | solution.py:80
  151.2 18.7 %all-gather.11.cloned.1.call-done = bf16[512,1024]{1,0:T(8,128)(2,1)} async-done(((bf16[256,1024]{1,0:T(8,128)(2,1)}), bf16[512,1024]{1,0:T(8,128)(2,1)}) %all-gather.11.cloned.1.call-update) | async-done | bytes 1048592 | tf_op jit(solution)/shard_map/all_gather | solution.py:76
  176.7 20.2 %all_to_all.39 = bf16[8,32,1024]{2,1,0:T(8,128)(2,1)} all-to-all(bf16[8,32,1024]{2,1,0:T(8,128)(2,1)} %bitcast.236), channel_id=1, replica_groups=mesh['dp'=8,'row'=2,'col'=2] {'dp'}, dimensions={0} | all-to-all | bytes 1048576 | tf_op jit(solution)/shard_map/all_to_all | solution.py:145
  216.4 9.3 fusion.74
  234.4 10.9 pad_maximum_fusion
  245.8 51.2 %reduce-scatter.26.cloned.1.call-done = f32[256,3072]{1,0:T(8,128)} async-done(((f32[512,3072]{1,0:T(8,128)}), f32[256,3072]{1,0:T(8,128)}) %reduce-scatter.26.cloned.1.call-update) | async-done | bytes 3145744 | tf_op jit(solution)/shard_map/reduce_scatter | solution.py:80
  297.0 146.9 %reduce-scatter.22.cloned.1.call-done = f32[256,6144]{1,0:T(8,128)} async-done(((f32[512,6144]{1,0:T(8,128)}), f32[256,6144]{1,0:T(8,128)}) %reduce-scatter.22.cloned.1.call-update) | async-done | bytes 6291472 | tf_op jit(solution)/shard_map/reduce_scatter | solution.py:80
  451.6 80.5 %all-gather.19.cloned.1.call-done = bf16[512,6144]{1,0:T(8,128)(2,1)} async-done(((bf16[256,6144]{1,0:T(8,128)(2,1)}), bf16[512,6144]{1,0:T(8,128)(2,1)}) %all-gather.19.cloned.1.call-update) | async-done | bytes 6291472 | tf_op jit(solution)/shard_map/all_gather | solution.py:76
  546.4 9.7 reduce-scatter.28.cloned.1.call-done
  565.9 10.3 all-gather.21.cloned.1.call-done
  587.8 30.4 %reduce-scatter.30.cloned.1.call-done = f32[256,1024]{1,0:T(8,128)} async-done(((f32[512,1024]{1,0:T(8,128)}), f32[256,1024]{1,0:T(8,128)}) %reduce-scatter.30.cloned.1.call-update) | async-done | bytes 1048592 | tf_op jit(solution)/shard_map/reduce_scatter | solution.py:80
  650.4 11.8 reduce-scatter.34.cloned.1.call-done
  665.0 32.4 %all-gather.23.cloned.1.call-done = bf16[512,2048]{1,0:T(8,128)(2,1)} async-done(((bf16[256,2048]{1,0:T(8,128)(2,1)}), bf16[512,2048]{1,0:T(8,128)(2,1)}) %all-gather.23.cloned.1.call-update) | async-done | bytes 2097168 | tf_op jit(solution)/shard_map/all_gather | solution.py:76
  712.5 32.0 %all-gather.15.cloned.1.call-done = bf16[512,3072]{1,0:T(8,128)(2,1)} async-done(((bf16[256,3072]{1,0:T(8,128)(2,1)}), bf16[512,3072]{1,0:T(8,128)(2,1)}) %all-gather.15.cloned.1.call-update) | async-done | bytes 3145744 | tf_op jit(solution)/shard_map/all_gather | solution.py:76
  801.7 19.5 %all_to_all.40 = bf16[8,32,1024]{2,1,0:T(8,128)(2,1)S(1)} all-to-all(bf16[8,32,1024]{2,1,0:T(8,128)(2,1)S(1)} %bitcast.232), channel_id=1, replica_groups=mesh['dp'=8,'row'=2,'col'=2] {'dp'}, dimensions={0} | all-to-all | bytes 1048576 | tf_op jit(solution)/shard_map/all_to_all | solution.py:428
  825.2 24.2 %reduce-scatter.44.cloned.1.call-done = bf16[128,1024]{1,0:T(8,128)(2,1)} async-done(((bf16[1024,1024]{1,0:T(8,128)(2,1)}), bf16[128,1024]{1,0:T(8,128)(2,1)}) %reduce-scatter.44.cloned.1.call-update) | async-done | bytes 262160 | tf_op jit(solution)/shard_map/reduce_scatter | solution.py:411
  851.2 118.4 %reduce-scatter.50.cloned.1.call-done = bf16[384,1024]{1,0:T(8,128)(2,1)} async-done(((bf16[3072,1024]{1,0:T(8,128)(2,1)}), bf16[384,1024]{1,0:T(8,128)(2,1)}) %reduce-scatter.50.cloned.1.call-update) | async-done | bytes 786448 | tf_op jit(solution)/shard_map/reduce_scatter | solution.py:420
  972.1 118.6 %reduce-scatter.46.cloned.1.call-done = bf16[128,3072]{1,0:T(8,128)(2,1)} async-done(((bf16[1024,3072]{1,0:T(8,128)(2,1)}), bf16[128,3072]{1,0:T(8,128)(2,1)}) %reduce-scatter.46.cloned.1.call-update) | async-done | bytes 786448 | tf_op jit(solution)/shard_map/reduce_scatter | solution.py:414
  1093.3 118.5 %reduce-scatter.48.cloned.1.call-done = bf16[128,3072]{1,0:T(8,128)(2,1)} async-done(((bf16[1024,3072]{1,0:T(8,128)(2,1)}), bf16[128,3072]{1,0:T(8,128)(2,1)}) %reduce-scatter.48.cloned.1.call-update) | async-done | bytes 786448 | tf_op jit(solution)/shard_map/reduce_scatter | solution.py:417
  1214.2 64.6 %reduce-scatter.40.cloned.1.call-done = bf16[128,512]{1,0:T(8,128)(2,1)} async-done(((bf16[1024,512]{1,0:T(8,128)(2,1)}), bf16[128,512]{1,0:T(8,128)(2,1)}) %reduce-scatter.40.cloned.1.call-update) | async-done | bytes 131088 | tf_op jit(solution)/shard_map/reduce_scatter | solution.py:405
  1280.5 64.1 %reduce-scatter.42.cloned.1.call-done = bf16[128,512]{1,0:T(8,128)(2,1)} async-done(((bf16[1024,512]{1,0:T(8,128)(2,1)}), bf16[128,512]{1,0:T(8,128)(2,1)}) %reduce-scatter.42.cloned.1.call-update) | async-done | bytes 131088 | tf_op jit(solution)/shard_map/reduce_scatter | solution.py:408
  1346.3 68.9 %reduce-scatter.38.cloned.1.call-done = bf16[128,1024]{1,0:T(8,128)(2,1)} async-done(((bf16[1024,1024]{1,0:T(8,128)(2,1)}), bf16[128,1024]{1,0:T(8,128)(2,1)}) %reduce-scatter.38.cloned.1.call-update) | async-done | bytes 262160 | tf_op jit(solution)/shard_map/reduce_scatter | solution.py:402
  1417.0 39.9 %all-reduce = (f32[2048]{0:T(1024)}, f32[128]{0:T(128)}, f32[128]{0:T(128)}, f32[2048]{0:T(1024)}) all-reduce(f32[2048]{0:T(1024)S(1)} %dynamic_update_slice.15, f32[128]{0:T(128)S(1)} %bitcast_reduce_fusion, f32[128]{0:T(128)S(1)} %bitcast_reduce_fusion.1, ...), channel_id=1, replica_groups=mesh['dp'=8,'row'=2,'col'=2] {'dp','row','col'}, use_global_device_ids=true, to_apply=%region_30.31 | all-reduce | flops 4352 | bytes 34816 | tf_op jit(solution)/shard_map/psum | solution.py:392
  (311 shorter events, 282.9 us)
Async XLA Ops:
  14.6 29.5 %all-gather.9.cloned.1.call-start = ((), (), s32[]{:S(2)}) async-start(), calls=%async_computation.21 | async-start | bytes 1572864 | tf_op jit(solution)/shard_map/all_gather | solution.py:72
  35.9 76.4 %reduce-scatter.18.cloned.1.call-start = ((), (), s32[]{:S(2)}) async-start(), calls=%async_computation.22 | async-start | bytes 6291456 | tf_op jit(solution)/shard_map/reduce_scatter | solution.py:80
  56.6 113.3 %all-gather.11.cloned.1.call-start = ((), (), s32[]{:S(2)}) async-start(), calls=%async_computation.23 | async-start | bytes 1572864 | tf_op jit(solution)/shard_map/all_gather | solution.py:76
  148.5 48.5 %reduce-scatter.20.cloned.1.call-start = ((), (), s32[]{:S(2)}) async-start(), calls=%async_computation.24 | async-start | bytes 3145728 | tf_op jit(solution)/shard_map/reduce_scatter | solution.py:89
  204.5 92.4 %reduce-scatter.26.cloned.1.call-start = ((), (), s32[]{:S(2)}) async-start(), calls=%async_computation.30 | async-start | bytes 9437184 | tf_op jit(solution)/shard_map/reduce_scatter | solution.py:80
  213.8 230.1 %reduce-scatter.22.cloned.1.call-start = ((), (), s32[]{:S(2)}) async-start(), calls=%async_computation.26 | async-start | bytes 18874368 | tf_op jit(solution)/shard_map/reduce_scatter | solution.py:80
  245.3 286.7 %all-gather.19.cloned.1.call-start = ((), (), s32[]{:S(2)}) async-start(), calls=%async_computation.31 | async-start | bytes 9437184 | tf_op jit(solution)/shard_map/all_gather | solution.py:76
  451.5 104.6 %reduce-scatter.28.cloned.1.call-start = ((), (), s32[]{:S(2)}) async-start(), calls=%async_computation.32 | async-start | bytes 3145728 | tf_op jit(solution)/shard_map/reduce_scatter | solution.py:89
  546.4 29.9 %all-gather.21.cloned.1.call-start = ((), (), s32[]{:S(2)}) async-start(), calls=%async_computation.33 | async-start | bytes 1572864 | tf_op jit(solution)/shard_map/all_gather | solution.py:72
  565.9 52.3 %reduce-scatter.30.cloned.1.call-start = ((), (), s32[]{:S(2)}) async-start(), calls=%async_computation.34 | async-start | bytes 3145728 | tf_op jit(solution)/shard_map/reduce_scatter | solution.py:80
  585.0 59.9 %reduce-scatter.32.cloned.1.call-start = ((), (), s32[]{:S(2)}) async-start(), calls=%async_computation.35 | async-start | bytes 786432 | tf_op jit(solution)/shard_map/reduce_scatter | solution.py:336
  630.2 32.0 %reduce-scatter.34.cloned.1.call-start = ((), (), s32[]{:S(2)}) async-start(), calls=%async_computation.36 | async-start | bytes 786432 | tf_op jit(solution)/shard_map/reduce_scatter | solution.py:342
  639.3 58.2 %all-gather.23.cloned.1.call-start = ((), (), s32[]{:S(2)}) async-start(), calls=%async_computation.37 | async-start | bytes 3145728 | tf_op jit(solution)/shard_map/all_gather | solution.py:76
  664.2 80.3 %all-gather.15.cloned.1.call-start = ((), (), s32[]{:S(2)}) async-start(), calls=%async_computation.27 | async-start | bytes 4718592 | tf_op jit(solution)/shard_map/all_gather | solution.py:76
  664.8 127.1 %reduce-scatter.36.cloned.1.call-start = ((), (), s32[]{:S(2)}) async-start(), calls=%async_computation.38 | async-start | bytes 3145728 | tf_op jit(solution)/shard_map/reduce_scatter | solution.py:89
  712.5 86.3 %reduce-scatter.24.cloned.1.call-start = ((), (), s32[]{:S(2)}) async-start(), calls=%async_computation.28 | async-start | bytes 3145728 | tf_op jit(solution)/shard_map/reduce_scatter | solution.py:89
  753.1 96.3 %reduce-scatter.44.cloned.1.call-start = ((), (), s32[]{:S(2)}) async-start(), calls=%async_computation.42 | async-start | bytes 2359296 | tf_op jit(solution)/shard_map/reduce_scatter | solution.py:411
  755.9 213.8 %reduce-scatter.50.cloned.1.call-start = ((), (), s32[]{:S(2)}) async-start(), calls=%async_computation.45 | async-start | bytes 7077888 | tf_op jit(solution)/shard_map/reduce_scatter | solution.py:420
  764.2 326.5 %reduce-scatter.46.cloned.1.call-start = ((), (), s32[]{:S(2)}) async-start(), calls=%async_computation.43 | async-start | bytes 7077888 | tf_op jit(solution)/shard_map/reduce_scatter | solution.py:414
  772.8 439.0 %reduce-scatter.48.cloned.1.call-start = ((), (), s32[]{:S(2)}) async-start(), calls=%async_computation.44 | async-start | bytes 7077888 | tf_op jit(solution)/shard_map/reduce_scatter | solution.py:417
  780.2 498.6 %reduce-scatter.40.cloned.1.call-start = ((), (), s32[]{:S(2)}) async-start(), calls=%async_computation.40 | async-start | bytes 1179648 | tf_op jit(solution)/shard_map/reduce_scatter | solution.py:405
  784.8 559.7 %reduce-scatter.42.cloned.1.call-start = ((), (), s32[]{:S(2)}) async-start(), calls=%async_computation.41 | async-start | bytes 1179648 | tf_op jit(solution)/shard_map/reduce_scatter | solution.py:408
  787.9 627.4 %reduce-scatter.38.cloned.1.call-start = ((), (), s32[]{:S(2)}) async-start(), calls=%async_computation.39 | async-start | bytes 2359296 | tf_op jit(solution)/shard_map/reduce_scatter | solution.py:402
  821.3 636.8 %all-to-all-start.1 = ((bf16[8,32,1024]{2,1,0:T(8,128)(2,1)}), bf16[8,32,1024]{2,1,0:T(8,128)(2,1)S(1)}, u32[]{:S(2)}, u32[]{:S(2)}) async-start(bf16[8,32,1024]{2,1,0:T(8,128)(2,1)} %bitcast.231), calls=%async_computation.5 | async-start | bytes 1048576 | tf_op jit(solution)/shard_map/all_to_all | solution.py:425
  (63 other events, 1290.3 us)
Sparse Core Ops, SparseCore 0:
  36.0 8.1 all-gather.8
  56.7 55.5 reduce-scatter.17
  148.6 21.2 all-gather.10
  176.8 9.5 reduce-scatter.19
  206.2 10.1 all-gather.12
  218.7 78.2 reduce-scatter.25
  299.4 144.4 reduce-scatter.21
  451.6 80.3 all-gather.18
  546.5 9.5 reduce-scatter.27
  566.0 10.1 all-gather.20
  585.1 32.9 reduce-scatter.29
  630.3 14.5 reduce-scatter.31
  647.6 14.5 reduce-scatter.33
  664.3 33.1 all-gather.22
  699.5 44.9 all-gather.14
  746.7 9.5 reduce-scatter.35
  758.4 10.7 reduce-scatter.23
  773.2 76.1 reduce-scatter.43
  853.2 116.3 reduce-scatter.49
  973.6 117.0 reduce-scatter.45
  1094.7 117.0 reduce-scatter.47
  1216.2 62.5 reduce-scatter.39
  1282.1 62.3 reduce-scatter.41
  1348.5 66.7 reduce-scatter.37
  (1 shorter events, 7.1 us)
where the time goes:
time: 1480 us; the launch traced here: 1470 us
  waiting for transfers between devices  1080 us (73%)
  blocking collectives  116 us (8%)
  matrix products  116 us (8%)
  other arithmetic  73.3 us (5%)
  local copies, waits for them, and re-layouts  51.9 us (4%)
  between operations  15.4 us (1%)
    reduce_scatter x4, waiting for transfers between devices, row_sums(): lax.psum_scatter(method(jnp.int32(0), lax.axis_size('row') * share_rows),...  282 us
    all_gather x4, waiting for transfers between devices, row_rows(): return lax.all_gather(values, 'row', axis=0, tiled=True)  164 us
    reduce_scatter x1, waiting for transfers between devices, shards(): lax.psum_scatter(gate_weight_grad.astype(jnp.bfloat16), 'dp', scatter_dim...  119 us
    reduce_scatter x1, waiting for transfers between devices, shards(): lax.psum_scatter(up_weight_grad.astype(jnp.bfloat16), 'dp', scatter_dimen...  119 us
    reduce_scatter x1, waiting for transfers between devices, shards(): lax.psum_scatter(down_weight_grad.astype(jnp.bfloat16), 'dp', scatter_dim...  118 us
    reduce_scatter x1, waiting for transfers between devices, shards(): lax.psum_scatter(query_weight_grad.astype(jnp.bfloat16), 'dp', scatter_di...  68.9 us
    reduce_scatter x1, waiting for transfers between devices, shards(): lax.psum_scatter(key_weight_grad.astype(jnp.bfloat16), 'dp', scatter_dime...  64.6 us
    reduce_scatter x1, waiting for transfers between devices, shards(): lax.psum_scatter(value_weight_grad.astype(jnp.bfloat16), 'dp', scatter_di...  64.1 us
  transfers between devices with their start and end apart: 27, of which 22 were waited for; matrix products, arithmetic and copies ran while one was open for 10% of the time, Pallas kernels for 0%

commit v1 on v0

v1 whole, which is shorter than its diff:
```python
import math

import jax
import jax.numpy as jnp
from jax import lax
from jax.sharding import PartitionSpec as P

D = 2048
HEAD_SIZE = 128
EPSILON = 1e-06
ROPE_BASE = 1000000.0
NEGATIVE = -1e30
BF16 = jnp.bfloat16
F32 = jnp.float32


def dot_nn(left, right):
    return jnp.dot(left, right, preferred_element_type=F32)


def dot_nt(left, right):
    return lax.dot_general(left, right, (((1,), (1,)), ((), ())), preferred_element_type=F32)


def dot_tn(left, right):
    return lax.dot_general(left, right, (((0,), (0,)), ((), ())), preferred_element_type=F32)


def swap_row(value):
    return lax.ppermute(value, "row", [(0, 1), (1, 0)])


def swap_col(value):
    return lax.ppermute(value, "col", [(0, 1), (1, 0)])


def swap_dp(value, bit):
    count = lax.axis_size("dp")
    return lax.ppermute(value, "dp", [(i, i ^ bit) for i in range(count)])


def swap_z(value):
    return swap_dp(value, 2)


def rotary_tables(position):
    half = HEAD_SIZE // 2
    frequency = ROPE_BASE ** (-2.0 * jnp.arange(half, dtype=F32) / HEAD_SIZE)
    angles = position.astype(F32)[:, None] * frequency[None, :]
    return jnp.cos(angles)[:, None, :], jnp.sin(angles)[:, None, :]


def rotate(values, cosine, sine):
    half = values.shape[-1] // 2
    first, second = values[..., :half], values[..., half:]
    return jnp.concatenate(
        [first * cosine - second * sine, second * cosine + first * sine], axis=-1
    )


def head_norm(raw, heads):
    shaped = raw.reshape(raw.shape[0], heads, HEAD_SIZE)
    inverse = lax.rsqrt(jnp.mean(shaped * shaped, axis=-1, keepdims=True) + EPSILON)
    return shaped * inverse, inverse


def head_norm_back(grad_pre, unit, inverse, gain):
    scaled = grad_pre * gain
    raw = inverse * (scaled - unit * jnp.mean(scaled * unit, axis=-1, keepdims=True))
    return raw.reshape(raw.shape[0], -1), jnp.sum(grad_pre * unit, axis=(0, 1))


def pick(value, index, axis):
    return lax.dynamic_index_in_dim(value, index, axis, keepdims=False)


def scatter_stage(value, axis, bit):
    mine = (lax.axis_index("dp") // bit) % 2
    got = swap_dp(pick(value, 1 - mine, axis).astype(BF16), bit)
    return pick(value, mine, axis).astype(F32) + got.astype(F32)


def high_bits(count):
    bits, bit = [], 4
    while bit < count:
        bits.append(bit)
        bit *= 2
    return bits


def split_rows(value):
    count = lax.axis_size("dp")
    levels = count.bit_length() - 1
    return value.reshape((2,) * levels + (value.shape[0] // count,) + value.shape[1:])


def by_half(index, own, other):
    first = index == 0
    return jnp.where(first, own, other), jnp.where(first, other, own)


def shards(
    tokens,
    cotangent,
    seq_lengths,
    balance_order,
    attention_gain,
    query_weight,
    key_weight,
    value_projection,
    query_gain,
    key_norm_gain,
    output_weight,
    feedforward_gain,
    gate_weight,
    up_weight,
    down_weight,
):
    count = lax.axis_size("dp")
    dp_index = lax.axis_index("dp")
    row = lax.axis_index("row")
    col = lax.axis_index("col")
    zbit = (dp_index // 2) % 2
    xbit = dp_index % 2
    half = tokens.shape[0]
    group = 2 * half
    features = tokens.shape[1]
    query_part = query_weight.shape[1] // 2
    key_part = key_weight.shape[1] // 2
    heads = query_part // HEAD_SIZE
    kv_heads = key_part // HEAD_SIZE
    repeat = heads // kv_heads
    ff_half = gate_weight.shape[1]
    runs = count // 8
    run = 2 * ff_half // count
    ff_part = ff_half // 4
    scale = 1.0 / math.sqrt(HEAD_SIZE)

    def ff_pieces(weight, part, axis):
        pieces = [
            lax.dynamic_slice_in_dim(weight, ((part * runs + i) * 2 + zbit) * run, run, axis)
            for i in range(runs)
        ]
        return pieces[0] if runs == 1 else jnp.concatenate(pieces, axis=axis)

    moved_in = lax.all_to_all(tokens, "dp", split_axis=0, concat_axis=0, tiled=True)
    quarter_rows = features // 2
    send_up = jnp.concatenate(
        [
            ff_pieces(lax.dynamic_slice_in_dim(w, xbit * quarter_rows, quarter_rows, 0), 1 - row, 1)
            for w in (gate_weight, up_weight)
        ],
        axis=1,
    )
    got_up = swap_row(send_up)
    got_up_pair = swap_dp(got_up, 1)
    low_up, high_up = by_half(xbit, got_up, got_up_pair)
    own_up = jnp.concatenate([ff_pieces(w, row, 1) for w in (gate_weight, up_weight)], axis=1)
    up_all = jnp.concatenate([own_up, low_up, high_up], axis=0)

    moved_grad = lax.all_to_all(cotangent, "dp", split_axis=0, concat_axis=0, tiled=True)

    base_ids = jnp.arange(half, dtype=jnp.int32)
    local_ids = jnp.concatenate([col * half + base_ids, (1 - col) * half + base_ids])
    slot_ids = jnp.arange(group, dtype=jnp.int32)
    slot = jnp.sum(
        jnp.where(balance_order[0][None, :] == local_ids[:, None], slot_ids[None, :], 0), axis=1
    )
    lengths = seq_lengths[0]
    seq_ends = jnp.cumsum(lengths)
    starts = seq_ends - lengths
    segment = jnp.sum((slot[:, None] >= seq_ends[None, :]).astype(jnp.int32), axis=1)
    hits = segment[:, None] == jnp.arange(lengths.shape[0], dtype=jnp.int32)[None, :]
    position = slot - jnp.sum(jnp.where(hits, starts[None, :], 0), axis=1)
    cosine, sine = rotary_tables(position)
    allowed = (segment[:, None] == segment[None, :]) & (position[None, :] <= position[:, None])

    def head_columns(part):
        return jnp.concatenate(
            [
                lax.dynamic_slice_in_dim(query_weight, part * query_part, query_part, 1),
                lax.dynamic_slice_in_dim(key_weight, part * key_part, key_part, 1),
                lax.dynamic_slice_in_dim(value_projection, part * key_part, key_part, 1),
            ],
            axis=1,
        )

    heads_own = head_columns(row)
    heads_other = head_columns(1 - row)
    x_low = jnp.concatenate([moved_in, swap_col(moved_in)], axis=0)
    x_all = x_low.astype(F32)
    square = jnp.sum(x_all * x_all, axis=1)
    square = square + swap_row(square)
    inverse_in = lax.rsqrt(square / D + EPSILON)[:, None]
    scaled_in = (x_all * attention_gain).astype(BF16)
    got_heads = swap_row(dot_nn(scaled_in, heads_other).astype(BF16))
    projected = (dot_nn(scaled_in, heads_own) + got_heads.astype(F32)) * inverse_in

    query_unit, query_inverse = head_norm(projected[:, :query_part], heads)
    key_unit, key_inverse = head_norm(projected[:, query_part : query_part + key_part], kv_heads)
    values = projected[:, query_part + key_part :].astype(BF16).reshape(group, kv_heads, HEAD_SIZE)
    query_rot = rotate(query_unit * query_gain, cosine, sine).astype(BF16)
    query_rot = query_rot.reshape(group, kv_heads, repeat, HEAD_SIZE)
    key_rot = rotate(key_unit * key_norm_gain, cosine, sine).astype(BF16)
    scores = jnp.einsum("bkrd,tkd->krbt", query_rot, key_rot, preferred_element_type=F32) * scale
    scores = jnp.where(allowed, scores, NEGATIVE)
    top = jnp.max(scores, axis=-1, keepdims=True)
    exps = jnp.exp(scores - top)
    total = jnp.sum(exps, axis=-1, keepdims=True)
    prob = exps / total
    prob_low = prob.astype(BF16)
    attention = jnp.einsum("krbt,tkd->bkrd", prob_low, values, preferred_element_type=F32)
    attention = attention.reshape(group, query_part).astype(BF16)
    attention_all = jnp.concatenate(by_half(row, attention, swap_row(attention)), axis=1)
    out_part = dot_nn(attention_all, output_weight)
    stream = x_all[:half]
    stream_mid = stream + out_part[:half] + swap_col(out_part[half:].astype(BF16)).astype(F32)

    square_mid = jnp.sum(stream_mid * stream_mid, axis=1)
    square_mid = square_mid + swap_row(square_mid)
    inverse_mid = lax.rsqrt(square_mid / D + EPSILON)[:, None]
    unit_mid = stream_mid * inverse_mid
    normed_mid = (unit_mid * feedforward_gain).astype(BF16)

    quarter = half // 2
    by_row = swap_row(normed_mid)
    by_z = swap_z(normed_mid)
    diagonal = jnp.concatenate([swap_row(by_z[:quarter]), swap_z(by_row[quarter:])], axis=0)
    near = jnp.concatenate([normed_mid, by_row], axis=1)
    far = jnp.concatenate([by_z, diagonal], axis=1)
    mid_all = jnp.concatenate([near, swap_col(near), far, swap_col(far)], axis=0)

    grad_z = swap_z(moved_grad)
    grad_col = swap_col(jnp.concatenate([moved_grad, grad_z], axis=0))
    grad_all = jnp.concatenate([moved_grad, grad_col[:half], grad_z, grad_col[half:]], axis=0)

    down_own = ff_pieces(down_weight, row, 0)
    down_other = ff_pieces(down_weight, 1 - row, 0)
    got_act = swap_row(dot_nt(grad_all, down_other).astype(BF16))
    act_grad = dot_nt(grad_all, down_own) + got_act.astype(F32)

    gate_up = dot_nn(mid_all, up_all)
    gate_value = gate_up[:, :ff_part]
    up_value = gate_up[:, ff_part:]
    sigmoid_gate = jax.nn.sigmoid(gate_value)
    silu_gate = gate_value * sigmoid_gate
    activated = (silu_gate * up_value).astype(BF16)
    gate_grad = act_grad * up_value * sigmoid_gate * (1.0 + gate_value * (1.0 - sigmoid_gate))
    up_grad = act_grad * silu_gate
    gate_up_grad = jnp.concatenate([gate_grad.astype(BF16), up_grad.astype(BF16)], axis=1)

    mid_part = dot_nt(gate_up_grad, up_all)
    got_mid = swap_col(
        jnp.concatenate([mid_part[half:group], mid_part[group + half :]], axis=0).astype(BF16)
    ).astype(F32)
    near_part = mid_part[:half] + got_mid[:half]
    far_part = mid_part[group : group + half] + got_mid[half:]
    to_row = near_part[:, features:]
    to_z = far_part[:, :features]
    to_both = far_part[:, features:].astype(BF16)
    via_row = swap_row(to_both[:quarter]).astype(F32)
    via_z = swap_z(to_both[quarter:]).astype(F32)
    to_z = jnp.concatenate([to_z[:quarter] + via_row, to_z[quarter:]], axis=0)
    to_row = jnp.concatenate([to_row[:quarter], to_row[quarter:] + via_z], axis=0)
    normed_mid_grad = (
        near_part[:, :features]
        + swap_row(to_row.astype(BF16)).astype(F32)
        + swap_z(to_z.astype(BF16)).astype(F32)
    )

    activated_all = jnp.concatenate(by_half(row, activated, swap_row(activated)), axis=1)
    down_pair = jnp.concatenate(by_half(row, down_own, down_other), axis=0)
    out_ff = dot_nn(activated_all, down_pair)
    out_ff = out_ff[:group] + swap_z(out_ff[group:].astype(BF16)).astype(F32)
    layer_out = stream_mid + out_ff[:half] + swap_col(out_ff[half:].astype(BF16)).astype(F32)

    def reduce_high(value, axis):
        for bit in reversed(high_bits(count)):
            value = scatter_stage(value, axis, bit)
        return value

    down_grad = split_units(dot_tn(activated_all, grad_all).astype(BF16), count)
    down_grad = scatter_stage(down_grad, down_grad.ndim - 3, 1)
    down_grad = reduce_high(down_grad, 0)

    def up_weight_rows(grad_part):
        whole = dot_tn(mid_all, grad_part).astype(BF16)
        levels = count.bit_length() - 1
        value = whole.reshape((2,) * (levels + 1) + (features // count, ff_part))
        value = scatter_stage(value, value.ndim - 3, 1)
        value = reduce_high(value, 1)
        own, other = value[0], value[1]
        got = swap_row(other.astype(BF16)).astype(F32)
        keep = [pick(part, zbit, 0) for part in (own, got)]
        sent = jnp.stack([pick(part, 1 - zbit, 0) for part in (own, got)]).astype(BF16)
        swapped = swap_z(sent).astype(F32)
        table = []
        for near_piece, far_piece in zip(by_half(row, keep[0], keep[1]), by_half(row, swapped[0], swapped[1])):
            table.append(by_half(zbit, near_piece, far_piece))
        return jnp.concatenate(
            [
                table[part][z][:, i * run : (i + 1) * run]
                for part in range(2)
                for i in range(runs)
                for z in range(2)
            ],
            axis=1,
        )

    gate_weight_grad = up_weight_rows(gate_up_grad[:, :ff_part])
    up_weight_grad = up_weight_rows(gate_up_grad[:, ff_part:])

    upstream = moved_grad.astype(F32)
    weighted_mid = normed_mid_grad * feedforward_gain
    mid_sum = jnp.sum(weighted_mid * unit_mid, axis=1)
    mid_sum = (mid_sum + swap_row(mid_sum))[:, None]
    stream_mid_grad = upstream + inverse_mid * (weighted_mid - unit_mid * mid_sum / D)
    feedforward_part = jnp.sum(normed_mid_grad * unit_mid, axis=0)
    branch_low = stream_mid_grad.astype(BF16)
    branch = jnp.concatenate([branch_low, swap_col(branch_low)], axis=0)

    out_own = lax.dynamic_slice_in_dim(output_weight, row * query_part, query_part, 0)
    out_other = lax.dynamic_slice_in_dim(output_weight, (1 - row) * query_part, query_part, 0)
    got_attention = swap_row(dot_nt(branch, out_other).astype(BF16))
    attention_grad = (dot_nt(branch, out_own) + got_attention.astype(F32)).astype(BF16)

    def reduce_heads(value):
        value = split_rows(value)
        value = scatter_stage(value, value.ndim - 4, 2)
        value = scatter_stage(value, value.ndim - 3, 1)
        return reduce_high(value, 0)

    output_weight_grad = reduce_heads(dot_tn(attention_all, branch).astype(BF16))

    grad_out = attention_grad.reshape(group, kv_heads, repeat, HEAD_SIZE)
    prob_grad = jnp.einsum("bkrd,tkd->krbt", grad_out, values, preferred_element_type=F32)
    centre = jnp.sum(prob * prob_grad, axis=-1, keepdims=True)
    score_grad = (prob * (prob_grad - centre)).astype(BF16)
    query_rot_grad = (
        jnp.einsum("krbt,tkd->bkrd", score_grad, key_rot, preferred_element_type=F32) * scale
    )
    key_rot_grad = (
        jnp.einsum("krbt,bkrd->tkd", score_grad, query_rot, preferred_element_type=F32) * scale
    )
    value_grad = jnp.einsum("krbt,bkrd->tkd", prob_low, grad_out, preferred_element_type=F32)
    query_pre_grad = rotate(query_rot_grad.reshape(group, heads, HEAD_SIZE), cosine, -sine)
    query_raw_grad, query_gain_part = head_norm_back(
        query_pre_grad, query_unit, query_inverse, query_gain
    )
    key_pre_grad = rotate(key_rot_grad, cosine, -sine)
    key_raw_grad, key_gain_part = head_norm_back(key_pre_grad, key_unit, key_inverse, key_norm_gain)
    projected_grad = jnp.concatenate(
        [
            query_raw_grad.astype(BF16),
            key_raw_grad.astype(BF16),
            value_grad.reshape(group, key_part).astype(BF16),
        ],
        axis=1,
    )
    projected_other = swap_row(projected_grad)
    in_part = dot_nt(projected_grad, heads_own) + dot_nt(projected_other, heads_other)
    normed_in_grad = in_part[:half] + swap_col(in_part[half:].astype(BF16)).astype(F32)

    normed_in = (x_all * inverse_in * attention_gain).astype(BF16)
    heads_grad_own = reduce_heads(dot_tn(normed_in, projected_grad).astype(BF16))
    heads_grad_other = reduce_heads(dot_tn(normed_in, projected_other).astype(BF16))

    def head_grad(start, width):
        own = heads_grad_own[:, start : start + width]
        other = heads_grad_other[:, start : start + width]
        return jnp.concatenate(by_half(row, own, other), axis=1)

    query_weight_grad = head_grad(0, query_part)
    key_weight_grad = head_grad(query_part, key_part)
    value_weight_grad = head_grad(query_part + key_part, key_part)

    unit_in = stream * inverse_in[:half]
    weighted_in = normed_in_grad * attention_gain
    in_sum = jnp.sum(weighted_in * unit_in, axis=1)
    in_sum = (in_sum + swap_row(in_sum))[:, None]
    stream_grad = stream_mid_grad + inverse_in[:half] * (weighted_in - unit_in * in_sum / D)
    attention_part = jnp.sum(normed_in_grad * unit_in, axis=0)

    feature_start = row * features
    zero_vector = jnp.zeros((D,), F32)
    gain_totals = lax.psum(
        (
            lax.dynamic_update_slice_in_dim(zero_vector, attention_part, feature_start, 0),
            lax.dynamic_update_slice_in_dim(zero_vector, feedforward_part, feature_start, 0),
            query_gain_part,
            key_gain_part,
        ),
        ("dp", "row", "col"),
    )
    out_back = lax.all_to_all(
        layer_out.astype(BF16), "dp", split_axis=0, concat_axis=0, tiled=True
    ).astype(F32)
    grad_back = lax.all_to_all(
        stream_grad.astype(BF16), "dp", split_axis=0, concat_axis=0, tiled=True
    ).astype(F32)
    return (
        out_back,
        grad_back,
        gain_totals[0],
        query_weight_grad,
        key_weight_grad,
        value_weight_grad,
        gain_totals[2],
        gain_totals[3],
        output_weight_grad,
        gain_totals[1],
        gate_weight_grad,
        up_weight_grad,
        down_grad,
    )


def split_units(value, count):
    levels = count.bit_length() - 1
    return value.reshape((2,) * (levels - 1) + (2 * value.shape[0] // count, value.shape[1]))


def solution(mesh):
    placed = (
        P(("dp", "col"), "row"),
        P(("dp", "col"), "row"),
        P("dp", None),
        P("dp", None),
        P("row"),
        P("row", "col"),
        P("row", "col"),
        P("row", "col"),
        P(),
        P(),
        P("col", "row"),
        P("row"),
        P("row", "col"),
        P("row", "col"),
        P("col", "row"),
    )
    return jax.shard_map(
        shards,
        mesh=mesh,
        in_specs=placed,
        out_specs=(
            P(("dp", "col"), "row"),
            P(("dp", "col"), "row"),
            P(),
            P(("row", "dp"), "col"),
            P(("row", "dp"), "col"),
            P(("row", "dp"), "col"),
            P(),
            P(),
            P(("col", "dp"), "row"),
            P(),
            P(("row", "dp"), "col"),
            P(("row", "dp"), "col"),
            P(("col", "dp"), "row"),
        ),
        check_vma=False,
    )
```

time: 1480 us -> 602 us (0.41)
  waiting for transfers between devices: 1080 us -> 233 us
  blocking collectives: 116 us -> 46.4 us
  starting transfers between devices: 13.3 us -> 61.1 us
  matrix products: 116 us -> 98.2 us
  other arithmetic: 73.3 us -> 90.3 us
    reduce_scatter x17 -> x0, waiting for transfers between devices: 880 us -> none  [the longest x4 282 us: row_sums(): lax.psum_scatter(method(jnp.int32(0), lax.axis_size('row') * share_rows),...]
    ppermute x0 -> x50, waiting for transfers between devices: none -> 222 us  [the longest x24 133 us: swap_dp(): return lax.ppermute(value, 'dp', [(i, i ^ bit) for i in range(count)])]
    all_gather x8 -> x0, waiting for transfers between devices: 185 us -> none  [the longest x4 164 us: row_rows(): return lax.all_gather(values, 'row', axis=0, tiled=True)]
    ppermute x0 -> x50, starting transfers between devices: none -> 41 us  [the longest x24 22.7 us: swap_dp(): return lax.ppermute(value, 'dp', [(i, i ^ bit) for i in range(count)])]
    all_to_all x2 -> x0, blocking collectives: 39.7 us -> none  [the longest x1 20.2 us: shards(): lax.all_to_all(cotangent, 'dp', split_axis=0, concat_axis=0, tiled=True)]
    dot_general x27 -> x23, matrix products: 116 us -> 92.9 us  [the longest x7 40.3 us: dot_nt(): lax.dot_general(left, right, (((1,), (1,)), ((), ())), preferred_element_...]
    gather x4 -> x0, local copies, waits for them, and re-layouts: 20.9 us -> none  [the longest x1 7.19 us: shards(): projected_grad_order = projected_grad_all[returned]]
    psum x4 -> x0, blocking collectives: 19.8 us -> none  [feature_sum(): return lax.psum(jnp.sum(values, axis=1), 'row')]
  transfers between devices with their start and end apart: 27 -> 54, of which waited for: 22 -> 21; matrix products, arithmetic and copies ran while one was open for 10% -> 35% of each run, Pallas kernels for 0% -> 0%
where the time goes in v1:
time: 602 us; the launch traced here: 592 us
  waiting for transfers between devices  233 us (39%)
  matrix products  98.2 us (16%)
  other arithmetic  90.3 us (15%)
  starting transfers between devices  61.1 us (10%)
  local copies, waits for them, and re-layouts  59.9 us (10%)
  blocking collectives  46.4 us (8%)
    ppermute x24, waiting for transfers between devices, swap_dp(): return lax.ppermute(value, 'dp', [(i, i ^ bit) for i in range(count)])  133 us
    ppermute x17, waiting for transfers between devices, swap_row(): return lax.ppermute(value, 'row', [(0, 1), (1, 0)])  88.8 us
    psum x1, blocking collectives, shards(): lax.psum((lax.dynamic_update_slice_in_dim(zero_vector, attention_part, fe...  46.4 us
    dot_general x7, matrix products, dot_nt(): lax.dot_general(left, right, (((1,), (1,)), ((), ())), preferred_element_...  40.3 us
    dot_general x6, matrix products, dot_tn(): lax.dot_general(left, right, (((0,), (0,)), ((), ())), preferred_element_...  26.6 us
    ppermute x24, starting transfers between devices, swap_dp(): return lax.ppermute(value, 'dp', [(i, i ^ bit) for i in range(count)])  22.7 us
    add x15, other arithmetic, scatter_stage(): return pick(value, mine, axis).astype(F32) + got.astype(F32)  20.5 us
    dot_general x5, matrix products, dot_nn(): return jnp.dot(left, right, preferred_element_type=F32)  19.7 us
  transfers between devices with their start and end apart: 54, of which 21 were waited for; matrix products, arithmetic and copies ran while one was open for 35% of the time, Pallas kernels for 0%

profile of v1, /device:TPU:0, one launch (start us, length us, event | category | flops | bytes accessed | tf_op | source)
XLA Modules:
  0.0 592.2 jit_solution(12301752410442507420)
XLA Ops:
  0.7 7.4 %all-to-all-start = ((bf16[8,32,1024]{2,1,0:T(8,128)(2,1)}), bf16[8,32,1024]{2,1,0:T(8,128)(2,1)S(1)}, u32[]{:S(2)}, u32[]{:S(2)}) async-start(bf16[8,32,1024]{2,1,0:T(8,128)(2,1)} %bitcast.345), calls=%async_computation | async-start | bytes 1048576 | tf_op jit(solution)/shard_map/all_to_all | solution.py:146
  11.2 11.4 %all-to-all-done = bf16[8,32,1024]{2,1,0:T(8,128)(2,1)S(1)} async-done(((bf16[8,32,1024]{2,1,0:T(8,128)(2,1)}), bf16[8,32,1024]{2,1,0:T(8,128)(2,1)S(1)}, u32[]{:S(2)}, u32[]{:S(2)}) %all-to-all-start) | async-done | bytes 524320 | tf_op jit(solution)/shard_map/all_to_all | solution.py:146
  32.5 20.4 %collective-permute-done.2 = f32[512]{0:T(512)S(1)} collective-permute-done((f32[512]{0:T(512)S(1)}, f32[512]{0:T(512)S(1)}, u32[]{:S(2)}, u32[]{:S(2)}) %collective-permute-start.2) | collective-permute-done | bytes 2080 | tf_op jit(solution)/shard_map/ppermute | solution.py:30
  69.1 5.3 fusion.96
  102.1 30.6 %collective-permute-done.5 = f32[256]{0:T(256)S(1)} collective-permute-done((f32[256]{0:T(256)S(1)}, f32[256]{0:T(256)S(1)}, u32[]{:S(2)}, u32[]{:S(2)}) %collective-permute-start.5) | collective-permute-done | bytes 1056 | tf_op jit(solution)/shard_map/ppermute | solution.py:30
  162.8 5.0 convolution_convert_fusion.6
  168.8 5.8 collective-permute-done.13
  178.4 12.5 %fusion.24 = f32[1024,1536]{1,0:T(8,128)} fusion(bf16[512,1536]{1,0:T(8,128)(2,1)} %get-tuple-element.50, bf16[512,1536]{1,0:T(8,128)(2,1)} %get-tuple-element.49, bf16[1024,768]{1,0:T(8,128)(2,1)S(1)} %copy-done.57, bf16[1024,768]{1,0:T(8,128)(2,1)} %get-tuple-element.113, bf16[256,2048]{1,0:T(8,128)(2,1)} %collective-permute-done.11, ...), kind=kOutput, calls=%fused_computation.90 | convolution fusion | flops 6496976896 | bytes 16777216 | tf_op jit(solution)/shard_map/dot_general | solution.py:18
  190.9 13.6 %collective-permute-done.19 = bf16[1024,768]{1,0:T(8,128)(2,1)} collective-permute-done((bf16[1024,768]{1,0:T(8,128)(2,1)}, bf16[1024,768]{1,0:T(8,128)(2,1)}, u32[]{:S(2)}, u32[]{:S(2)}) %collective-permute-start.19) | collective-permute-done | bytes 1572896 | tf_op jit(solution)/shard_map/ppermute | solution.py:30
  204.5 8.3 %multiply_convert_fusion.1 = (bf16[1024,768]{1,0:T(8,128)(2,1)S(1)}, bf16[1024,768]{1,0:T(8,128)(2,1)S(1)}, bf16[1024,768]{1,0:T(8,128)(2,1)}) fusion(f32[1024,1536]{1,0:T(8,128)} %fusion.24, bf16[1024,768]{1,0:T(8,128)(2,1)} %collective-permute-done.19, bf16[3072,1024]{1,0:T(8,128)(2,1)} %param.29, s32[]{:T(128)S(6)} %select_n.349, ...), kind=kOutput, calls=%fused_computation.27 | convolution fusion | flops 1632370688 | bytes 16252932 | tf_op jit(solution)/shard_map/dot_general | solution.py:22
  213.8 8.4 %convolution_convert_fusion.1 = bf16[2048,768]{1,0:T(8,128)(2,1)S(1)} fusion(bf16[1024,768]{1,0:T(8,128)(2,1)S(1)} %get-tuple-element.33, bf16[256,2048]{1,0:T(8,128)(2,1)} %collective-permute-done.11, bf16[128,1024]{1,0:T(8,128)(2,1)} %collective-permute-done.10, bf16[128,1024]{1,0:T(8,128)(2,1)} %collective-permute-done.9, ...), kind=kOutput, calls=%fused_computation.11 | convolution fusion | flops 3252158464 | bytes 8912896 | tf_op jit(solution)/shard_map/dot_general | solution.py:26
  225.1 8.3 %convolution_convert_fusion.2 = bf16[2048,768]{1,0:T(8,128)(2,1)S(1)} fusion(bf16[1024,768]{1,0:T(8,128)(2,1)S(1)} %get-tuple-element.32, bf16[256,2048]{1,0:T(8,128)(2,1)} %collective-permute-done.11, bf16[128,1024]{1,0:T(8,128)(2,1)} %collective-permute-done.10, bf16[128,1024]{1,0:T(8,128)(2,1)} %collective-permute-done.9, ...), kind=kOutput, calls=%fused_computation.12 | convolution fusion | flops 3252158464 | bytes 8912896 | tf_op jit(solution)/shard_map/dot_general | solution.py:26
  235.5 20.2 %fusion.97 = (bf16[1024,2048]{1,0:T(8,128)(2,1)}, f32[1024,2048]{1,0:T(8,128)}) fusion(bf16[512,1536]{1,0:T(8,128)(2,1)} %get-tuple-element.50, bf16[512,1536]{1,0:T(8,128)(2,1)} %get-tuple-element.49, bf16[1024,768]{1,0:T(8,128)(2,1)S(1)} %copy-done.58, bf16[1024,768]{1,0:T(8,128)(2,1)S(1)} %copy-done.59, bf16[1024,768]{1,0:T(8,128)(2,1)} %copy-done.111, ...), kind=kOutput, calls=%fused_computation.312 | convolution fusion | flops 6476005376 | bytes 22020096 | tf_op jit(solution)/shard_map/dot_general | solution.py:22
  270.3 24.7 %collective-permute-done.40 = bf16[2,2,2,128,768]{4,3,2,0,1:T(8,128)(2,1)} collective-permute-done((bf16[2,2,2,128,768]{4,3,2,0,1:T(8,128)(2,1)S(1)}, bf16[2,2,2,128,768]{4,3,2,0,1:T(8,128)(2,1)}, u32[]{:S(2)}, u32[]{:S(2)}) %collective-permute-start.40) | collective-permute-done | bytes 1572896 | tf_op jit(solution)/shard_map/ppermute | solution.py:39
  309.4 15.2 %collective-permute-done.45 = bf16[2,2,128,768]{3,2,1,0:T(8,128)(2,1)} collective-permute-done((bf16[2,2,128,768]{3,2,1,0:T(8,128)(2,1)}, bf16[2,2,128,768]{3,2,1,0:T(8,128)(2,1)}, u32[]{:S(2)}, u32[]{:S(2)}) %collective-permute-start.45) | collective-permute-done | bytes 786464 | tf_op jit(solution)/shard_map/ppermute | solution.py:39
  327.0 13.7 %collective-permute-done.41 = bf16[2,2,128,768]{3,2,1,0:T(8,128)(2,1)} collective-permute-done((bf16[2,2,128,768]{3,2,1,0:T(8,128)(2,1)}, bf16[2,2,128,768]{3,2,1,0:T(8,128)(2,1)}, u32[]{:S(2)}, u32[]{:S(2)}) %collective-permute-start.41) | collective-permute-done | bytes 786464 | tf_op jit(solution)/shard_map/ppermute | solution.py:39
  343.2 12.2 %collective-permute-done.21 = bf16[128,1024]{1,0:T(8,128)(2,1)S(1)} collective-permute-done((bf16[128,1024]{1,0:T(8,128)(2,1)S(1)}, bf16[128,1024]{1,0:T(8,128)(2,1)S(1)}, u32[]{:S(2)}, u32[]{:S(2)}) %collective-permute-start.21) | collective-permute-done | bytes 262176 | tf_op jit(solution)/shard_map/ppermute | solution.py:39
  359.8 7.4 %collective-permute-done.42 = bf16[2,128,768]{2,1,0:T(8,128)(2,1)S(1)} collective-permute-done((bf16[2,128,768]{2,1,0:T(8,128)(2,1)S(1)}, bf16[2,128,768]{2,1,0:T(8,128)(2,1)S(1)}, u32[]{:S(2)}, u32[]{:S(2)}) %collective-permute-start.42) | collective-permute-done | bytes 393248 | tf_op jit(solution)/shard_map/ppermute | solution.py:30
  367.4 5.5 collective-permute-done.22
  405.4 14.5 %collective-permute-done.49 = bf16[384,1024]{1,0:T(8,128)(2,1)} collective-permute-done((bf16[384,1024]{1,0:T(8,128)(2,1)}, bf16[384,1024]{1,0:T(8,128)(2,1)}, u32[]{:S(2)}, u32[]{:S(2)}) %collective-permute-start.49) | collective-permute-done | bytes 786464 | tf_op jit(solution)/shard_map/ppermute | solution.py:39
  462.4 8.3 %collective-permute-done.31 = bf16[2,2,128,1024]{3,2,0,1:T(8,128)(2,1)} collective-permute-done((bf16[2,2,128,1024]{3,2,0,1:T(8,128)(2,1)}, bf16[2,2,128,1024]{3,2,0,1:T(8,128)(2,1)}, u32[]{:S(2)}, u32[]{:S(2)}) %collective-permute-start.31) | collective-permute-done | bytes 1048608 | tf_op jit(solution)/shard_map/ppermute | solution.py:39
  492.3 26.6 %collective-permute-done.34 = bf16[2,2,128,1024]{3,2,0,1:T(8,128)(2,1)} collective-permute-done((bf16[2,2,128,1024]{3,2,0,1:T(8,128)(2,1)}, bf16[2,2,128,1024]{3,2,0,1:T(8,128)(2,1)}, u32[]{:S(2)}, u32[]{:S(2)}) %collective-permute-start.34) | collective-permute-done | bytes 1048608 | tf_op jit(solution)/shard_map/ppermute | solution.py:39
  525.2 46.4 %all-reduce = (f32[2048]{0:T(1024)}, f32[128]{0:T(128)}, f32[128]{0:T(128)}, f32[2048]{0:T(1024)}) all-reduce(f32[2048]{0:T(1024)S(1)} %dynamic_update_slice.6, f32[128]{0:T(128)S(1)} %bitcast_reduce_fusion, f32[128]{0:T(128)S(1)} %bitcast_reduce_fusion.1, ...), channel_id=1, replica_groups=mesh['dp'=8,'row'=2,'col'=2] {'dp','row','col'}, use_global_device_ids=true, to_apply=%region_16.17 | all-reduce | flops 4352 | bytes 34816 | tf_op jit(solution)/shard_map/psum | solution.py:386
  577.9 11.6 %collective-permute-done.36 = bf16[128,1024]{1,0:T(8,128)(2,1)S(1)} collective-permute-done((bf16[128,1024]{1,0:T(8,128)(2,1)}, bf16[128,1024]{1,0:T(8,128)(2,1)S(1)}, u32[]{:S(2)}, u32[]{:S(2)}) %collective-permute-start.36) | collective-permute-done | bytes 262176 | tf_op jit(solution)/shard_map/ppermute | solution.py:39
  (497 shorter events, 246.1 us)
Async XLA Ops:
  27.2 25.7 %collective-permute-start.1 = (bf16[512,1024]{1,0:T(8,128)(2,1)S(1)}, bf16[512,1024]{1,0:T(8,128)(2,1)S(1)}, u32[]{:S(2)}, u32[]{:S(2)}) collective-permute-start(bf16[512,1024]{1,0:T(8,128)(2,1)S(1)} %convolution_convert_fusion.7), channel_id=1, source_target_pairs={{0,2},{2,0},{1,3},{3,1},{4,6},{6,4},{5,7},{7,5},{8,10},{10,8},{9,1... | collective-permute-start | bytes 3145736 | tf_op jit(solution)/shard_map/ppermute | solution.py:30
  95.6 41.9 %collective-permute-start.12 = (bf16[512,1536]{1,0:T(8,128)(2,1)}, bf16[512,1536]{1,0:T(8,128)(2,1)}, u32[]{:S(2)}, u32[]{:S(2)}) collective-permute-start(bf16[512,1536]{1,0:T(8,128)(2,1)} %pad_maximum_fusion.9), channel_id=1, source_target_pairs={{0,2},{2,0},{1,3},{3,1},{4,6},{6,4},{5,7},{7,5},{8,10},{10,8},{9,1... | collective-permute-start | bytes 4718600 | tf_op jit(solution)/shard_map/ppermute | solution.py:30
  97.3 37.9 %collective-permute-start.17 = (bf16[256,1024]{1,0:T(8,128)(2,1)}, bf16[256,1024]{1,0:T(8,128)(2,1)}, u32[]{:S(2)}, u32[]{:S(2)}) collective-permute-start(bf16[256,1024]{1,0:T(8,128)(2,1)} %bitcast.19), channel_id=1, source_target_pairs={{0,8},{4,12},{8,0},{12,4},{16,24},{20,28},{24,16},{28,20},{1,9},{5... | collective-permute-start | bytes 1572872 | tf_op jit(solution)/shard_map/ppermute | solution.py:39
  101.0 31.7 %collective-permute-start.5 = (f32[256]{0:T(256)S(1)}, f32[256]{0:T(256)S(1)}, u32[]{:S(2)}, u32[]{:S(2)}) collective-permute-start(f32[256]{0:T(256)S(1)} %get-tuple-element.27), channel_id=1, source_target_pairs={{0,2},{2,0},{1,3},{3,1},{4,6},{6,4},{5,7},{7,5},{8,10},{10,8},{9,1... | collective-permute-start | bytes 3080 | tf_op jit(solution)/shard_map/ppermute | solution.py:30
  137.5 37.1 %collective-permute-start.13 = (bf16[512,1536]{1,0:T(8,128)(2,1)}, bf16[512,1536]{1,0:T(8,128)(2,1)}, u32[]{:S(2)}, u32[]{:S(2)}) collective-permute-start(bf16[512,1536]{1,0:T(8,128)(2,1)} %collective-permute-done.12), channel_id=1, source_target_pairs={{0,4},{4,0},{8,12},{12,8},{16,20},{20,16},{24,28},{28,24},{1,5},{5... | collective-permute-start | bytes 4718600 | tf_op jit(solution)/shard_map/ppermute | solution.py:39
  167.8 36.7 %collective-permute-start.19 = (bf16[1024,768]{1,0:T(8,128)(2,1)}, bf16[1024,768]{1,0:T(8,128)(2,1)}, u32[]{:S(2)}, u32[]{:S(2)}) collective-permute-start(bf16[1024,768]{1,0:T(8,128)(2,1)} %convolution_convert_fusion.6), channel_id=1, source_target_pairs={{0,2},{2,0},{1,3},{3,1},{4,6},{6,4},{5,7},{7,5},{8,10},{10,8},{9,1... | collective-permute-start | bytes 4718600 | tf_op jit(solution)/shard_map/ppermute | solution.py:30
  212.9 44.8 %collective-permute-start.14 = (bf16[1024,768]{1,0:T(8,128)(2,1)}, bf16[1024,768]{1,0:T(8,128)(2,1)}, u32[]{:S(2)}, u32[]{:S(2)}) collective-permute-start(bf16[1024,768]{1,0:T(8,128)(2,1)} %get-tuple-element.34), channel_id=1, source_target_pairs={{0,2},{2,0},{1,3},{3,1},{4,6},{6,4},{5,7},{7,5},{8,10},{10,8},{9,1... | collective-permute-start | bytes 4718600 | tf_op jit(solution)/shard_map/ppermute | solution.py:30
  223.7 42.8 %collective-permute-start.44 = (bf16[2,2,2,128,768]{4,3,2,0,1:T(8,128)(2,1)}, bf16[2,2,2,128,768]{4,3,2,0,1:T(8,128)(2,1)}, u32[]{:S(2)}, u32[]{:S(2)}) collective-permute-start(bf16[2,2,2,128,768]{4,3,2,0,1:T(8,128)(2,1)} %bitcast.312), channel_id=1, source_target_pairs={{0,4},{4,0},{8,12},{12,8},{16,20},{20,16},{24,28},{28,24},{1,5},{5... | collective-permute-start | bytes 4718600 | tf_op jit(solution)/shard_map/ppermute | solution.py:39
  233.8 61.3 %collective-permute-start.40 = (bf16[2,2,2,128,768]{4,3,2,0,1:T(8,128)(2,1)S(1)}, bf16[2,2,2,128,768]{4,3,2,0,1:T(8,128)(2,1)}, u32[]{:S(2)}, u32[]{:S(2)}) collective-permute-start(bf16[2,2,2,128,768]{4,3,2,0,1:T(8,128)(2,1)S(1)} %bitcast.343), channel_id=1, source_target_pairs={{0,4},{4,0},{8,12},{12,8},{16,20},{20,16},{24,28},{28,24},{1,5},{5... | collective-permute-start | bytes 4718600 | tf_op jit(solution)/shard_map/ppermute | solution.py:39
  257.6 46.6 %collective-permute-start.20 = (bf16[512,2048]{1,0:T(8,128)(2,1)S(1)}, bf16[512,2048]{1,0:T(8,128)(2,1)S(1)}, u32[]{:S(2)}, u32[]{:S(2)}) collective-permute-start(bf16[512,2048]{1,0:T(8,128)(2,1)S(1)} %pad_maximum_fusion.6), channel_id=1, source_target_pairs={{0,1},{1,0},{2,3},{3,2},{4,5},{5,4},{6,7},{7,6},{8,9},{9,8},{10,11... | collective-permute-start | bytes 6291464 | tf_op jit(solution)/shard_map/ppermute | solution.py:34
  265.9 111.2 %collective-permute-start.48 = (bf16[2,384,1024]{2,1,0:T(8,128)(2,1)}, bf16[2,384,1024]{2,1,0:T(8,128)(2,1)}, u32[]{:S(2)}, u32[]{:S(2)}) collective-permute-start(bf16[2,384,1024]{2,1,0:T(8,128)(2,1)} %dynamic-slice_bitcast_fusion), channel_id=1, source_target_pairs={{0,4},{4,0},{8,12},{12,8},{16,20},{20,16},{24,28},{28,24},{1,5},{5... | collective-permute-start | bytes 4718600 | tf_op jit(solution)/shard_map/ppermute | solution.py:39
  269.2 55.4 %collective-permute-start.45 = (bf16[2,2,128,768]{3,2,1,0:T(8,128)(2,1)}, bf16[2,2,128,768]{3,2,1,0:T(8,128)(2,1)}, u32[]{:S(2)}, u32[]{:S(2)}) collective-permute-start(bf16[2,2,128,768]{3,2,1,0:T(8,128)(2,1)} %fusion.40), channel_id=1, source_target_pairs={{0,16},{4,20},{8,24},{12,28},{16,0},{20,4},{24,8},{28,12},{1,17},{... | collective-permute-start | bytes 2359304 | tf_op jit(solution)/shard_map/ppermute | solution.py:39
  298.0 42.8 %collective-permute-start.41 = (bf16[2,2,128,768]{3,2,1,0:T(8,128)(2,1)}, bf16[2,2,128,768]{3,2,1,0:T(8,128)(2,1)}, u32[]{:S(2)}, u32[]{:S(2)}) collective-permute-start(bf16[2,2,128,768]{3,2,1,0:T(8,128)(2,1)} %fusion.39), channel_id=1, source_target_pairs={{0,16},{4,20},{8,24},{12,28},{16,0},{20,4},{24,8},{28,12},{1,17},{... | collective-permute-start | bytes 2359304 | tf_op jit(solution)/shard_map/ppermute | solution.py:39
  303.5 54.3 %collective-permute-start.15 = (bf16[512,1024]{1,0:T(8,128)(2,1)}, bf16[512,1024]{1,0:T(8,128)(2,1)}, u32[]{:S(2)}, u32[]{:S(2)}) collective-permute-start(bf16[512,1024]{1,0:T(8,128)(2,1)} %slice.424), channel_id=1, source_target_pairs={{0,8},{4,12},{8,0},{12,4},{16,24},{20,28},{24,16},{28,20},{1,9},{5... | collective-permute-start | bytes 3145736 | tf_op jit(solution)/shard_map/ppermute | solution.py:39
  307.9 47.4 %collective-permute-start.21 = (bf16[128,1024]{1,0:T(8,128)(2,1)S(1)}, bf16[128,1024]{1,0:T(8,128)(2,1)S(1)}, u32[]{:S(2)}, u32[]{:S(2)}) collective-permute-start(bf16[128,1024]{1,0:T(8,128)(2,1)S(1)} %get-tuple-element.86), channel_id=1, source_target_pairs={{0,8},{4,12},{8,0},{12,4},{16,24},{20,28},{24,16},{28,20},{1,9},{5... | collective-permute-start | bytes 786440 | tf_op jit(solution)/shard_map/ppermute | solution.py:39
  324.6 32.6 %collective-permute-start.23 = (bf16[128,1024]{1,0:T(8,128)(2,1)S(1)}, bf16[128,1024]{1,0:T(8,128)(2,1)S(1)}, u32[]{:S(2)}, u32[]{:S(2)}) collective-permute-start(bf16[128,1024]{1,0:T(8,128)(2,1)S(1)} %get-tuple-element.88), channel_id=1, source_target_pairs={{0,2},{2,0},{1,3},{3,1},{4,6},{6,4},{5,7},{7,5},{8,10},{10,8},{9,1... | collective-permute-start | bytes 786440 | tf_op jit(solution)/shard_map/ppermute | solution.py:30
  380.3 39.6 %collective-permute-start.49 = (bf16[384,1024]{1,0:T(8,128)(2,1)}, bf16[384,1024]{1,0:T(8,128)(2,1)}, u32[]{:S(2)}, u32[]{:S(2)}) collective-permute-start(bf16[384,1024]{1,0:T(8,128)(2,1)} %fusion.41), channel_id=1, source_target_pairs={{0,16},{4,20},{8,24},{12,28},{16,0},{20,4},{24,8},{28,12},{1,17},{... | collective-permute-start | bytes 2359304 | tf_op jit(solution)/shard_map/ppermute | solution.py:39
  384.7 68.7 %all-to-all-start.1 = ((bf16[8,32,1024]{2,1,0:T(8,128)(2,1)}), bf16[8,32,1024]{2,1,0:T(8,128)(2,1)}, u32[]{:S(2)}, u32[]{:S(2)}) async-start(bf16[8,32,1024]{2,1,0:T(8,128)(2,1)} %bitcast.342), calls=%async_computation.1 | async-start | bytes 1048576 | tf_op jit(solution)/shard_map/all_to_all | solution.py:395
  403.5 55.4 %collective-permute-start.37 = (bf16[2,2,128,1024]{3,2,0,1:T(8,128)(2,1)}, bf16[2,2,128,1024]{3,2,0,1:T(8,128)(2,1)}, u32[]{:S(2)}, u32[]{:S(2)}) collective-permute-start(bf16[2,2,128,1024]{3,2,0,1:T(8,128)(2,1)} %bitcast.314), channel_id=1, source_target_pairs={{0,8},{4,12},{8,0},{12,4},{16,24},{20,28},{24,16},{28,20},{1,9},{5... | collective-permute-start | bytes 3145736 | tf_op jit(solution)/shard_map/ppermute | solution.py:39
  478.6 40.3 %collective-permute-start.34 = (bf16[2,2,128,1024]{3,2,0,1:T(8,128)(2,1)}, bf16[2,2,128,1024]{3,2,0,1:T(8,128)(2,1)}, u32[]{:S(2)}, u32[]{:S(2)}) collective-permute-start(bf16[2,2,128,1024]{3,2,0,1:T(8,128)(2,1)} %bitcast.315), channel_id=1, source_target_pairs={{0,8},{4,12},{8,0},{12,4},{16,24},{20,28},{24,16},{28,20},{1,9},{5... | collective-permute-start | bytes 3145736 | tf_op jit(solution)/shard_map/ppermute | solution.py:39
  480.8 43.4 %collective-permute-start.39 = (bf16[128,1024]{1,0:T(8,128)(2,1)}, bf16[128,1024]{1,0:T(8,128)(2,1)S(1)}, u32[]{:S(2)}, u32[]{:S(2)}) collective-permute-start(bf16[128,1024]{1,0:T(8,128)(2,1)} %fusion.59), channel_id=1, source_target_pairs={{0,16},{4,20},{8,24},{12,28},{16,0},{20,4},{24,8},{28,12},{1,17},{... | collective-permute-start | bytes 786440 | tf_op jit(solution)/shard_map/ppermute | solution.py:39
  484.6 87.0 %collective-permute-start.33 = (bf16[128,1024]{1,0:T(8,128)(2,1)}, bf16[128,1024]{1,0:T(8,128)(2,1)}, u32[]{:S(2)}, u32[]{:S(2)}) collective-permute-start(bf16[128,1024]{1,0:T(8,128)(2,1)} %fusion.57), channel_id=1, source_target_pairs={{0,16},{4,20},{8,24},{12,28},{16,0},{20,4},{24,8},{28,12},{1,17},{... | collective-permute-start | bytes 786440 | tf_op jit(solution)/shard_map/ppermute | solution.py:39
  488.1 87.6 %all-to-all-start.3 = ((bf16[8,32,1024]{2,1,0:T(8,128)(2,1)}), bf16[8,32,1024]{2,1,0:T(8,128)(2,1)}, u32[]{:S(2)}, u32[]{:S(2)}) async-start(bf16[8,32,1024]{2,1,0:T(8,128)(2,1)} %bitcast.339), calls=%async_computation.3 | async-start | bytes 1048576 | tf_op jit(solution)/shard_map/all_to_all | solution.py:398
  522.8 50.7 %collective-permute-start.35 = (bf16[2,128,1024]{2,1,0:T(8,128)(2,1)}, bf16[2,128,1024]{2,1,0:T(8,128)(2,1)}, u32[]{:S(2)}, u32[]{:S(2)}) collective-permute-start(bf16[2,128,1024]{2,1,0:T(8,128)(2,1)} %fusion.44), channel_id=1, source_target_pairs={{0,4},{4,0},{8,12},{12,8},{16,20},{20,16},{24,28},{28,24},{1,5},{5... | collective-permute-start | bytes 1572872 | tf_op jit(solution)/shard_map/ppermute | solution.py:39
  (142 other events, 1623.3 us)

commit v2 on v1

v2 whole, which is shorter than its diff:
```python
import math

import jax
import jax.numpy as jnp
from jax import lax
from jax.experimental import pallas as pl
from jax.experimental.pallas import tpu as pltpu
from jax.sharding import PartitionSpec as P

D = 2048
HEAD_SIZE = 128
EPSILON = 1e-06
ROPE_BASE = 1000000.0
NEGATIVE = -1e30
EXTRA = 8
VMEM_LIMIT = 40 << 20
BF16 = jnp.bfloat16
F32 = jnp.float32


def dot_nn(left, right):
    return jnp.dot(left, right, preferred_element_type=F32)


def dot_nt(left, right):
    return lax.dot_general(left, right, (((1,), (1,)), ((), ())), preferred_element_type=F32)


def dot_tn(left, right):
    return lax.dot_general(left, right, (((0,), (0,)), ((), ())), preferred_element_type=F32)


def swap_row(value):
    return lax.ppermute(value, "row", [(0, 1), (1, 0)])


def swap_col(value):
    return lax.ppermute(value, "col", [(0, 1), (1, 0)])


def swap_dp(value, bit):
    count = lax.axis_size("dp")
    return lax.ppermute(value, "dp", [(i, i ^ bit) for i in range(count)])


def swap_z(value):
    return swap_dp(value, 2)


def rotary_tables(position):
    half = HEAD_SIZE // 2
    frequency = ROPE_BASE ** (-2.0 * jnp.arange(half, dtype=F32) / HEAD_SIZE)
    angles = position.astype(F32)[:, None] * frequency[None, :]
    cosine, sine = jnp.cos(angles), jnp.sin(angles)
    return jnp.concatenate([cosine, cosine], axis=1), jnp.concatenate([-sine, sine], axis=1)


def pick(value, index, axis):
    return lax.dynamic_index_in_dim(value, index, axis, keepdims=False)


def high_bits(count):
    bits, bit = [], 4
    while bit < count:
        bits.append(bit)
        bit *= 2
    return bits


def split_rows(value, levels):
    return value.reshape((2,) * levels + (value.shape[0] >> levels,) + value.shape[1:])


def two_rows(value):
    high = lax.reduce_precision(value, 8, 7)
    return [high.astype(BF16), (value - high).astype(BF16)]


def with_rows(values, rows):
    count = lax.axis_size("dp")
    width = values[0].shape[1]
    block = jnp.stack([jnp.pad(r, (0, width - r.shape[0])) for r in rows])
    block = jnp.pad(block, ((0, EXTRA - len(rows)), (0, 0)))
    shares = [value.reshape(count, -1, width) for value in values]
    block = jnp.broadcast_to(block[None], (count, EXTRA, width))
    return jnp.concatenate(shares + [block], axis=1)


def exchange(value):
    return lax.all_to_all(value, "dp", split_axis=0, concat_axis=0, tiled=True)


def after(value, *earlier):
    return lax.optimization_barrier((value,) + earlier)[0]


def together(*values):
    return lax.optimization_barrier(values)


class Line:
    def __init__(self, value):
        self.last = value

    def hold(self, *values):
        held = together(*values, self.last)[:-1]
        return held[0] if len(held) == 1 else held

    def passed(self, value):
        self.last = value
        return value


def by_half(index, own, other):
    first = index == 0
    return jnp.where(first, own, other), jnp.where(first, other, own)


TIMES = {
    "gate_and_up": 12.0,
    "gate_and_up_back": 7.0,
    "attend": 7.0,
    "attend_back": 12.0,
    "product_tn": 3.0,
    "product_nt": 3.0,
    "down_proj": 3.0,
    "heads_forward": 3.5,
    "heads_backward": 3.0,
    "mid_all": 2.5,
}


def light(name):
    amount = TIMES.get(name, 1.5) * 0.1
    return pl.CostEstimate(
        flops=int(amount * 1.15e9) + 1, bytes_accessed=int(amount * 3.69e6), transcendentals=0
    )


def params(grid_axes=1):
    return pltpu.CompilerParams(vmem_limit_bytes=VMEM_LIMIT)


def scalars(*values):
    return jnp.stack([jnp.asarray(v, jnp.int32) for v in values])


def lanes_of(sums):
    return jnp.broadcast_to(sums, (sums.shape[0], HEAD_SIZE)).T[:8]


def column_of(lanes):
    return lanes.T[:, :1]


def local_call(kernel, inputs, outputs, name):
    return pl.pallas_call(
        kernel,
        out_shape=[jax.ShapeDtypeStruct(shape, dtype) for shape, dtype in outputs],
        compiler_params=params(),
        cost_estimate=light(name),
        name=name,
    )(*inputs)


def grid_call(kernel, grid, picks, inputs, in_specs, out_specs, outputs, name):
    return pl.pallas_call(
        kernel,
        grid_spec=pltpu.PrefetchScalarGridSpec(
            num_scalar_prefetch=1, grid=(grid,), in_specs=in_specs, out_specs=out_specs
        ),
        out_shape=[jax.ShapeDtypeStruct(shape, dtype) for shape, dtype in outputs],
        compiler_params=params(),
        cost_estimate=light(name),
        name=name,
    )(picks, *inputs)


def assemble(shape, pieces, name):
    def kernel(*refs):
        for (first, column, piece), ref in zip(pieces, refs):
            rows, columns = piece.shape
            refs[-1][first : first + rows, column : column + columns] = ref[...]

    values = [piece for _, _, piece in pieces]
    return local_call(kernel, values, [(shape, values[0].dtype)], name)[0]


def product(left, right, kind, dtype, tile, part=0, size=None, block=0, rows=None):
    contract = {"nn": ((1,), (0,)), "nt": ((1,), (1,)), "tn": ((0,), (0,))}[kind]
    size = right.shape[0] if size is None else size
    rows = left.shape[0] if rows is None else rows
    if kind == "tn":
        shape, steps = (left.shape[1], right.shape[1]), left.shape[1] // tile
        specs = [
            pl.BlockSpec((rows, tile), lambda j, s: (block, j)),
            pl.BlockSpec((size, right.shape[1]), lambda j, s: (s[0], 0)),
        ]
        out = pl.BlockSpec((tile, shape[1]), lambda j, s: (j, 0))
    else:
        width = right.shape[1] if kind == "nn" else size
        shape, steps = (rows, width), width // tile
        if kind == "nn":
            right_spec = pl.BlockSpec((size, tile), lambda j, s: (s[0], j))
        else:
            right_spec = pl.BlockSpec(
                (tile, right.shape[1]), lambda j, s: (s[0] * (size // tile) + j, 0)
            )
        specs = [pl.BlockSpec((rows, left.shape[1]), lambda j, s: (block, 0)), right_spec]
        out = pl.BlockSpec((rows, tile), lambda j, s: (0, j))

    def kernel(picks, left_ref, right_ref, out_ref):
        out_ref[...] = lax.dot_general(
            left_ref[...], right_ref[...], (contract, ((), ())), preferred_element_type=F32
        ).astype(out_ref.dtype)

    return grid_call(
        kernel, steps, scalars(part), (left, right), specs, [out], [(shape, dtype)], "product_" + kind
    )[0]


def product_onto(left, right, part, size, own, tile, name):
    rows, width = own.shape
    half = rows // 2

    def kernel(picks, left_ref, right_ref, own_ref, kept_ref, sent_ref):
        total = own_ref[...] + dot_nn(left_ref[...], right_ref[...])
        kept_ref[...] = total[:half]
        sent_ref[...] = total[half:].astype(BF16)

    return grid_call(
        kernel,
        width // tile,
        scalars(part),
        (left, right, own),
        [
            pl.BlockSpec(left.shape, lambda j, s: (0, 0)),
            pl.BlockSpec((size, tile), lambda j, s: (s[0], j)),
            pl.BlockSpec((rows, tile), lambda j, s: (0, j)),
        ],
        [pl.BlockSpec((half, tile), lambda j, s: (0, j))] * 2,
        [((half, width), F32), ((half, width), BF16)],
        name,
    )


def heads_forward(scaled, query_weight, key_weight, value_weight, part, dtype):
    group, features = scaled.shape
    query_part, tile = query_weight.shape[1] // 2, key_weight.shape[1] // 2
    steps = query_part // tile

    def kernel(picks, x_ref, query_ref, key_ref, value_ref, out_ref):
        step = pl.program_id(0)
        for condition, ref in (
            (step < steps, query_ref),
            (step == steps, key_ref),
            (step == steps + 1, value_ref),
        ):

            @pl.when(condition)
            def _():
                out_ref[...] = dot_nn(x_ref[...], ref[...]).astype(out_ref.dtype)

    return grid_call(
        kernel,
        steps + 2,
        scalars(part),
        (scaled, query_weight, key_weight, value_weight),
        [
            pl.BlockSpec((group, features), lambda j, s: (0, 0)),
            pl.BlockSpec(
                (features, tile), lambda j, s: (0, s[0] * steps + jnp.minimum(j, steps - 1))
            ),
            pl.BlockSpec((features, tile), lambda j, s: (0, s[0])),
            pl.BlockSpec((features, tile), lambda j, s: (0, s[0])),
        ],
        [pl.BlockSpec((group, tile), lambda j, s: (0, j))],
        [((group, query_part + 2 * tile), dtype)],
        "heads_forward",
    )[0]


def heads_backward(grads, query_weight, key_weight, value_weight, part, own=None):
    group = grads.shape[0]
    half = group // 2
    features = query_weight.shape[0]
    query_part, key_part = query_weight.shape[1] // 2, key_weight.shape[1] // 2
    tile = features // 2

    def kernel(picks, grads_ref, query_ref, key_ref, value_ref, *refs):
        total = dot_nt(grads_ref[:, :query_part], query_ref[...])
        total += dot_nt(grads_ref[:, query_part : query_part + key_part], key_ref[...])
        total += dot_nt(grads_ref[:, query_part + key_part :], value_ref[...])
        if own is None:
            refs[0][...] = total
        else:
            total += refs[0][...]
            refs[1][...] = total[:half]
            refs[2][...] = total[half:].astype(BF16)

    whole = pl.BlockSpec((group, tile), lambda j, s: (0, j))
    split = pl.BlockSpec((half, tile), lambda j, s: (0, j))
    outputs = [((group, features), F32)]
    if own is not None:
        outputs = [((half, features), F32), ((half, features), BF16)]
    return grid_call(
        kernel,
        2,
        scalars(part),
        (grads, query_weight, key_weight, value_weight) + (() if own is None else (own,)),
        [
            pl.BlockSpec(grads.shape, lambda j, s: (0, 0)),
            pl.BlockSpec((tile, query_part), lambda j, s: (j, s[0])),
            pl.BlockSpec((tile, key_part), lambda j, s: (j, s[0])),
            pl.BlockSpec((tile, key_part), lambda j, s: (j, s[0])),
        ]
        + ([] if own is None else [whole]),
        [whole] if own is None else [split, split],
        outputs,
        "heads_backward",
    )


def up_kernel(picks, mid_ref, gate_ref, up_ref, *refs):
    parts = 4
    gate_parts, up_parts = refs[:parts], refs[parts : 2 * parts]
    kept_ref, *got_refs = refs[2 * parts : -3]
    gate_grad_ref, up_grad_ref, act_ref = refs[-3:]
    features = gate_ref.shape[0]
    share = gate_parts[0].shape[0]

    def columns(own_ref, part_refs):
        total = dot_nn(mid_ref[:, :features], own_ref[...])
        for i, ref in enumerate(part_refs):
            at = pl.multiple_of(features + picks[1 + i] * share, share)
            total += dot_nn(mid_ref[:, pl.ds(at, share)], ref[...])
        return total

    gate = columns(gate_ref, gate_parts)
    up = columns(up_ref, up_parts)
    got = jnp.concatenate([ref[...] for ref in got_refs], axis=0)
    act_grad = kept_ref[...] + got.astype(F32)
    sigmoid = jax.nn.sigmoid(gate)
    silu = gate * sigmoid
    act_ref[...] = (silu * up).astype(BF16)
    gate_grad_ref[...] = (act_grad * up * sigmoid * (1.0 + gate * (1.0 - sigmoid))).astype(BF16)
    up_grad_ref[...] = (act_grad * silu).astype(BF16)


def gate_and_up(mid, gate, up, base, pieces, places, kept, got):
    rows = mid.shape[0]
    features = gate.shape[0]
    width = kept.shape[1]
    tile = width // 3
    share = pieces[0][0].shape[0]

    def columns(height, first):
        return pl.BlockSpec((height, tile), lambda j, s: (0, first + j))

    own = pl.BlockSpec((features, tile), lambda j, s: (0, 3 * s[0] + j))
    return grid_call(
        up_kernel,
        3,
        scalars(base, *places),
        (mid, gate, up, *pieces[0], *pieces[1], kept, *got),
        [pl.BlockSpec(mid.shape, lambda j, s: (0, 0)), own, own]
        + [columns(share, 0)] * (2 * len(places))
        + [columns(rows, 0)]
        + [columns(g.shape[0], 0) for g in got],
        [columns(rows, 0)] * 3,
        [((rows, width), BF16)] * 3,
        "gate_and_up",
    )


def up_back_kernel(picks, gate_grad_ref, up_grad_ref, gate_ref, up_ref, *refs):
    *pieces, out_ref = refs
    count = len(pieces) // 2
    features = gate_ref.shape[0]
    share = pieces[0].shape[0]
    gate_grad, up_grad = gate_grad_ref[...], up_grad_ref[...]
    for i in range(features // (2 * share)):
        at = slice(i * 2 * share, (i + 1) * 2 * share)
        total = dot_nt(gate_grad, gate_ref[at, :]) + dot_nt(up_grad, up_ref[at, :])
        out_ref[:, at] = total.astype(out_ref.dtype)
    for i in range(count):
        total = dot_nt(gate_grad, pieces[i][...]) + dot_nt(up_grad, pieces[count + i][...])
        at = pl.multiple_of(features + picks[1 + i] * share, share)
        out_ref[:, pl.ds(at, share)] = total.astype(out_ref.dtype)


def gate_and_up_back(gate_grad, up_grad, block, gate, up, base, pieces, places, dtype):
    rows = gate_grad.shape[0] // 2
    width = gate_grad.shape[1]
    features = gate.shape[0]
    grads = pl.BlockSpec((rows, width), lambda j, s: (block, 0))
    own = pl.BlockSpec((features, width), lambda j, s: (0, s[0]))
    pieces = (*pieces[0], *pieces[1])
    piece = pl.BlockSpec(pieces[0].shape, lambda j, s: (0, 0))
    shape = (rows, features + len(places) * pieces[0].shape[0])
    return grid_call(
        up_back_kernel,
        1,
        scalars(base, *places),
        (gate_grad, up_grad, gate, up, *pieces),
        [grads, grads, own, own] + [piece] * len(pieces),
        [pl.BlockSpec(shape, lambda j, s: (0, 0))],
        [(shape, dtype)],
        "gate_and_up_back",
    )[0]


def in_place(weight):
    return pltpu.with_memory_space_constraint(weight, pltpu.MemorySpace.HBM)


def my_bit(bit):
    return (lax.axis_index("dp") // bit) % 2


def view(shape, columns=None, **at):
    at = {int(axis[1:]): place for axis, place in at.items()}
    parts, part = columns or (1, 0)
    last = len(shape) - 1
    block = tuple(
        None if axis in at else length // (parts if axis == last else 1)
        for axis, length in enumerate(shape)
    )
    return pl.BlockSpec(
        block,
        lambda j, s: tuple(
            s[at[axis]] if axis in at else (part if axis == last else 0)
            for axis in range(len(shape))
        ),
    )


def without(shape, *axes):
    return tuple(length for axis, length in enumerate(shape) if axis not in axes)


def take(value, axis, index, columns=None):
    shape = without(value.shape, axis)
    shape = shape[:-1] + (shape[-1] // (columns or (1, 0))[0],)

    def kernel(picks, in_ref, out_ref):
        out_ref[...] = in_ref[...].astype(BF16)

    return grid_call(
        kernel,
        1,
        scalars(index),
        (value,),
        [view(value.shape, columns, **{f"a{axis}": 0})],
        [view(shape)],
        [(shape, BF16)],
        "take",
    )[0]


def start_stage(value, axis, bit):
    return swap_dp(take(value, axis, 1 - my_bit(bit)), bit)


def end_stage(value, got, axis, bit, next_axis=None, next_index=None, columns=None):
    joined = got.shape
    side = {} if axis is None else {f"a{axis}": 0}
    mine = 0 if axis is None else my_bit(bit)
    if next_axis is None:

        def kernel(picks, value_ref, got_ref, out_ref):
            out_ref[...] = value_ref[...].astype(F32) + got_ref[...].astype(F32)

        return grid_call(
            kernel,
            1,
            scalars(mine),
            (value, got),
            [view(value.shape, **side), view(joined)],
            [view(joined)],
            [(joined, F32)],
            "join",
        )[0]
    shape = without(joined, next_axis)
    behind = next_axis + (1 if axis is not None and next_axis >= axis else 0)

    def kernel(picks, keep_ref, keep_got, send_ref, send_got, kept_ref, sent_ref):
        kept_ref[...] = keep_ref[...].astype(F32) + keep_got[...].astype(F32)
        sent_ref[...] = (send_ref[...].astype(F32) + send_got[...].astype(F32)).astype(BF16)

    return grid_call(
        kernel,
        1,
        scalars(mine, next_index, 1 - next_index),
        (value, got, value, got),
        [
            view(value.shape, columns, **side, **{f"a{behind}": 1}),
            view(joined, **{f"a{next_axis}": 1}),
            view(value.shape, columns, **side, **{f"a{behind}": 2}),
            view(joined, **{f"a{next_axis}": 2}),
        ],
        [view(shape)] * 2,
        [(shape, F32), (shape, BF16)],
        "join_and_split",
    )


def add_got(kept, got):
    def kernel(kept_ref, got_ref, out_ref):
        out_ref[...] = kept_ref[...].astype(F32) + got_ref[...].astype(F32)

    return local_call(kernel, (kept, got), [(kept.shape, F32)], "add_got")[0]


def split_top(own, other, row):
    mine = my_bit(lax.axis_size("dp") // 2) == row

    def kernel(picks, own_ref, other_ref, kept_ref, sent_ref):
        for first, second, flag in ((own_ref, other_ref, 1), (other_ref, own_ref, 0)):

            @pl.when(picks[0] == flag)
            def _():
                kept_ref[...] = first[...].astype(F32)
                sent_ref[...] = second[...].astype(BF16)

    spec = view(own.shape)
    return grid_call(
        kernel,
        1,
        scalars(mine),
        (own, other),
        [spec, spec],
        [spec, spec],
        [(own.shape, F32), (own.shape, BF16)],
        "split_top",
    )


def join_core_kernel(kept_ref, got_ref, own_ref, row_ref, z_ref, row_both_ref, z_both_ref):
    half, features = own_ref.shape
    quarter = half // 2
    near = kept_ref[:half, :] + got_ref[:half, :].astype(F32)
    far = kept_ref[half:, :] + got_ref[half:, :].astype(F32)
    own_ref[...] = near[:, :features]
    row_ref[...] = near[:, features:]
    z_ref[...] = far[:, :features]
    row_both_ref[...] = far[:quarter, features:].astype(BF16)
    z_both_ref[...] = far[quarter:, features:].astype(BF16)


def join_corner_kernel(row_ref, z_ref, via_row_ref, via_z_ref, to_row_ref, to_z_ref):
    quarter = via_row_ref.shape[0]
    to_row_ref[:quarter, :] = row_ref[:quarter, :].astype(BF16)
    to_row_ref[quarter:, :] = (row_ref[quarter:, :] + via_z_ref[...].astype(F32)).astype(BF16)
    to_z_ref[:quarter, :] = (z_ref[:quarter, :] + via_row_ref[...].astype(F32)).astype(BF16)
    to_z_ref[quarter:, :] = z_ref[quarter:, :].astype(BF16)


def norm_sums_kernel(*refs):
    parts = refs[:-6]
    base_ref, inverse_ref, gain_ref, grad_ref, sums_ref, gain_grad_ref = refs[-6:]
    grad = sum(part[...].astype(F32) for part in parts)
    unit = base_ref[...].astype(F32) * column_of(inverse_ref[...])
    along = grad * unit
    grad_ref[...] = grad
    sums_ref[...] = lanes_of(jnp.sum(along * gain_ref[...], axis=1, keepdims=True))
    gain_grad_ref[...] = jnp.sum(along, axis=0, keepdims=True)


def norm_sums(parts, base, inverse, gain):
    rows, features = base.shape
    return local_call(
        norm_sums_kernel,
        (*parts, base, inverse, gain),
        [((rows, features), F32), ((8, rows), F32), ((1, features), F32)],
        "norm_sums",
    )


def norm_grad_kernel(
    grad_ref, base_ref, inverse_ref, gain_ref, sums_ref, got_sums_ref, rest_ref, *out_refs
):
    inverse = column_of(inverse_ref[...])
    unit = base_ref[...].astype(F32) * inverse
    mean = column_of(sums_ref[...] + got_sums_ref[...]) * (1.0 / D)
    out = rest_ref[...].astype(F32) + inverse * (grad_ref[...] * gain_ref[...] - unit * mean)
    for out_ref in out_refs:
        out_ref[...] = out.astype(out_ref.dtype)


def norm_grad(grad, base, inverse, gain, sums, got_sums, rest, dtypes):
    return local_call(
        norm_grad_kernel,
        (grad, base, inverse, gain, sums, got_sums, rest),
        [(grad.shape, dtype) for dtype in dtypes],
        "norm_grad",
    )


def middle_kernel(x_ref, part_ref, got_ref, mid_ref, square_ref):
    mid = x_ref[...].astype(F32) + part_ref[...] + got_ref[...].astype(F32)
    mid_ref[...] = mid
    square_ref[...] = lanes_of(jnp.sum(mid * mid, axis=1, keepdims=True))


def normed_kernel(mid_ref, square_ref, got_ref, gain_ref, normed_ref, inverse_ref):
    inverse = lax.rsqrt((square_ref[...] + got_ref[...]) * (1.0 / D) + EPSILON)
    inverse_ref[...] = inverse
    unit = mid_ref[...].astype(F32) * column_of(inverse)
    normed_ref[...] = (unit * gain_ref[...]).astype(BF16)


def scaled_kernel(own_ref, got_ref, gain_ref, x_ref, scaled_ref, square_ref):
    half = own_ref.shape[0]
    for first, ref in ((0, own_ref), (half, got_ref)):
        at = slice(first, first + half)
        values = ref[...].astype(F32)
        x_ref[at, :] = ref[...]
        scaled_ref[at, :] = (values * gain_ref[...]).astype(BF16)
        square_ref[:, at] = lanes_of(jnp.sum(values * values, axis=1, keepdims=True))


def normed_in_kernel(x_ref, inverse_ref, gain_ref, normed_ref):
    unit = x_ref[...].astype(F32) * column_of(inverse_ref[...])
    normed_ref[...] = (unit * gain_ref[...]).astype(BF16)


def block_of(weight, block_row, block_column, shape):
    def kernel(picks, in_ref, out_ref):
        out_ref[...] = in_ref[...]

    return grid_call(
        kernel,
        1,
        scalars(block_row, block_column),
        (weight,),
        [pl.BlockSpec(shape, lambda j, s: (s[0], s[1]))],
        [pl.BlockSpec(shape, lambda j, s: (0, 0))],
        [(shape, BF16)],
        "block_of",
    )[0]


def side_kernel(*refs):
    kept_ref, sent_ref = refs[-2:]
    parts = (len(refs) - 2) // 2
    width = refs[0].shape[-1]
    for i in range(parts):
        total = refs[i][...].astype(F32) + refs[parts + i][...].astype(F32)
        at = slice(i * width, (i + 1) * width)
        kept_ref[:, :, at] = total[0]
        sent_ref[:, :, at] = total[1].astype(BF16)


def layer_out_kernel(mid_ref, kept_ref, got_ref, out_ref):
    out_ref[...] = (mid_ref[...] + kept_ref[...] + got_ref[...].astype(F32)).astype(BF16)


def out_near_kernel(kept_ref, got_ref, near_ref, far_ref):
    half = near_ref.shape[0]
    near_ref[...] = kept_ref[:half, :] + got_ref[:half, :].astype(F32)
    far_ref[...] = (kept_ref[half:, :] + got_ref[half:, :].astype(F32)).astype(BF16)


def turn(values, cosine, sine):
    return values * cosine + pltpu.roll(values, HEAD_SIZE // 2, 1) * sine


def unit_of(raw):
    inverse = lax.rsqrt(jnp.mean(raw * raw, axis=-1, keepdims=True) + EPSILON)
    return raw * inverse, inverse


def scores_to_prob(query_rot, key_rot, allowed):
    scores = dot_nt(query_rot, key_rot) * (1.0 / math.sqrt(HEAD_SIZE))
    scores = jnp.where(allowed, scores, NEGATIVE)
    exps = jnp.exp(scores - jnp.max(scores, axis=-1, keepdims=True))
    return exps * (1.0 / jnp.sum(exps, axis=-1, keepdims=True))


def head_inputs(own, got, inverse_in, width):
    raw = (own[...] + got[...].astype(F32)) * inverse_in
    return [raw[:, i * HEAD_SIZE : (i + 1) * HEAD_SIZE] for i in range(width // HEAD_SIZE)]


def attend_kernel(
    query_own, query_got, key_own, key_got, value_own, value_got, inverse_ref, cosine_ref,
    sine_ref, slot_ref, start_ref, across_ref, query_gain_ref, key_gain_ref, out_ref,
):
    inverse_in = column_of(inverse_ref[...])
    cosine, sine = cosine_ref[...], sine_ref[...]
    across = across_ref[...]
    (key_raw,) = head_inputs(key_own, key_got, inverse_in, HEAD_SIZE)
    (value,) = head_inputs(value_own, value_got, inverse_in, HEAD_SIZE)
    key_rot = turn(unit_of(key_raw)[0] * key_gain_ref[...], cosine, sine).astype(BF16)
    value = value.astype(BF16)
    slots, first = column_of(slot_ref[...]), column_of(start_ref[...])
    rows = out_ref.shape[0] // 2

    for block in range(2):
        at = slice(block * rows, (block + 1) * rows)
        allowed = (across <= slots[at]) & (across >= first[at])
        for i in range(query_own.shape[1] // HEAD_SIZE):
            head = slice(i * HEAD_SIZE, (i + 1) * HEAD_SIZE)
            raw = (query_own[at, head] + query_got[at, head].astype(F32)) * inverse_in[at]
            pre = unit_of(raw)[0] * query_gain_ref[...]
            query_rot = turn(pre, cosine_ref[at, :], sine_ref[at, :]).astype(BF16)
            prob = scores_to_prob(query_rot, key_rot, allowed).astype(BF16)
            out_ref[at, head] = dot_nn(prob, value).astype(BF16)


def attend_back_kernel(
    query_own, query_got, key_own, key_got, value_own, value_got, inverse_ref, cosine_ref,
    sine_ref, slot_ref, start_ref, across_ref, query_gain_ref, key_gain_ref, grad_own, grad_got,
    out_ref, gain_ref,
):
    step = pl.program_id(0)
    repeat = query_own.shape[1] // HEAD_SIZE
    kv_heads = out_ref.shape[1] // (query_own.shape[1] + 2 * HEAD_SIZE)
    scale = 1.0 / math.sqrt(HEAD_SIZE)
    inverse_in = column_of(inverse_ref[...])
    cosine, sine = cosine_ref[...], sine_ref[...]
    across = across_ref[...]
    allowed = (across <= column_of(slot_ref[...])) & (across >= column_of(start_ref[...]))
    query_gain, key_gain = query_gain_ref[...], key_gain_ref[...]

    @pl.when(step == 0)
    def _():
        gain_ref[...] = jnp.zeros_like(gain_ref)

    (key_raw,) = head_inputs(key_own, key_got, inverse_in, HEAD_SIZE)
    (value,) = head_inputs(value_own, value_got, inverse_in, HEAD_SIZE)
    key_unit, key_inverse = unit_of(key_raw)
    key_rot = turn(key_unit * key_gain, cosine, sine).astype(BF16)
    value = value.astype(BF16)

    def norm_back(rot_grad, unit, inverse, gain, at):
        pre = rot_grad * cosine - pltpu.roll(rot_grad, HEAD_SIZE // 2, 1) * sine
        gain_ref[at : at + 1, :] += jnp.sum(pre * unit, axis=0, keepdims=True)
        scaled = pre * gain
        return inverse * (scaled - unit * jnp.mean(scaled * unit, axis=-1, keepdims=True))

    key_grad = jnp.zeros(key_raw.shape, F32)
    value_grad = jnp.zeros(key_raw.shape, F32)
    for i, query_raw in enumerate(
        head_inputs(query_own, query_got, inverse_in, query_own.shape[1])
    ):
        at = slice(i * HEAD_SIZE, (i + 1) * HEAD_SIZE)
        query_unit, query_inverse = unit_of(query_raw)
        query_rot = turn(query_unit * query_gain, cosine, sine).astype(BF16)
        prob = scores_to_prob(query_rot, key_rot, allowed)
        grad_out = (grad_own[:, at] + grad_got[:, at].astype(F32)).astype(BF16)
        prob_grad = dot_nt(grad_out, value)
        centre = jnp.sum(prob * prob_grad, axis=-1, keepdims=True)
        score_grad = (prob * (prob_grad - centre)).astype(BF16)
        value_grad += dot_tn(prob.astype(BF16), grad_out)
        key_grad += dot_tn(score_grad, query_rot)
        query_grad = norm_back(
            dot_nn(score_grad, key_rot) * scale, query_unit, query_inverse, query_gain, 0
        )
        column = pl.multiple_of((step * repeat + i) * HEAD_SIZE, HEAD_SIZE)
        out_ref[:, pl.ds(column, HEAD_SIZE)] = query_grad.astype(BF16)
    key_grad = norm_back(key_grad * scale, key_unit, key_inverse, key_gain, 1)
    column = pl.multiple_of((kv_heads * repeat + step) * HEAD_SIZE, HEAD_SIZE)
    out_ref[:, pl.ds(column, HEAD_SIZE)] = key_grad.astype(BF16)
    column = pl.multiple_of((kv_heads * (repeat + 1) + step) * HEAD_SIZE, HEAD_SIZE)
    out_ref[:, pl.ds(column, HEAD_SIZE)] = value_grad.astype(BF16)


def attention_specs(group, kv_heads, repeat):
    def block(width, first):
        return pl.BlockSpec((group, width), lambda j: (0, first + j))

    def whole(rows, columns):
        return pl.BlockSpec((rows, columns), lambda j: (0, 0))

    query = block(repeat * HEAD_SIZE, 0)
    key = block(HEAD_SIZE, kv_heads * repeat)
    value = block(HEAD_SIZE, kv_heads * (repeat + 1))
    return [query, query, key, key, value, value] + [
        whole(8, group),
        whole(group, HEAD_SIZE),
        whole(group, HEAD_SIZE),
        whole(8, group),
        whole(8, group),
        whole(1, group),
        whole(1, HEAD_SIZE),
        whole(1, HEAD_SIZE),
    ]


def attend(own, got, shared, kv_heads, repeat):
    group = own.shape[0]
    width = kv_heads * repeat * HEAD_SIZE
    return pl.pallas_call(
        attend_kernel,
        grid=(kv_heads,),
        in_specs=attention_specs(group, kv_heads, repeat),
        out_specs=pl.BlockSpec((group, repeat * HEAD_SIZE), lambda j: (0, j)),
        out_shape=jax.ShapeDtypeStruct((group, width), BF16),
        compiler_params=pltpu.CompilerParams(vmem_limit_bytes=VMEM_LIMIT),
        cost_estimate=light("attend"),
        name="attend",
    )(own, got, own, got, own, got, *shared)


def attend_back(own, got, shared, grad_own, grad_got, kv_heads, repeat):
    group, width = own.shape
    grad_block = pl.BlockSpec((group, repeat * HEAD_SIZE), lambda j: (0, j))
    return pl.pallas_call(
        attend_back_kernel,
        grid=(kv_heads,),
        in_specs=attention_specs(group, kv_heads, repeat) + [grad_block, grad_block],
        out_specs=[
            pl.BlockSpec((group, width), lambda j: (0, 0)),
            pl.BlockSpec((2, HEAD_SIZE), lambda j: (0, 0)),
        ],
        out_shape=[
            jax.ShapeDtypeStruct((group, width), BF16),
            jax.ShapeDtypeStruct((2, HEAD_SIZE), F32),
        ],
        compiler_params=pltpu.CompilerParams(vmem_limit_bytes=VMEM_LIMIT),
        cost_estimate=light("attend_back"),
        name="attend_back",
    )(own, got, own, got, own, got, *shared, grad_own, grad_got)

def shards(
    tokens,
    cotangent,
    seq_lengths,
    balance_order,
    attention_gain,
    query_weight,
    key_weight,
    value_projection,
    query_gain,
    key_norm_gain,
    output_weight,
    feedforward_gain,
    gate_weight,
    up_weight,
    down_weight,
):
    count = lax.axis_size("dp")
    levels = count.bit_length() - 1
    row = lax.axis_index("row")
    col = lax.axis_index("col")
    xbit, zbit, wbit = my_bit(1), my_bit(2), my_bit(4)
    half = tokens.shape[0]
    quarter = half // 2
    group = 2 * half
    pair = 2 * group
    features = tokens.shape[1]
    query_part = query_weight.shape[1] // 2
    key_part = key_weight.shape[1] // 2
    heads = query_part // HEAD_SIZE
    kv_heads = key_part // HEAD_SIZE
    repeat = heads // kv_heads
    ff_half = gate_weight.shape[1]
    runs = count // 8
    projections = tuple(map(in_place, (query_weight, key_weight, value_projection)))
    output_weight = in_place(output_weight)
    if runs == 1:
        gate_weight, up_weight, down_weight = map(in_place, (gate_weight, up_weight, down_weight))
    run = 2 * ff_half // count
    ff_part = ff_half // 4
    all_bits = high_bits(count)[::-1]

    def ff_block(weight, part, axis):
        if runs == 1:
            return weight, part * 2 + zbit
        pieces = [
            lax.dynamic_slice_in_dim(weight, ((part * runs + i) * 2 + zbit) * run, run, axis)
            for i in range(runs)
        ]
        return jnp.concatenate(pieces, axis=axis), 0

    moved_in = exchange(tokens)
    share = features // 4
    gate_far, far_base = ff_block(gate_weight, 1 - row, 1)
    up_far, _ = ff_block(up_weight, 1 - row, 1)
    gate_sent, up_sent = (
        block_of(weight, wbit * 2 + xbit, far_base, (share, ff_part))
        for weight in (gate_far, up_far)
    )
    got_gate, got_up = swap_row(gate_sent), swap_row(up_sent)

    base_ids = jnp.arange(half, dtype=jnp.int32)
    local_ids = jnp.concatenate([col * half + base_ids, (1 - col) * half + base_ids])
    slot_ids = jnp.arange(group, dtype=jnp.int32)
    slot = jnp.sum(
        jnp.where(balance_order[0][None, :] == local_ids[:, None], slot_ids[None, :], 0), axis=1
    )
    lengths = seq_lengths[0]
    seq_ends = jnp.cumsum(lengths)
    starts = seq_ends - lengths
    segment = jnp.sum((slot[:, None] >= seq_ends[None, :]).astype(jnp.int32), axis=1)
    hits = segment[:, None] == jnp.arange(lengths.shape[0], dtype=jnp.int32)[None, :]
    start = jnp.sum(jnp.where(hits, starts[None, :], 0), axis=1)
    cosine, sine = rotary_tables(slot - start)
    slot_lanes = jnp.broadcast_to(slot.astype(F32)[None], (8, group))
    start_lanes = jnp.broadcast_to(start.astype(F32)[None], (8, group))
    moved_in, cosine, sine, slot_lanes, start_lanes, got_gate, got_up = together(
        moved_in, cosine, sine, slot_lanes, start_lanes, got_gate, got_up
    )

    gain_in = attention_gain.astype(F32)[None]
    gain_mid = feedforward_gain.astype(F32)[None]
    x_low, scaled_in, square = local_call(
        scaled_kernel,
        (moved_in, swap_col(moved_in), gain_in),
        [((group, features), BF16), ((group, features), BF16), ((8, group), F32)],
        "scaled",
    )
    moved_grad = exchange(after(cotangent, moved_in))
    heads_sent = heads_forward(after(scaled_in, got_gate, got_up), *projections, 1 - row, BF16)
    got_square = swap_row(square)
    got_heads = swap_row(heads_sent)
    kept_heads = heads_forward(after(scaled_in, heads_sent), *projections, row, F32)
    got_gate, got_up = together(got_gate, got_up, heads_sent)[:2]
    got_gate_x, got_up_x = swap_dp(got_gate, 1), swap_dp(got_up, 1)
    got_gate_w, got_up_w = swap_dp(got_gate, 4), swap_dp(got_up, 4)

    down_own, own_at = ff_block(down_weight, row, 0)
    down_other, other_at = ff_block(down_weight, 1 - row, 0)

    def act_back(rows_of, weight, at, dtype):
        return product(rows_of, weight, "nt", dtype, ff_part // 3, at, ff_part)

    moved_grad = after(moved_grad, kept_heads)
    grad_z = swap_z(moved_grad)
    grad_near = swap_col(moved_grad)
    act_sent = [
        act_back(rows_of, down_other, other_at, BF16) for rows_of in (moved_grad, grad_near)
    ]
    got_heads, kept_heads, got_square, got_gate_x, got_gate_w, grad_z, *act_sent = together(
        got_heads, kept_heads, got_square, got_gate_x, got_gate_w, grad_z, *act_sent
    )
    inverse_in = lax.rsqrt((square + got_square) / D + EPSILON)
    shared = (
        inverse_in,
        cosine,
        sine,
        slot_lanes,
        start_lanes,
        slot_lanes[:1],
        query_gain.astype(F32)[None],
        key_norm_gain.astype(F32)[None],
    )
    got_act = [swap_row(act_sent[0])]
    got_gate_wx = swap_dp(got_gate_w, 1)
    grad_far = swap_col(grad_z)
    attention = attend(kept_heads, got_heads, shared, kv_heads, repeat)
    attention, got_act[0], grad_far = together(attention, got_act[0], grad_far)
    attention_other = swap_row(attention)
    got_act.append(swap_row(after(act_sent[1], attention)))
    out_own = product(attention, output_weight, "nn", F32, features // 2, row, query_part)
    far_sent = [
        act_back(after(rows_of, out_own), down_other, other_at, BF16)
        for rows_of in (grad_z, grad_far)
    ]
    attention_other, got_act[1], got_gate_wx, got_up_x, got_up_w, out_own, *far_sent = together(
        attention_other, got_act[1], got_gate_wx, got_up_x, got_up_w, out_own, *far_sent
    )
    got_up_wx = swap_dp(got_up_w, 1)
    out_kept, out_sent = product_onto(
        attention_other, output_weight, 1 - row, query_part, out_own, features // 2, "out_proj"
    )
    out_got = swap_col(out_sent)
    stream_mid, square_mid = local_call(
        middle_kernel,
        (moved_in, out_kept, out_got),
        [((half, features), F32), ((8, half), F32)],
        "middle",
    )
    got_square = swap_row(square_mid)
    grad_all = assemble(
        (pair, features),
        [
            (0, 0, moved_grad),
            (half, 0, grad_z),
            (group, 0, grad_near),
            (group + half, 0, after(grad_far, square_mid)),
        ],
        "grad_all",
    )
    normed_mid, inverse_mid = local_call(
        normed_kernel,
        (stream_mid, square_mid, got_square, gain_mid),
        [((half, features), BF16), ((8, half), F32)],
        "normed",
    )

    by_row = swap_row(normed_mid)
    by_z = swap_z(normed_mid)
    act_kept = act_back(after(grad_all, normed_mid), down_own, own_at, F32)
    by_row, by_z, act_kept, got_up_wx = together(by_row, by_z, act_kept, got_up_wx)
    corner_a = swap_row(by_z[:quarter])
    corner_b = swap_z(by_row[quarter:])
    got_act.extend(swap_row(after(sent, by_row)) for sent in far_sent)
    near = [
        (0, 0, normed_mid),
        (0, features, by_row),
        (half, 0, by_z),
        (half, features, corner_a),
        (half + quarter, features, corner_b),
    ]
    crossed = [(group + first, at, swap_col(piece)) for first, at, piece in near]
    mid_all = assemble((pair, 2 * features), near + crossed, "mid_all")

    gate_own, own_base = ff_block(gate_weight, row, 1)
    up_own, _ = ff_block(up_weight, row, 1)
    places = (
        wbit * 2 + xbit,
        wbit * 2 + 1 - xbit,
        (1 - wbit) * 2 + xbit,
        (1 - wbit) * 2 + 1 - xbit,
    )
    pieces = (
        (got_gate, got_gate_x, got_gate_w, got_gate_wx),
        (got_up, got_up_x, got_up_w, got_up_wx),
    )
    up_weights = (gate_own, up_own, own_base, pieces, places)
    gate_grad, up_grad, activated = gate_and_up(
        mid_all, *up_weights, act_kept, (got_act[0], got_act[2], got_act[1], got_act[3])
    )

    quarters = [activated[i * half : (i + 1) * half] for i in range(4)]
    others = [swap_row(quarters[0])]
    line = Line(activated)
    top_bit, lower_bits = all_bits[0], all_bits[1:]

    def up_rows(grad_part):
        whole = product(mid_all, grad_part, "tn", BF16, features // 2)
        return whole.reshape((2,) * (levels + 1) + (features // count, ff_part))

    def down_part(part, rows_of):
        whole = product(part, rows_of, "tn", BF16, ff_part // 2)
        return split_rows(whole, levels - 2)

    def first_stage(value, axis, bit):
        sent = line.passed(take(value, axis, 1 - my_bit(bit)))
        return swap_dp(sent, bit)

    def late_stage(value, got, axis, bit, next_axis, next_bit):
        kept, sent = end_stage(value, line.hold(got), axis, bit, next_axis, my_bit(next_bit))
        return kept, swap_dp(line.passed(sent), next_bit)

    mid_sent = line.passed(gate_and_up_back(gate_grad, up_grad, 1, *up_weights, BF16))
    got_mid = swap_col(mid_sent)
    gate_grad, others[0] = line.hold(gate_grad, others[0])
    gate_rows = up_rows(gate_grad)
    gate_got = first_stage(gate_rows, levels, 1)
    mid_kept = gate_and_up_back(line.hold(gate_grad), up_grad, 0, *up_weights, F32)
    block = (half, features)
    mid_own, to_row, to_z, row_both, z_both = local_call(
        join_core_kernel,
        (mid_kept, got_mid),
        [(block, F32)] * 3 + [((quarter, features), BF16)] * 2,
        "join_core",
    )
    via_row = swap_row(row_both)
    via_z = swap_z(z_both)
    line.passed(row_both)
    up_cols = up_rows(line.hold(up_grad))
    up_got = first_stage(up_cols, levels, 1)
    via_row, via_z = line.hold(via_row, via_z)
    to_row, to_z = local_call(
        join_corner_kernel,
        (to_row, to_z, via_row, via_z),
        [(block, BF16), (block, BF16)],
        "join_corner",
    )
    got_row, got_z = swap_row(to_row), swap_z(to_z)
    line.passed(to_row)
    down_first = down_part(activated, line.hold(grad_all))
    down_got = first_stage(down_first, down_first.ndim - 3, 1)
    got_row, got_z = line.hold(got_row, got_z)
    normed_mid_grad, mid_sum, feedforward_part = norm_sums(
        (mid_own, got_row, got_z), stream_mid, inverse_mid, gain_mid
    )
    got_sum = swap_row(line.passed(mid_sum))
    others.append(swap_row(line.hold(quarters[1])))
    got_sum, gate_got = line.hold(got_sum, gate_got)
    stream_mid_grad, branch_low = norm_grad(
        normed_mid_grad, stream_mid, inverse_mid, gain_mid, mid_sum, got_sum, moved_grad, (F32, BF16)
    )
    line.passed(branch_low)
    branch_got = swap_col(branch_low)
    gate_rows, gate_got = late_stage(gate_rows, gate_got, levels, 1, 1, top_bit)
    branch = assemble(
        (group, features), [(0, 0, branch_low), (half, 0, line.hold(branch_got))], "branch"
    )
    attention_sent = product(branch, output_weight, "nt", BF16, query_part, 1 - row, query_part)
    attention_sent, others[1] = together(attention_sent, others[1])
    got_attention = swap_row(attention_sent)
    line.passed(attention_sent)

    others.extend(swap_row(line.hold(part)) for part in quarters[2:])
    attention_kept = line.passed(
        product(line.hold(branch), output_weight, "nt", F32, query_part, row, query_part)
    )
    output_first, output_sent = [], []
    for part in (attention, attention_other):
        whole = product(line.hold(part), branch, "tn", BF16, query_part // 2)
        whole = split_rows(whole, levels - 1)
        output_sent.append(line.passed(take(whole, whole.ndim - 4, 1 - zbit)))
        output_first.append(whole)
    got_attention, *output_sent = line.hold(got_attention, *output_sent)
    line.passed(got_attention)
    output_got = [swap_dp(sent, 2) for sent in output_sent]
    projected_grad, head_gains = attend_back(
        kept_heads, got_heads, shared, attention_kept, line.hold(got_attention), kv_heads, repeat
    )
    projected_grad, others[2], others[3], gate_got, up_got, down_got = together(
        projected_grad, others[2], others[3], gate_got, up_got, down_got
    )
    projected_other = swap_row(projected_grad)
    line.passed(projected_grad)
    up_cols, up_got = late_stage(up_cols, up_got, levels, 1, 1, top_bit)

    (normed_in,) = local_call(
        normed_in_kernel,
        (x_low, line.hold(inverse_in), gain_in),
        [((group, features), BF16)],
        "normed_in",
    )

    def projection_rows(part):
        whole = split_rows(product(normed_in, part, "tn", BF16, features // 2), levels)
        return whole, first_stage(whole, levels - 2, 2)

    heads_first, heads_got = projection_rows(line.hold(projected_grad))
    activated_other = assemble(
        (pair, ff_part),
        [(i * half, 0, other) for i, other in enumerate(line.hold(*others))],
        "activated_other",
    )
    down_second = down_part(activated_other, grad_all)
    down_got_other = first_stage(down_second, down_second.ndim - 3, 1)
    in_own = line.passed(heads_backward(line.hold(projected_grad), *projections, row)[0])
    out_own = line.passed(
        product(line.hold(activated), down_own, "nn", F32, features // 2, own_at, ff_part)
    )
    out_kept, out_sent = product_onto(
        line.hold(activated_other),
        down_other,
        other_at,
        ff_part,
        out_own,
        features // 2,
        "down_proj",
    )
    out_got = swap_col(line.passed(out_sent))
    out_near, out_far = local_call(
        out_near_kernel, (out_kept, line.hold(out_got)), [(block, F32), (block, BF16)], "out_near"
    )
    line.passed(out_far)
    projected_other, in_own, out_far, down_got_other, *output_got = line.hold(
        projected_other, in_own, out_far, down_got_other, *output_got
    )
    layer_z = swap_z(out_far)
    line.passed(projected_other)
    in_kept, in_sent = heads_backward(projected_other, *projections, 1 - row, in_own)
    in_got = swap_col(line.passed(in_sent))
    down_rows = []
    for v, got in ((down_first, down_got), (down_second, down_got_other)):
        down_rows.append(line.passed(end_stage(v, line.hold(got), v.ndim - 3, 1)))
    down_kept, down_sent = split_top(*down_rows, row)
    down_got = swap_dp(line.passed(down_sent), top_bit)
    in_values = (moved_in, inverse_in[:, :half], gain_in)
    normed_in_grad, in_sum, attention_part = norm_sums(
        (in_kept, line.hold(in_got)), *in_values
    )
    got_sum = swap_row(line.passed(in_sum))
    output_rows, output_got = zip(
        *(
            late_stage(v, got, v.ndim - 4, 2, v.ndim - 4, 1)
            for v, got in zip(output_first, output_got)
        )
    )
    heads_second, heads_got_other = projection_rows(line.hold(projected_other))
    got_sum, up_got, heads_got, layer_z = line.hold(got_sum, up_got, heads_got, layer_z)
    (stream_grad,) = norm_grad(
        normed_in_grad, *in_values, in_sum, got_sum, stream_mid_grad, (BF16,)
    )
    (layer_out,) = local_call(
        layer_out_kernel, (stream_mid, out_near, line.hold(layer_z)), [(block, BF16)], "layer_out"
    )
    rows = two_rows(attention_part[0]) + two_rows(feedforward_part[0])
    rows += two_rows(head_gains.reshape(-1))
    back = exchange(line.passed(with_rows((stream_grad, layer_out), rows)))

    output_rows = [
        line.passed(add_got(kept, line.hold(got))) for kept, got in zip(output_rows, output_got)
    ]
    output_kept, output_sent = split_top(*output_rows, row)
    output_got = swap_dp(line.passed(output_sent), top_bit)
    heads_own, heads_got = late_stage(heads_first, heads_got, levels - 2, 2, levels - 2, 1)
    for bit in lower_bits:
        gate_rows, gate_got = late_stage(gate_rows, gate_got, None, None, 1, bit)
        up_cols, up_got = late_stage(up_cols, up_got, None, None, 1, bit)
    shape = gate_rows.shape[1:-1] + (2 * ff_part,)
    side_own, side_sent = local_call(
        side_kernel,
        (gate_rows, up_cols, *line.hold(gate_got, up_got)),
        [(shape, F32), (shape, BF16)],
        "side",
    )
    side_got = swap_row(line.passed(side_sent))
    back, side_got, heads_got, heads_got_other, down_got = line.hold(
        back, side_got, heads_got, heads_got_other, down_got
    )
    line.passed(side_got)
    heads_own, heads_got = late_stage(heads_own, heads_got, None, None, 0, top_bit)
    heads_other, heads_got_other = late_stage(
        heads_second, heads_got_other, levels - 2, 2, levels - 2, 1
    )
    side_got = line.hold(side_got)
    sent = jnp.stack([pick(part, 1 - zbit, 0).astype(BF16) for part in (side_own, side_got)])
    side_z = swap_z(line.passed(sent))
    output_got, heads_got, heads_got_other, side_z = line.hold(
        output_got, heads_got, heads_got_other, side_z
    )
    line.passed(heads_got)
    heads_other, heads_got_other = late_stage(heads_other, heads_got_other, None, None, 0, top_bit)

    def finish(kept, got):
        value = line.passed(add_got(kept, line.hold(got)))
        for bit in lower_bits:
            value = pick(value, my_bit(bit), 0) + swap_dp(
                pick(value, 1 - my_bit(bit), 0).astype(BF16), bit
            ).astype(F32)
        return value

    output_weight_grad = finish(output_kept, output_got)
    down_grad = finish(down_kept, down_got)
    heads_grad_own = finish(heads_own, heads_got)

    def up_columns(at):
        columns = slice(at, at + ff_part)
        keep = [pick(part[..., columns], zbit, 0) for part in (side_own, side_got.astype(F32))]
        swapped = side_z[..., columns].astype(F32)
        table = [
            by_half(zbit, near_piece, far_piece)
            for near_piece, far_piece in zip(
                by_half(row, keep[0], keep[1]), by_half(row, swapped[0], swapped[1])
            )
        ]
        return jnp.concatenate(
            [
                table[part][z][:, i * run : (i + 1) * run]
                for part in range(2)
                for i in range(runs)
                for z in range(2)
            ],
            axis=1,
        )

    gate_weight_grad = line.passed(up_columns(0))
    up_weight_grad = up_columns(ff_part)
    heads_grad_other = finish(heads_other, heads_got_other)

    def head_grad(start, width):
        own = heads_grad_own[:, start : start + width]
        other = heads_grad_other[:, start : start + width]
        return jnp.concatenate(by_half(row, own, other), axis=1)

    query_weight_grad = head_grad(0, query_part)
    key_weight_grad = head_grad(query_part, key_part)
    value_weight_grad = head_grad(query_part + key_part, key_part)

    back = back.reshape(count, -1, features).astype(F32)
    share = half // count
    grad_back = back[:, :share].reshape(half, features)
    out_back = back[:, share : 2 * share].reshape(half, features)
    totals = jnp.sum(back[:, 2 * share :], axis=0)
    gains = jnp.concatenate([totals[i] + totals[i + 1] for i in (0, 2, 4)])[None]
    gains = gains + swap_col(gains)
    gain_low, gain_high = (part[0] for part in by_half(row, gains, swap_row(gains)))
    attention_total = jnp.concatenate([gain_low[:features], gain_high[:features]])
    feedforward_total = jnp.concatenate(
        [gain_low[features : 2 * features], gain_high[features : 2 * features]]
    )
    head_totals = (gain_low + gain_high)[2 * features :]
    return (
        out_back,
        grad_back,
        attention_total,
        query_weight_grad,
        key_weight_grad,
        value_weight_grad,
        head_totals[:HEAD_SIZE],
        head_totals[HEAD_SIZE : 2 * HEAD_SIZE],
        output_weight_grad,
        feedforward_total,
        gate_weight_grad,
        up_weight_grad,
        down_grad,
    )


def solution(mesh):
    placed = (
        P(("dp", "col"), "row"),
        P(("dp", "col"), "row"),
        P("dp", None),
        P("dp", None),
        P("row"),
        P("row", "col"),
        P("row", "col"),
        P("row", "col"),
        P(),
        P(),
        P("col", "row"),
        P("row"),
        P("row", "col"),
        P("row", "col"),
        P("col", "row"),
    )
    return jax.shard_map(
        shards,
        mesh=mesh,
        in_specs=placed,
        out_specs=(
            P(("dp", "col"), "row"),
            P(("dp", "col"), "row"),
            P(),
            P(("row", "dp"), "col"),
            P(("row", "dp"), "col"),
            P(("row", "dp"), "col"),
            P(),
            P(),
            P(("col", "dp"), "row"),
            P(),
            P(("row", "dp"), "col"),
            P(("row", "dp"), "col"),
            P(("col", "dp"), "row"),
        ),
        check_vma=False,
    )
```

time: 602 us -> 524 us (0.87)
  Pallas kernels: 0 us -> 155 us
  matrix products: 98.2 us -> 0 us
  other arithmetic: 90.3 us -> 13.1 us
  blocking collectives: 46.4 us -> 0 us
  waiting for transfers between devices: 233 us -> 202 us
  starting transfers between devices: 61.1 us -> 81.2 us
    pallas_call x0 -> x73, Pallas kernels: none -> 155 us  [the longest x48 114 us: grid_call(): pl.pallas_call(kernel, grid_spec=pltpu.PrefetchScalarGridSpec(num_scalar_...]
    dot_general x23 -> x0, matrix products: 92.9 us -> none  [the longest x7 40.3 us: dot_nt(): lax.dot_general(left, right, (((1,), (1,)), ((), ())), preferred_element_...]
    psum x1 -> x0, blocking collectives: 46.4 us -> none  [shards(): lax.psum((lax.dynamic_update_slice_in_dim(zero_vector, attention_part, fe...]
    unnamed x227 -> x310, local copies, waits for them, and re-layouts: 12.6 us -> 52.1 us
    ppermute x17 -> x24, waiting for transfers between devices: 88.8 us -> 60.7 us  [swap_row(): return lax.ppermute(value, 'row', [(0, 1), (1, 0)])]
    add x18 -> x3, other arithmetic: 22.1 us -> 0.06 us  [the longest x1 0.02 us: shards(): head_totals = (gain_low + gain_high)[2 * features:]]
    ppermute x24 -> x31, starting transfers between devices: 22.7 us -> 36.3 us  [swap_dp(): return lax.ppermute(value, 'dp', [(i, i ^ bit) for i in range(count)])]
    convert_element_type x17 -> x6, other arithmetic: 13.6 us -> 1.69 us  [the longest x1 1.54 us: shards(): back = back.reshape(count, -1, features).astype(F32)]
  transfers between devices with their start and end apart: 54 -> 72, of which waited for: 21 -> 34; matrix products, arithmetic and copies ran while one was open for 35% -> 4% of each run, Pallas kernels for 0% -> 21%
where the time goes in v2:
time: 524 us; the launch traced here: 519 us
  waiting for transfers between devices  202 us (39%)
  Pallas kernels  155 us (30%)
  starting transfers between devices  81.2 us (15%)
  local copies, waits for them, and re-layouts  65.7 us (13%)
  other arithmetic  13.1 us (2%)
    ppermute x31, waiting for transfers between devices, swap_dp(): return lax.ppermute(value, 'dp', [(i, i ^ bit) for i in range(count)])  130 us
    pallas_call x48, Pallas kernels, grid_call(): pl.pallas_call(kernel, grid_spec=pltpu.PrefetchScalarGridSpec(num_scalar_...  114 us
    ppermute x24, waiting for transfers between devices, swap_row(): return lax.ppermute(value, 'row', [(0, 1), (1, 0)])  60.7 us
    unnamed x310, local copies, waits for them, and re-layouts  52.1 us
    ppermute x31, starting transfers between devices, swap_dp(): return lax.ppermute(value, 'dp', [(i, i ^ bit) for i in range(count)])  36.3 us
    ppermute x24, starting transfers between devices, swap_row(): return lax.ppermute(value, 'row', [(0, 1), (1, 0)])  28.8 us
    pallas_call x23, Pallas kernels, local_call(): pl.pallas_call(kernel, out_shape=[jax.ShapeDtypeStruct(shape, dtype) for...  21.2 us
    all_to_all x3, starting transfers between devices, exchange(): return lax.all_to_all(value, 'dp', split_axis=0, concat_axis=0, tiled=True)  15.3 us
  transfers between devices with their start and end apart: 72, of which 34 were waited for; matrix products, arithmetic and copies ran while one was open for 4% of the time, Pallas kernels for 21%

profile of v2, /device:TPU:0, one launch (start us, length us, event | category | flops | bytes accessed | tf_op | source)
XLA Modules:
  0.0 519.3 jit_solution(10617538450492198921)
XLA Ops:
  7.1 6.3 %all-to-all-start = ((bf16[8,32,1024]{2,1,0:T(8,128)(2,1)}), bf16[8,32,1024]{2,1,0:T(8,128)(2,1)S(1)}, u32[]{:S(2)}, u32[]{:S(2)}) async-start(bf16[8,32,1024]{2,1,0:T(8,128)(2,1)} %bitcast.1), calls=%async_computation | async-start | bytes 1048576 | tf_op jit(solution)/shard_map/all_to_all | solution.py:90
  16.7 6.2 %collective-permute-done.1.refs_4_ = bf16[256,768]{1,0:T(8,128)(2,1)S(1)} collective-permute-done((bf16[256,768]{1,0:T(8,128)(2,1)S(1)}, bf16[256,768]{1,0:T(8,128)(2,1)S(1)}, u32[]{:S(2)}, u32[]{:S(2)}) %collective-permute-start.1) | collective-permute-done | bytes 393248 | tf_op jit(solution)/shard_map/ppermute | solution.py:34
  28.0 4.7 all-to-all-start.1
  59.1 5.9 %collective-permute-done.4 = f32[8,512]{1,0:T(8,128)S(1)} collective-permute-done((f32[8,512]{1,0:T(8,128)S(1)}, f32[8,512]{1,0:T(8,128)S(1)}, u32[]{:S(2)}, u32[]{:S(2)}) %collective-permute-start.4) | collective-permute-done | bytes 16416 | tf_op jit(solution)/shard_map/ppermute | solution.py:34
  73.5 7.2 %attend.1.left_ref = bf16[512,512]{1,0:T(8,128)(2,1)S(1)} custom-call(f32[512,1024]{1,0:T(8,128)S(1)} %heads_forward.3.query_own.key_own.value_own, bf16[512,1024]{1,0:T(8,128)(2,1)S(1)} %collective-permute-done.3.query_got.key_got.value_got, f32[512,1024]{1,0:T(8,128)S(1)} %heads_forward.3.query_own.key_own.value_own, ...), custom_call_target="tpu_custom_call" | custom-call | flops 805000000 | bytes 2583000 | tf_op jit(solution)/shard_map/attend/pallas_call | solution.py:795
  98.7 7.0 %collective-permute-done.15.refs_6_ = bf16[256,768]{1,0:T(8,128)(2,1)} collective-permute-done((bf16[256,768]{1,0:T(8,128)(2,1)S(1)}, bf16[256,768]{1,0:T(8,128)(2,1)}, u32[]{:S(2)}, u32[]{:S(2)}) %collective-permute-start.15) | collective-permute-done | bytes 393248 | tf_op jit(solution)/shard_map/ppermute | solution.py:43
  136.1 5.0 collective-permute-done.21.refs_3_
  151.3 6.4 %collective-permute-done.28.refs_10_ = bf16[256,768]{1,0:T(8,128)(2,1)} collective-permute-done((bf16[256,768]{1,0:T(8,128)(2,1)}, bf16[256,768]{1,0:T(8,128)(2,1)}, u32[]{:S(2)}, u32[]{:S(2)}) %collective-permute-start.28) | collective-permute-done | bytes 393248 | tf_op jit(solution)/shard_map/ppermute | solution.py:34
  157.7 12.0 %gate_and_up.1 = (bf16[1024,768]{1,0:T(8,128)(2,1)S(1)}, bf16[1024,768]{1,0:T(8,128)(2,1)S(1)}, bf16[1024,768]{1,0:T(8,128)(2,1)S(1)}) custom-call(s32[5]{0:T(128)S(1)} %copy-done.127, bf16[1024,2048]{1,0:T(8,128)(2,1)} %copy-done, bf16[1024,3072]{1,0:T(8,128)(2,1)} %gate_ref.5, bf16[1024,3072]{1,0:T(8,128)(2,1)} %up_ref.5, ...), custom_call_target="tpu_custom_call" | custom-call | flops 1380000000 | bytes 4428000 | tf_op jit(solution)/shard_map/gate_and_up/pallas_call | solution.py:167
  169.7 8.6 %gate_and_up_back.2 = bf16[512,2048]{1,0:T(8,128)(2,1)} custom-call(s32[5]{0:T(128)S(1)} %copy-done.127, bf16[1024,768]{1,0:T(8,128)(2,1)S(1)} %get-tuple-element.247.gate_grad_ref.right_ref, bf16[1024,768]{1,0:T(8,128)(2,1)S(1)} %get-tuple-element.253.up_grad_ref.right_ref, bf16[1024,3072]{1,0:T(8,128)(2,1)} %gate_ref.5, bf16[1024,3072]{1,0:T(8,128)(2,1)} %up_ref.5, ...), custom_call_target="tpu_custom_call" | custom-call | flops 805000000 | bytes 2583000 | tf_op jit(solution)/shard_map/gate_and_up_back/pallas_call | solution.py:167
  181.0 10.3 %collective-permute-done.30.refs_0_ = bf16[256,768]{1,0:T(8,128)(2,1)} collective-permute-done((bf16[256,768]{1,0:T(8,128)(2,1)}, bf16[256,768]{1,0:T(8,128)(2,1)}, u32[]{:S(2)}, u32[]{:S(2)}) %collective-permute-start.30) | collective-permute-done | bytes 393248 | tf_op jit(solution)/shard_map/ppermute | solution.py:34
  201.7 6.1 %gate_and_up_back.3.kept_ref = f32[512,2048]{1,0:T(8,128)S(1)} custom-call(s32[5]{0:T(128)S(1)} %copy-done.128, bf16[1024,768]{1,0:T(8,128)(2,1)S(1)} %copy-done.25, bf16[1024,768]{1,0:T(8,128)(2,1)S(1)} %copy-done.21, bf16[1024,3072]{1,0:T(8,128)(2,1)} %gate_ref.5, bf16[1024,3072]{1,0:T(8,128)(2,1)} %up_ref.5, ...), custom_call_target="tpu_custom_call" | custom-call | flops 805000000 | bytes 2583000 | tf_op jit(solution)/shard_map/gate_and_up_back/pallas_call | solution.py:167
  213.3 4.5 product_tn.9
  228.2 4.9 collective-permute-done.34.refs_1_
  257.2 10.2 %collective-permute-done.40.grad_got = bf16[512,512]{1,0:T(8,128)(2,1)S(1)} collective-permute-done((bf16[512,512]{1,0:T(8,128)(2,1)S(1)}, bf16[512,512]{1,0:T(8,128)(2,1)S(1)}, u32[]{:S(2)}, u32[]{:S(2)}) %collective-permute-start.40) | collective-permute-done | bytes 524320 | tf_op jit(solution)/shard_map/ppermute | solution.py:34
  276.0 11.9 %attend_back.1 = (bf16[512,1024]{1,0:T(8,128)(2,1)S(1)}, f32[2,128]{1,0:T(2,128)S(1)}) custom-call(f32[512,1024]{1,0:T(8,128)S(1)} %heads_forward.3.query_own.key_own.value_own, bf16[512,1024]{1,0:T(8,128)(2,1)S(1)} %collective-permute-done.3.query_got.key_got.value_got, f32[512,1024]{1,0:T(8,128)S(1)} %heads_forward.3.query_own.key_own.value_own, ...), custom_call_target="tpu_custom_call" | custom-call | flops 1380000000 | bytes 4428000 | tf_op jit(solution)/shard_map/attend_back/pallas_call | solution.py:810
  318.5 10.8 %collective-permute-done.49.keep_got.send_got = bf16[2,128,1024]{2,1,0:T(8,128)(2,1)S(1)} collective-permute-done((bf16[2,128,1024]{2,1,0:T(8,128)(2,1)S(1)}, bf16[2,128,1024]{2,1,0:T(8,128)(2,1)S(1)}, u32[]{:S(2)}, u32[]{:S(2)}) %collective-permute-start.49) | collective-permute-done | bytes 524320 | tf_op jit(solution)/shard_map/ppermute | solution.py:43
  330.0 10.4 %collective-permute-done.50.keep_got.send_got = bf16[2,128,1024]{2,1,0:T(8,128)(2,1)S(1)} collective-permute-done((bf16[2,128,1024]{2,1,0:T(8,128)(2,1)S(1)}, bf16[2,128,1024]{2,1,0:T(8,128)(2,1)S(1)}, u32[]{:S(2)}, u32[]{:S(2)}) %collective-permute-start.50) | collective-permute-done | bytes 524320 | tf_op jit(solution)/shard_map/ppermute | solution.py:43
  366.4 18.3 %collective-permute-done.53.refs_3_ = bf16[2,2,128,768]{3,2,1,0:T(8,128)(2,1)} collective-permute-done((bf16[2,2,128,768]{3,2,1,0:T(8,128)(2,1)}, bf16[2,2,128,768]{3,2,1,0:T(8,128)(2,1)}, u32[]{:S(2)}, u32[]{:S(2)}) %collective-permute-start.53) | collective-permute-done | bytes 786464 | tf_op jit(solution)/shard_map/ppermute | solution.py:43
  384.7 5.3 %collective-permute-done.55.got_ref = bf16[256,1024]{1,0:T(8,128)(2,1)} collective-permute-done((bf16[256,1024]{1,0:T(8,128)(2,1)}, bf16[256,1024]{1,0:T(8,128)(2,1)}, u32[]{:S(2)}, u32[]{:S(2)}) %collective-permute-start.55) | collective-permute-done | bytes 524320 | tf_op jit(solution)/shard_map/ppermute | solution.py:43
  405.5 15.3 %collective-permute-done.56.got_ref = bf16[128,1024]{1,0:T(8,128)(2,1)S(1)} collective-permute-done((bf16[128,1024]{1,0:T(8,128)(2,1)}, bf16[128,1024]{1,0:T(8,128)(2,1)S(1)}, u32[]{:S(2)}, u32[]{:S(2)}) %collective-permute-start.56) | collective-permute-done | bytes 262176 | tf_op jit(solution)/shard_map/ppermute | solution.py:43
  440.6 28.0 %collective-permute-done.61.got_ref = bf16[384,1024]{1,0:T(8,128)(2,1)} collective-permute-done((bf16[384,1024]{1,0:T(8,128)(2,1)}, bf16[384,1024]{1,0:T(8,128)(2,1)}, u32[]{:S(2)}, u32[]{:S(2)}) %collective-permute-start.61) | collective-permute-done | bytes 786464 | tf_op jit(solution)/shard_map/ppermute | solution.py:43
  485.4 16.0 %collective-permute-done.67 = bf16[2,128,1536]{2,1,0:T(8,128)(2,1)S(1)} collective-permute-done((bf16[2,128,1536]{2,1,0:T(8,128)(2,1)S(1)}, bf16[2,128,1536]{2,1,0:T(8,128)(2,1)S(1)}, u32[]{:S(2)}, u32[]{:S(2)}) %collective-permute-start.67) | collective-permute-done | bytes 786464 | tf_op jit(solution)/shard_map/ppermute | solution.py:43
  511.4 5.1 collective-permute-done.68.got_ref
  (569 shorter events, 290.1 us)
Async XLA Ops:
  38.9 32.2 %collective-permute-start.3 = (bf16[512,1024]{1,0:T(8,128)(2,1)}, bf16[512,1024]{1,0:T(8,128)(2,1)S(1)}, u32[]{:S(2)}, u32[]{:S(2)}) collective-permute-start(bf16[512,1024]{1,0:T(8,128)(2,1)} %heads_forward.2), channel_id=1, source_target_pairs={{0,2},{2,0},{1,3},{3,1},{4,6},{6,4},{5,7},{7,5},{8,10},{10,8},{9,1... | collective-permute-start | bytes 3145736 | tf_op jit(solution)/shard_map/ppermute | solution.py:34
  48.1 23.0 %collective-permute-start.7 = (bf16[256,1024]{1,0:T(8,128)(2,1)}, bf16[256,1024]{1,0:T(8,128)(2,1)S(1)}, u32[]{:S(2)}, u32[]{:S(2)}) collective-permute-start(bf16[256,1024]{1,0:T(8,128)(2,1)} %bitcast.13.left_ref.refs_0_.rest_ref), channel_id=1, source_target_pairs={{0,8},{4,12},{8,0},{12,4},{16,24},{20,28},{24,16},{28,20},{1,9},{5... | collective-permute-start | bytes 1572872 | tf_op jit(solution)/shard_map/ppermute | solution.py:43
  83.4 23.1 %collective-permute-start.11 = (bf16[512,512]{1,0:T(8,128)(2,1)S(1)}, bf16[512,512]{1,0:T(8,128)(2,1)S(1)}, u32[]{:S(2)}, u32[]{:S(2)}) collective-permute-start(bf16[512,512]{1,0:T(8,128)(2,1)S(1)} %attend.1.left_ref), channel_id=1, source_target_pairs={{0,2},{2,0},{1,3},{3,1},{4,6},{6,4},{5,7},{7,5},{8,10},{10,8},{9,1... | collective-permute-start | bytes 1572872 | tf_op jit(solution)/shard_map/ppermute | solution.py:34
  178.3 29.6 %collective-permute-start.31 = (bf16[512,2048]{1,0:T(8,128)(2,1)}, bf16[512,2048]{1,0:T(8,128)(2,1)}, u32[]{:S(2)}, u32[]{:S(2)}) collective-permute-start(bf16[512,2048]{1,0:T(8,128)(2,1)} %gate_and_up_back.2), channel_id=1, source_target_pairs={{0,1},{1,0},{2,3},{3,2},{4,5},{5,4},{6,7},{7,6},{8,9},{9,8},{10,11... | collective-permute-start | bytes 6291464 | tf_op jit(solution)/shard_map/ppermute | solution.py:38
  199.6 37.5 %collective-permute-start.37 = (bf16[2,2,2,128,768]{4,3,2,1,0:T(8,128)(2,1)S(1)}, bf16[2,2,2,128,768]{4,3,2,1,0:T(8,128)(2,1)}, u32[]{:S(2)}, u32[]{:S(2)}) collective-permute-start(bf16[2,2,2,128,768]{4,3,2,1,0:T(8,128)(2,1)S(1)} %take.8), channel_id=1, source_target_pairs={{0,4},{4,0},{8,12},{12,8},{16,20},{20,16},{24,28},{28,24},{1,5},{5... | collective-permute-start | bytes 4718600 | tf_op jit(solution)/shard_map/ppermute | solution.py:43
  222.4 66.1 %collective-permute-start.44 = (bf16[2,2,2,128,768]{4,3,2,1,0:T(8,128)(2,1)}, bf16[2,2,2,128,768]{4,3,2,1,0:T(8,128)(2,1)}, u32[]{:S(2)}, u32[]{:S(2)}) collective-permute-start(bf16[2,2,2,128,768]{4,3,2,1,0:T(8,128)(2,1)} %take.9), channel_id=1, source_target_pairs={{0,4},{4,0},{8,12},{12,8},{16,20},{20,16},{24,28},{28,24},{1,5},{5... | collective-permute-start | bytes 4718600 | tf_op jit(solution)/shard_map/ppermute | solution.py:43
  253.7 34.7 %collective-permute-start.45 = (bf16[384,1024]{1,0:T(8,128)(2,1)}, bf16[384,1024]{1,0:T(8,128)(2,1)}, u32[]{:S(2)}, u32[]{:S(2)}) collective-permute-start(bf16[384,1024]{1,0:T(8,128)(2,1)} %take.10), channel_id=1, source_target_pairs={{0,4},{4,0},{8,12},{12,8},{16,20},{20,16},{24,28},{28,24},{1,5},{5... | collective-permute-start | bytes 2359304 | tf_op jit(solution)/shard_map/ppermute | solution.py:43
  254.8 36.8 %collective-permute-start.43 = (bf16[2,2,128,768]{3,2,1,0:T(8,128)(2,1)}, bf16[2,2,128,768]{3,2,1,0:T(8,128)(2,1)}, u32[]{:S(2)}, u32[]{:S(2)}) collective-permute-start(bf16[2,2,128,768]{3,2,1,0:T(8,128)(2,1)} %get-tuple-element.268), channel_id=1, source_target_pairs={{0,16},{4,20},{8,24},{12,28},{16,0},{20,4},{24,8},{28,12},{1,17},{... | collective-permute-start | bytes 2359304 | tf_op jit(solution)/shard_map/ppermute | solution.py:43
  256.1 35.4 %collective-permute-start.42 = (bf16[256,768]{1,0:T(8,128)(2,1)}, bf16[256,768]{1,0:T(8,128)(2,1)}, u32[]{:S(2)}, u32[]{:S(2)}) collective-permute-start(bf16[256,768]{1,0:T(8,128)(2,1)} %get-tuple-element.278), channel_id=1, source_target_pairs={{0,2},{2,0},{1,3},{3,1},{4,6},{6,4},{5,7},{7,5},{8,10},{10,8},{9,1... | collective-permute-start | bytes 1179656 | tf_op jit(solution)/shard_map/ppermute | solution.py:34
  268.2 23.4 %collective-permute-start.41 = (bf16[256,768]{1,0:T(8,128)(2,1)}, bf16[256,768]{1,0:T(8,128)(2,1)}, u32[]{:S(2)}, u32[]{:S(2)}) collective-permute-start(bf16[256,768]{1,0:T(8,128)(2,1)} %get-tuple-element.277), channel_id=1, source_target_pairs={{0,2},{2,0},{1,3},{3,1},{4,6},{6,4},{5,7},{7,5},{8,10},{10,8},{9,1... | collective-permute-start | bytes 1179656 | tf_op jit(solution)/shard_map/ppermute | solution.py:34
  312.5 28.8 %collective-permute-start.46 = (bf16[512,1024]{1,0:T(8,128)(2,1)S(1)}, bf16[512,1024]{1,0:T(8,128)(2,1)S(1)}, u32[]{:S(2)}, u32[]{:S(2)}) collective-permute-start(bf16[512,1024]{1,0:T(8,128)(2,1)S(1)} %get-tuple-element.294.right_ref.grads_ref), channel_id=1, source_target_pairs={{0,2},{2,0},{1,3},{3,1},{4,6},{6,4},{5,7},{7,5},{8,10},{10,8},{9,1... | collective-permute-start | bytes 3145736 | tf_op jit(solution)/shard_map/ppermute | solution.py:34
  313.4 27.9 %collective-permute-start.48 = (bf16[384,1024]{1,0:T(8,128)(2,1)S(1)}, bf16[384,1024]{1,0:T(8,128)(2,1)S(1)}, u32[]{:S(2)}, u32[]{:S(2)}) collective-permute-start(bf16[384,1024]{1,0:T(8,128)(2,1)S(1)} %take.14), channel_id=1, source_target_pairs={{0,4},{4,0},{8,12},{12,8},{16,20},{20,16},{24,28},{28,24},{1,5},{5... | collective-permute-start | bytes 2359304 | tf_op jit(solution)/shard_map/ppermute | solution.py:43
  314.4 26.0 %collective-permute-start.50 = (bf16[2,128,1024]{2,1,0:T(8,128)(2,1)S(1)}, bf16[2,128,1024]{2,1,0:T(8,128)(2,1)S(1)}, u32[]{:S(2)}, u32[]{:S(2)}) collective-permute-start(bf16[2,128,1024]{2,1,0:T(8,128)(2,1)S(1)} %take.12), channel_id=1, source_target_pairs={{0,8},{4,12},{8,0},{12,4},{16,24},{20,28},{24,16},{28,20},{1,9},{5... | collective-permute-start | bytes 1572872 | tf_op jit(solution)/shard_map/ppermute | solution.py:43
  316.5 68.2 %collective-permute-start.54 = (bf16[2,2,128,1024]{3,2,1,0:T(8,128)(2,1)}, bf16[2,2,128,1024]{3,2,1,0:T(8,128)(2,1)}, u32[]{:S(2)}, u32[]{:S(2)}) collective-permute-start(bf16[2,2,128,1024]{3,2,1,0:T(8,128)(2,1)} %take.13), channel_id=1, source_target_pairs={{0,8},{4,12},{8,0},{12,4},{16,24},{20,28},{24,16},{28,20},{1,9},{5... | collective-permute-start | bytes 3145736 | tf_op jit(solution)/shard_map/ppermute | solution.py:43
  346.5 38.2 %collective-permute-start.53 = (bf16[2,2,128,768]{3,2,1,0:T(8,128)(2,1)}, bf16[2,2,128,768]{3,2,1,0:T(8,128)(2,1)}, u32[]{:S(2)}, u32[]{:S(2)}) collective-permute-start(bf16[2,2,128,768]{3,2,1,0:T(8,128)(2,1)} %copy-done.140), channel_id=1, source_target_pairs={{0,16},{4,20},{8,24},{12,28},{16,0},{20,4},{24,8},{28,12},{1,17},{... | collective-permute-start | bytes 2359304 | tf_op jit(solution)/shard_map/ppermute | solution.py:43
  347.0 43.0 %collective-permute-start.55 = (bf16[256,1024]{1,0:T(8,128)(2,1)}, bf16[256,1024]{1,0:T(8,128)(2,1)}, u32[]{:S(2)}, u32[]{:S(2)}) collective-permute-start(bf16[256,1024]{1,0:T(8,128)(2,1)} %copy-done.141), channel_id=1, source_target_pairs={{0,8},{4,12},{8,0},{12,4},{16,24},{20,28},{24,16},{28,20},{1,9},{5... | collective-permute-start | bytes 1572872 | tf_op jit(solution)/shard_map/ppermute | solution.py:43
  357.3 32.7 %collective-permute-start.52 = (f32[8,256]{1,0:T(8,128)S(1)}, f32[8,256]{1,0:T(8,128)S(1)}, u32[]{:S(2)}, u32[]{:S(2)}) collective-permute-start(f32[8,256]{1,0:T(8,128)S(1)} %get-tuple-element.314.sums_ref), channel_id=1, source_target_pairs={{0,2},{2,0},{1,3},{3,1},{4,6},{6,4},{5,7},{7,5},{8,10},{10,8},{9,1... | collective-permute-start | bytes 24584 | tf_op jit(solution)/shard_map/ppermute | solution.py:34
  394.7 73.8 %all-to-all-start.2 = ((bf16[8,72,1024]{2,1,0:T(8,128)(2,1)}), bf16[8,72,1024]{2,1,0:T(8,128)(2,1)}, u32[]{:S(2)}, u32[]{:S(2)}) async-start(bf16[8,72,1024]{2,1,0:T(8,128)(2,1)} %pad_maximum_fusion.2), calls=%async_computation.2 | async-start | bytes 2359296 | tf_op jit(solution)/shard_map/all_to_all | solution.py:90
  401.0 23.7 %collective-permute-start.57 = (bf16[128,1024]{1,0:T(8,128)(2,1)S(1)}, bf16[128,1024]{1,0:T(8,128)(2,1)S(1)}, u32[]{:S(2)}, u32[]{:S(2)}) collective-permute-start(bf16[128,1024]{1,0:T(8,128)(2,1)S(1)} %copy-done.144), channel_id=1, source_target_pairs={{0,4},{4,0},{8,12},{12,8},{16,20},{20,16},{24,28},{28,24},{1,5},{5... | collective-permute-start | bytes 786440 | tf_op jit(solution)/shard_map/ppermute | solution.py:43
  401.2 67.3 %collective-permute-start.60 = (bf16[2,2,128,1024]{3,2,1,0:T(8,128)(2,1)}, bf16[2,2,128,1024]{3,2,1,0:T(8,128)(2,1)S(1)}, u32[]{:S(2)}, u32[]{:S(2)}) collective-permute-start(bf16[2,2,128,1024]{3,2,1,0:T(8,128)(2,1)} %copy-done.90), channel_id=1, source_target_pairs={{0,8},{4,12},{8,0},{12,4},{16,24},{20,28},{24,16},{28,20},{1,9},{5... | collective-permute-start | bytes 3145736 | tf_op jit(solution)/shard_map/ppermute | solution.py:43
  403.1 65.4 %collective-permute-start.61 = (bf16[384,1024]{1,0:T(8,128)(2,1)}, bf16[384,1024]{1,0:T(8,128)(2,1)}, u32[]{:S(2)}, u32[]{:S(2)}) collective-permute-start(bf16[384,1024]{1,0:T(8,128)(2,1)} %copy-done.139), channel_id=1, source_target_pairs={{0,16},{4,20},{8,24},{12,28},{16,0},{20,4},{24,8},{28,12},{1,17},{... | collective-permute-start | bytes 2359304 | tf_op jit(solution)/shard_map/ppermute | solution.py:43
  432.8 35.7 %collective-permute-start.58 = (bf16[2,128,1536]{2,1,0:T(8,128)(2,1)}, bf16[2,128,1536]{2,1,0:T(8,128)(2,1)}, u32[]{:S(2)}, u32[]{:S(2)}) collective-permute-start(bf16[2,128,1536]{2,1,0:T(8,128)(2,1)} %get-tuple-element.345), channel_id=1, source_target_pairs={{0,2},{2,0},{1,3},{3,1},{4,6},{6,4},{5,7},{7,5},{8,10},{10,8},{9,1... | collective-permute-start | bytes 2359304 | tf_op jit(solution)/shard_map/ppermute | solution.py:34
  433.9 34.6 %collective-permute-start.59 = (bf16[2,128,1024]{2,1,0:T(8,128)(2,1)}, bf16[2,128,1024]{2,1,0:T(8,128)(2,1)S(1)}, u32[]{:S(2)}, u32[]{:S(2)}) collective-permute-start(bf16[2,128,1024]{2,1,0:T(8,128)(2,1)} %get-tuple-element.342), channel_id=1, source_target_pairs={{0,4},{4,0},{8,12},{12,8},{16,20},{20,16},{24,28},{28,24},{1,5},{5... | collective-permute-start | bytes 1572872 | tf_op jit(solution)/shard_map/ppermute | solution.py:43
  434.0 51.4 %collective-permute-start.64 = (bf16[128,1024]{1,0:T(8,128)(2,1)}, bf16[128,1024]{1,0:T(8,128)(2,1)S(1)}, u32[]{:S(2)}, u32[]{:S(2)}) collective-permute-start(bf16[128,1024]{1,0:T(8,128)(2,1)} %copy-done.142), channel_id=1, source_target_pairs={{0,16},{4,20},{8,24},{12,28},{16,0},{20,4},{24,8},{28,12},{1,17},{... | collective-permute-start | bytes 786440 | tf_op jit(solution)/shard_map/ppermute | solution.py:43
  (203 other events, 1409.2 us)

commit v3 on v2

--- a/solution.py
+++ b/solution.py
@@ -71,21 +71,6 @@
     return value.reshape((2,) * levels + (value.shape[0] >> levels,) + value.shape[1:])
 
 
-def two_rows(value):
-    high = lax.reduce_precision(value, 8, 7)
-    return [high.astype(BF16), (value - high).astype(BF16)]
-
-
-def with_rows(values, rows):
-    count = lax.axis_size("dp")
-    width = values[0].shape[1]
-    block = jnp.stack([jnp.pad(r, (0, width - r.shape[0])) for r in rows])
-    block = jnp.pad(block, ((0, EXTRA - len(rows)), (0, 0)))
-    shares = [value.reshape(count, -1, width) for value in values]
-    block = jnp.broadcast_to(block[None], (count, EXTRA, width))
-    return jnp.concatenate(shares + [block], axis=1)
-
-
 def exchange(value):
     return lax.all_to_all(value, "dp", split_axis=0, concat_axis=0, tiled=True)
 
@@ -116,24 +101,27 @@
     return jnp.where(first, own, other), jnp.where(first, other, own)
 
 
-TIMES = {
-    "gate_and_up": 12.0,
-    "gate_and_up_back": 7.0,
-    "attend": 7.0,
-    "attend_back": 12.0,
-    "product_tn": 3.0,
-    "product_nt": 3.0,
-    "down_proj": 3.0,
-    "heads_forward": 3.5,
-    "heads_backward": 3.0,
-    "mid_all": 2.5,
+WINDOWS = {
+    "heads_kept": 6.0,
+    "attend": 2.0,
+    "out_own": 3.0,
+    "act_kept": 3.0,
+    "gate_and_up": 3.0,
+    "mid_sent": 3.0,
+    "mid_kept": 1.5,
+    "up_rows": 2.5,
+    "down_first": 3.0,
+    "attention_kept": 3.5,
+    "attend_back": 2.0,
+    "normed_in": 6.5,
+    "heads_second": 2.0,
 }
 
 
 def light(name):
-    amount = TIMES.get(name, 1.5) * 0.1
+    amount = WINDOWS.get(name, 0.05) * 0.1
     return pl.CostEstimate(
-        flops=int(amount * 1.15e9) + 1, bytes_accessed=int(amount * 3.69e6), transcendentals=0
+        flops=int(amount * 1.15e9), bytes_accessed=int(amount * 3.69e6), transcendentals=0
     )
 
 
@@ -186,7 +174,9 @@
     return local_call(kernel, values, [(shape, values[0].dtype)], name)[0]
 
 
-def product(left, right, kind, dtype, tile, part=0, size=None, block=0, rows=None):
+def product(
+    left, right, kind, dtype, tile, part=0, size=None, block=0, rows=None, name=None
+):
     contract = {"nn": ((1,), (0,)), "nt": ((1,), (1,)), "tn": ((0,), (0,))}[kind]
     size = right.shape[0] if size is None else size
     rows = left.shape[0] if rows is None else rows
@@ -215,7 +205,14 @@
         ).astype(out_ref.dtype)
 
     return grid_call(
-        kernel, steps, scalars(part), (left, right), specs, [out], [(shape, dtype)], "product_" + kind
+        kernel,
+        steps,
+        scalars(part),
+        (left, right),
+        specs,
+        [out],
+        [(shape, dtype)],
+        name or "product_" + kind,
     )[0]
 
 
@@ -244,7 +241,35 @@
     )
 
 
-def heads_forward(scaled, query_weight, key_weight, value_weight, part, dtype):
+def down_product(act_all, down_own, down_other, own_at, other_at, tile):
+    rows, width = act_all.shape
+    half, size, features = rows // 2, width // 2, down_own.shape[1]
+    quarter = half // 2
+
+    def kernel(picks, act_ref, own_ref, other_ref, kept_ref, near_ref, far_ref):
+        total = dot_nn(act_ref[:, :size], own_ref[...]) + dot_nn(act_ref[:, size:], other_ref[...])
+        kept_ref[...] = total[:half]
+        near_ref[...] = total[half : half + quarter].astype(BF16)
+        far_ref[...] = total[half + quarter :].astype(BF16)
+
+    return grid_call(
+        kernel,
+        features // tile,
+        scalars(own_at, other_at),
+        (act_all, down_own, down_other),
+        [
+            pl.BlockSpec(act_all.shape, lambda j, s: (0, 0)),
+            pl.BlockSpec((size, tile), lambda j, s: (s[0], j)),
+            pl.BlockSpec((size, tile), lambda j, s: (s[1], j)),
+        ],
+        [pl.BlockSpec((half, tile), lambda j, s: (0, j))]
+        + [pl.BlockSpec((quarter, tile), lambda j, s: (0, j))] * 2,
+        [((half, features), F32), ((quarter, features), BF16), ((quarter, features), BF16)],
+        "down_proj",
+    )
+
+
+def heads_forward(scaled, query_weight, key_weight, value_weight, part, dtype, name):
     group, features = scaled.shape
     query_part, tile = query_weight.shape[1] // 2, key_weight.shape[1] // 2
     steps = query_part // tile
@@ -276,7 +301,7 @@
         ],
         [pl.BlockSpec((group, tile), lambda j, s: (0, j))],
         [((group, query_part + 2 * tile), dtype)],
-        "heads_forward",
+        name,
     )[0]
 
 
@@ -374,7 +399,7 @@
 
 
 def up_back_kernel(picks, gate_grad_ref, up_grad_ref, gate_ref, up_ref, *refs):
-    *pieces, out_ref = refs
+    *pieces, near_ref, far_ref = refs
     count = len(pieces) // 2
     features = gate_ref.shape[0]
     share = pieces[0].shape[0]
@@ -382,14 +407,14 @@
     for i in range(features // (2 * share)):
         at = slice(i * 2 * share, (i + 1) * 2 * share)
         total = dot_nt(gate_grad, gate_ref[at, :]) + dot_nt(up_grad, up_ref[at, :])
-        out_ref[:, at] = total.astype(out_ref.dtype)
+        near_ref[:, at] = total.astype(near_ref.dtype)
     for i in range(count):
         total = dot_nt(gate_grad, pieces[i][...]) + dot_nt(up_grad, pieces[count + i][...])
-        at = pl.multiple_of(features + picks[1 + i] * share, share)
-        out_ref[:, pl.ds(at, share)] = total.astype(out_ref.dtype)
-
-
-def gate_and_up_back(gate_grad, up_grad, block, gate, up, base, pieces, places, dtype):
+        at = pl.multiple_of(picks[1 + i] * share, share)
+        far_ref[:, pl.ds(at, share)] = total.astype(far_ref.dtype)
+
+
+def gate_and_up_back(gate_grad, up_grad, block, gate, up, base, pieces, places, dtype, name):
     rows = gate_grad.shape[0] // 2
     width = gate_grad.shape[1]
     features = gate.shape[0]
@@ -397,17 +422,17 @@
     own = pl.BlockSpec((features, width), lambda j, s: (0, s[0]))
     pieces = (*pieces[0], *pieces[1])
     piece = pl.BlockSpec(pieces[0].shape, lambda j, s: (0, 0))
-    shape = (rows, features + len(places) * pieces[0].shape[0])
+    shape = (rows, features)
     return grid_call(
         up_back_kernel,
         1,
         scalars(base, *places),
         (gate_grad, up_grad, gate, up, *pieces),
         [grads, grads, own, own] + [piece] * len(pieces),
-        [pl.BlockSpec(shape, lambda j, s: (0, 0))],
-        [(shape, dtype)],
-        "gate_and_up_back",
-    )[0]
+        [pl.BlockSpec(shape, lambda j, s: (0, 0))] * 2,
+        [(shape, dtype)] * 2,
+        name,
+    )
 
 
 def in_place(weight):
@@ -536,16 +561,18 @@
     )
 
 
-def join_core_kernel(kept_ref, got_ref, own_ref, row_ref, z_ref, row_both_ref, z_both_ref):
-    half, features = own_ref.shape
+def join_core_kernel(
+    near_ref, far_ref, got_near, got_far, own_ref, row_ref, z_ref, row_both_ref, z_both_ref
+):
+    half = own_ref.shape[0]
     quarter = half // 2
-    near = kept_ref[:half, :] + got_ref[:half, :].astype(F32)
-    far = kept_ref[half:, :] + got_ref[half:, :].astype(F32)
-    own_ref[...] = near[:, :features]
-    row_ref[...] = near[:, features:]
-    z_ref[...] = far[:, :features]
-    row_both_ref[...] = far[:quarter, features:].astype(BF16)
-    z_both_ref[...] = far[quarter:, features:].astype(BF16)
+    near = near_ref[...] + got_near[...].astype(F32)
+    far = far_ref[...] + got_far[...].astype(F32)
+    own_ref[...] = near[:half]
+    row_ref[...] = far[:half]
+    z_ref[...] = near[half:]
+    row_both_ref[...] = far[half : half + quarter].astype(BF16)
+    z_both_ref[...] = far[half + quarter :].astype(BF16)
 
 
 def join_corner_kernel(row_ref, z_ref, via_row_ref, via_z_ref, to_row_ref, to_z_ref):
@@ -652,14 +679,37 @@
         sent_ref[:, :, at] = total[1].astype(BF16)
 
 
+def pack_back(grad, attention_part, feedforward_part, head_gains, count):
+    rows, features = grad.shape
+    share = rows // count
+
+    def kernel(grad_ref, attention_ref, feedforward_ref, heads_ref, out_ref):
+        rest = jnp.zeros((1, features - 2 * HEAD_SIZE), F32)
+        heads = jnp.concatenate([heads_ref[:1, :], heads_ref[1:, :], rest], axis=1)
+        values = jnp.concatenate([attention_ref[...], feedforward_ref[...], heads, heads], axis=0)
+        high = values.astype(BF16)
+        low = (values - high.astype(F32)).astype(BF16)
+        extra = jnp.concatenate([high.astype(F32), low.astype(F32)], axis=0).astype(BF16)
+        for i in range(count):
+            out_ref[i, :share, :] = grad_ref[i * share : (i + 1) * share, :]
+            out_ref[i, share:, :] = extra
+
+    return local_call(
+        kernel,
+        (grad, attention_part, feedforward_part, head_gains),
+        [((count, share + EXTRA, features), BF16)],
+        "pack_back",
+    )[0]
+
+
 def layer_out_kernel(mid_ref, kept_ref, got_ref, out_ref):
     out_ref[...] = (mid_ref[...] + kept_ref[...] + got_ref[...].astype(F32)).astype(BF16)
 
 
-def out_near_kernel(kept_ref, got_ref, near_ref, far_ref):
+def out_near_kernel(kept_ref, got_near, got_far, near_ref, far_ref):
     half = near_ref.shape[0]
-    near_ref[...] = kept_ref[:half, :] + got_ref[:half, :].astype(F32)
-    far_ref[...] = (kept_ref[half:, :] + got_ref[half:, :].astype(F32)).astype(BF16)
+    near_ref[...] = kept_ref[:half, :] + got_near[...].astype(F32)
+    far_ref[...] = (kept_ref[half:, :] + got_far[...].astype(F32)).astype(BF16)
 
 
 def turn(values, cosine, sine):
@@ -913,10 +963,12 @@
         "scaled",
     )
     moved_grad = exchange(after(cotangent, moved_in))
-    heads_sent = heads_forward(after(scaled_in, got_gate, got_up), *projections, 1 - row, BF16)
+    heads_sent = heads_forward(after(scaled_in, got_gate, got_up), *projections, 1 - row, BF16, "heads_sent")
     got_square = swap_row(square)
     got_heads = swap_row(heads_sent)
-    kept_heads = heads_forward(after(scaled_in, heads_sent), *projections, row, F32)
+    kept_heads = heads_forward(
+        after(scaled_in, heads_sent), *projections, row, F32, "heads_kept"
+    )
     got_gate, got_up = together(got_gate, got_up, heads_sent)[:2]
     got_gate_x, got_up_x = swap_dp(got_gate, 1), swap_dp(got_up, 1)
     got_gate_w, got_up_w = swap_dp(got_gate, 4), swap_dp(got_up, 4)
@@ -924,8 +976,8 @@
     down_own, own_at = ff_block(down_weight, row, 0)
     down_other, other_at = ff_block(down_weight, 1 - row, 0)
 
-    def act_back(rows_of, weight, at, dtype):
-        return product(rows_of, weight, "nt", dtype, ff_part // 3, at, ff_part)
+    def act_back(rows_of, weight, at, dtype, name="act_sent"):
+        return product(rows_of, weight, "nt", dtype, ff_part // 3, at, ff_part, name=name)
 
     moved_grad = after(moved_grad, kept_heads)
     grad_z = swap_z(moved_grad)
@@ -954,7 +1006,9 @@
     attention, got_act[0], grad_far = together(attention, got_act[0], grad_far)
     attention_other = swap_row(attention)
     got_act.append(swap_row(after(act_sent[1], attention)))
-    out_own = product(attention, output_weight, "nn", F32, features // 2, row, query_part)
+    out_own = product(
+        attention, output_weight, "nn", F32, features // 2, row, query_part, name="out_own"
+    )
     far_sent = [
         act_back(after(rows_of, out_own), down_other, other_at, BF16)
         for rows_of in (grad_z, grad_far)
@@ -993,7 +1047,7 @@
 
     by_row = swap_row(normed_mid)
     by_z = swap_z(normed_mid)
-    act_kept = act_back(after(grad_all, normed_mid), down_own, own_at, F32)
+    act_kept = act_back(after(grad_all, normed_mid), down_own, own_at, F32, "act_kept")
     by_row, by_z, act_kept, got_up_wx = together(by_row, by_z, act_kept, got_up_wx)
     corner_a = swap_row(by_z[:quarter])
     corner_b = swap_z(by_row[quarter:])
@@ -1025,46 +1079,44 @@
         mid_all, *up_weights, act_kept, (got_act[0], got_act[2], got_act[1], got_act[3])
     )
 
-    quarters = [activated[i * half : (i + 1) * half] for i in range(4)]
-    others = [swap_row(quarters[0])]
+    act_got = swap_row(activated)
     line = Line(activated)
     top_bit, lower_bits = all_bits[0], all_bits[1:]
-
-    def up_rows(grad_part):
-        whole = product(mid_all, grad_part, "tn", BF16, features // 2)
+    top_place = jnp.where(my_bit(top_bit) == row, 0, 1)
+
+    def up_rows(grad_part, name):
+        whole = product(mid_all, grad_part, "tn", BF16, features // 2, name=name)
         return whole.reshape((2,) * (levels + 1) + (features // count, ff_part))
-
-    def down_part(part, rows_of):
-        whole = product(part, rows_of, "tn", BF16, ff_part // 2)
-        return split_rows(whole, levels - 2)
 
     def first_stage(value, axis, bit):
         sent = line.passed(take(value, axis, 1 - my_bit(bit)))
         return swap_dp(sent, bit)
 
-    def late_stage(value, got, axis, bit, next_axis, next_bit):
-        kept, sent = end_stage(value, line.hold(got), axis, bit, next_axis, my_bit(next_bit))
+    def late_stage(value, got, axis, bit, next_axis, next_bit, place=None):
+        place = my_bit(next_bit) if place is None else place
+        kept, sent = end_stage(value, line.hold(got), axis, bit, next_axis, place)
         return kept, swap_dp(line.passed(sent), next_bit)
 
-    mid_sent = line.passed(gate_and_up_back(gate_grad, up_grad, 1, *up_weights, BF16))
-    got_mid = swap_col(mid_sent)
-    gate_grad, others[0] = line.hold(gate_grad, others[0])
-    gate_rows = up_rows(gate_grad)
+    mid_sent = gate_and_up_back(gate_grad, up_grad, 1, *up_weights, BF16, "mid_sent")
+    line.passed(mid_sent[0])
+    got_mid = [swap_col(sent) for sent in mid_sent]
+    gate_rows = up_rows(line.hold(gate_grad), "gate_rows")
     gate_got = first_stage(gate_rows, levels, 1)
-    mid_kept = gate_and_up_back(line.hold(gate_grad), up_grad, 0, *up_weights, F32)
+    mid_kept = gate_and_up_back(line.hold(gate_grad), up_grad, 0, *up_weights, F32, "mid_kept")
+    *got_mid, kept_near, act_got = together(*got_mid, mid_kept[0], act_got)
     block = (half, features)
     mid_own, to_row, to_z, row_both, z_both = local_call(
         join_core_kernel,
-        (mid_kept, got_mid),
+        (kept_near, mid_kept[1], *got_mid),
         [(block, F32)] * 3 + [((quarter, features), BF16)] * 2,
         "join_core",
     )
     via_row = swap_row(row_both)
     via_z = swap_z(z_both)
     line.passed(row_both)
-    up_cols = up_rows(line.hold(up_grad))
-    up_got = first_stage(up_cols, levels, 1)
-    via_row, via_z = line.hold(via_row, via_z)
+    up_cols = up_rows(line.hold(up_grad), "up_rows")
+    up_sent = line.passed(take(up_cols, levels, 1 - xbit))
+    via_row, via_z, up_sent = line.hold(via_row, via_z, up_sent)
     to_row, to_z = local_call(
         join_corner_kernel,
         (to_row, to_z, via_row, via_z),
@@ -1072,15 +1124,20 @@
         "join_corner",
     )
     got_row, got_z = swap_row(to_row), swap_z(to_z)
+    up_got = swap_dp(up_sent, 1)
     line.passed(to_row)
-    down_first = down_part(activated, line.hold(grad_all))
-    down_got = first_stage(down_first, down_first.ndim - 3, 1)
-    got_row, got_z = line.hold(got_row, got_z)
+    act_all = assemble(
+        (pair, 2 * ff_part), [(0, 0, activated), (0, ff_part, line.hold(act_got))], "act_all"
+    )
+    down_rows = product(act_all, grad_all, "tn", BF16, ff_part // 2, name="down_first")
+    down_rows = split_rows(down_rows, levels - 1)
+    down_sent = line.passed(take(down_rows, levels - 2, 1 - xbit))
+    got_row, got_z, down_sent = line.hold(got_row, got_z, down_sent)
     normed_mid_grad, mid_sum, feedforward_part = norm_sums(
         (mid_own, got_row, got_z), stream_mid, inverse_mid, gain_mid
     )
     got_sum = swap_row(line.passed(mid_sum))
-    others.append(swap_row(line.hold(quarters[1])))
+    down_got = swap_dp(down_sent, 1)
     got_sum, gate_got = line.hold(got_sum, gate_got)
     stream_mid_grad, branch_low = norm_grad(
         normed_mid_grad, stream_mid, inverse_mid, gain_mid, mid_sum, got_sum, moved_grad, (F32, BF16)
@@ -1092,28 +1149,42 @@
         (group, features), [(0, 0, branch_low), (half, 0, line.hold(branch_got))], "branch"
     )
     attention_sent = product(branch, output_weight, "nt", BF16, query_part, 1 - row, query_part)
-    attention_sent, others[1] = together(attention_sent, others[1])
     got_attention = swap_row(attention_sent)
     line.passed(attention_sent)
 
-    others.extend(swap_row(line.hold(part)) for part in quarters[2:])
     attention_kept = line.passed(
-        product(line.hold(branch), output_weight, "nt", F32, query_part, row, query_part)
-    )
-    output_first, output_sent = [], []
-    for part in (attention, attention_other):
-        whole = product(line.hold(part), branch, "tn", BF16, query_part // 2)
-        whole = split_rows(whole, levels - 1)
-        output_sent.append(line.passed(take(whole, whole.ndim - 4, 1 - zbit)))
-        output_first.append(whole)
-    got_attention, *output_sent = line.hold(got_attention, *output_sent)
+        product(
+            line.hold(branch),
+            output_weight,
+            "nt",
+            F32,
+            query_part,
+            row,
+            query_part,
+            name="attention_kept",
+        )
+    )
+    attention_all = assemble(
+        (group, 2 * query_part),
+        [(0, 0, line.hold(attention)), (0, query_part, attention_other)],
+        "attention_all",
+    )
+    output_rows = product(attention_all, branch, "tn", BF16, query_part, name="output_rows")
+    output_rows = split_rows(output_rows, levels)
+    output_sent = line.passed(take(output_rows, levels - 2, 1 - zbit))
+    output_got = swap_dp(output_sent, 2)
+    out_kept, *out_sent = down_product(
+        line.hold(act_all), down_own, down_other, own_at, other_at, features // 2
+    )
+    line.passed(out_kept)
+    out_got = [swap_col(sent) for sent in out_sent]
+    got_attention, out_kept = line.hold(got_attention, out_kept)
     line.passed(got_attention)
-    output_got = [swap_dp(sent, 2) for sent in output_sent]
     projected_grad, head_gains = attend_back(
         kept_heads, got_heads, shared, attention_kept, line.hold(got_attention), kv_heads, repeat
     )
-    projected_grad, others[2], others[3], gate_got, up_got, down_got = together(
-        projected_grad, others[2], others[3], gate_got, up_got, down_got
+    projected_grad, up_got, gate_got, output_got, *out_got = together(
+        projected_grad, up_got, gate_got, output_got, *out_got
     )
     projected_other = swap_row(projected_grad)
     line.passed(projected_grad)
@@ -1126,77 +1197,43 @@
         "normed_in",
     )
 
-    def projection_rows(part):
-        whole = split_rows(product(normed_in, part, "tn", BF16, features // 2), levels)
-        return whole, first_stage(whole, levels - 2, 2)
-
-    heads_first, heads_got = projection_rows(line.hold(projected_grad))
-    activated_other = assemble(
-        (pair, ff_part),
-        [(i * half, 0, other) for i, other in enumerate(line.hold(*others))],
-        "activated_other",
-    )
-    down_second = down_part(activated_other, grad_all)
-    down_got_other = first_stage(down_second, down_second.ndim - 3, 1)
+    def projection_rows(part, name):
+        whole = product(normed_in, part, "tn", BF16, features // 2, name=name)
+        whole = split_rows(whole, levels)
+        return whole, line.passed(take(whole, levels - 2, 1 - zbit))
+
+    heads_first, heads_sent_own = projection_rows(line.hold(projected_grad), "heads_first")
     in_own = line.passed(heads_backward(line.hold(projected_grad), *projections, row)[0])
-    out_own = line.passed(
-        product(line.hold(activated), down_own, "nn", F32, features // 2, own_at, ff_part)
-    )
-    out_kept, out_sent = product_onto(
-        line.hold(activated_other),
-        down_other,
-        other_at,
-        ff_part,
-        out_own,
-        features // 2,
-        "down_proj",
-    )
-    out_got = swap_col(line.passed(out_sent))
+    heads_got = swap_dp(heads_sent_own, 2)
     out_near, out_far = local_call(
-        out_near_kernel, (out_kept, line.hold(out_got)), [(block, F32), (block, BF16)], "out_near"
-    )
-    line.passed(out_far)
-    projected_other, in_own, out_far, down_got_other, *output_got = line.hold(
-        projected_other, in_own, out_far, down_got_other, *output_got
-    )
-    layer_z = swap_z(out_far)
+        out_near_kernel, (out_kept, *line.hold(*out_got)), [(block, F32), (block, BF16)], "out_near"
+    )
+    layer_z = swap_z(line.passed(out_far))
+    projected_other, in_own, down_got = line.hold(projected_other, in_own, down_got)
     line.passed(projected_other)
     in_kept, in_sent = heads_backward(projected_other, *projections, 1 - row, in_own)
     in_got = swap_col(line.passed(in_sent))
-    down_rows = []
-    for v, got in ((down_first, down_got), (down_second, down_got_other)):
-        down_rows.append(line.passed(end_stage(v, line.hold(got), v.ndim - 3, 1)))
-    down_kept, down_sent = split_top(*down_rows, row)
-    down_got = swap_dp(line.passed(down_sent), top_bit)
+    down_rows, down_got = late_stage(down_rows, down_got, levels - 2, 1, 0, top_bit, top_place)
     in_values = (moved_in, inverse_in[:, :half], gain_in)
     normed_in_grad, in_sum, attention_part = norm_sums(
         (in_kept, line.hold(in_got)), *in_values
     )
     got_sum = swap_row(line.passed(in_sum))
-    output_rows, output_got = zip(
-        *(
-            late_stage(v, got, v.ndim - 4, 2, v.ndim - 4, 1)
-            for v, got in zip(output_first, output_got)
-        )
-    )
-    heads_second, heads_got_other = projection_rows(line.hold(projected_other))
-    got_sum, up_got, heads_got, layer_z = line.hold(got_sum, up_got, heads_got, layer_z)
+    output_rows, output_got = late_stage(
+        output_rows, output_got, levels - 2, 2, levels - 2, 1
+    )
+    heads_second, heads_sent_other = projection_rows(line.hold(projected_other), "heads_second")
+    got_sum, up_got, heads_got, heads_sent_other = line.hold(
+        got_sum, up_got, heads_got, heads_sent_other
+    )
+    heads_got_other = swap_dp(heads_sent_other, 2)
     (stream_grad,) = norm_grad(
         normed_in_grad, *in_values, in_sum, got_sum, stream_mid_grad, (BF16,)
     )
-    (layer_out,) = local_call(
-        layer_out_kernel, (stream_mid, out_near, line.hold(layer_z)), [(block, BF16)], "layer_out"
-    )
-    rows = two_rows(attention_part[0]) + two_rows(feedforward_part[0])
-    rows += two_rows(head_gains.reshape(-1))
-    back = exchange(line.passed(with_rows((stream_grad, layer_out), rows)))
-
-    output_rows = [
-        line.passed(add_got(kept, line.hold(got))) for kept, got in zip(output_rows, output_got)
-    ]
-    output_kept, output_sent = split_top(*output_rows, row)
-    output_got = swap_dp(line.passed(output_sent), top_bit)
-    heads_own, heads_got = late_stage(heads_first, heads_got, levels - 2, 2, levels - 2, 1)
+    grad_back = exchange(
+        line.passed(pack_back(stream_grad, attention_part, feedforward_part, head_gains, count))
+    )
+
     for bit in lower_bits:
         gate_rows, gate_got = late_stage(gate_rows, gate_got, None, None, 1, bit)
         up_cols, up_got = late_stage(up_cols, up_got, None, None, 1, bit)
@@ -1208,22 +1245,29 @@
         "side",
     )
     side_got = swap_row(line.passed(side_sent))
-    back, side_got, heads_got, heads_got_other, down_got = line.hold(
-        back, side_got, heads_got, heads_got_other, down_got
+    heads_own, heads_got = late_stage(heads_first, heads_got, levels - 2, 2, levels - 2, 1)
+    (layer_out,) = local_call(
+        layer_out_kernel, (stream_mid, out_near, line.hold(layer_z)), [(block, BF16)], "layer_out"
+    )
+    line.passed(layer_out)
+    output_got, side_got, heads_got, layer_out = line.hold(
+        output_got, side_got, heads_got, layer_out
     )
     line.passed(side_got)
+    output_rows, output_got = late_stage(
+        output_rows, output_got, None, None, 0, top_bit, top_place
+    )
     heads_own, heads_got = late_stage(heads_own, heads_got, None, None, 0, top_bit)
+    sent = jnp.stack([pick(part, 1 - zbit, 0).astype(BF16) for part in (side_own, side_got)])
+    side_z = swap_z(line.passed(sent))
+    grad_back, layer_out = line.hold(grad_back, layer_out)
+    line.passed(grad_back)
+    out_back = exchange(layer_out)
+    heads_got_other, down_got = line.hold(heads_got_other, down_got)
+    line.passed(down_got)
     heads_other, heads_got_other = late_stage(
         heads_second, heads_got_other, levels - 2, 2, levels - 2, 1
     )
-    side_got = line.hold(side_got)
-    sent = jnp.stack([pick(part, 1 - zbit, 0).astype(BF16) for part in (side_own, side_got)])
-    side_z = swap_z(line.passed(sent))
-    output_got, heads_got, heads_got_other, side_z = line.hold(
-        output_got, heads_got, heads_got_other, side_z
-    )
-    line.passed(heads_got)
-    heads_other, heads_got_other = late_stage(heads_other, heads_got_other, None, None, 0, top_bit)
 
     def finish(kept, got):
         value = line.passed(add_got(kept, line.hold(got)))
@@ -1233,9 +1277,10 @@
             ).astype(F32)
         return value
 
-    output_weight_grad = finish(output_kept, output_got)
-    down_grad = finish(down_kept, down_got)
-    heads_grad_own = finish(heads_own, heads_got)
+    down_grad = finish(down_rows, down_got)
+    heads_other, heads_got_other = late_stage(heads_other, heads_got_other, None, None, 0, top_bit)
+    output_weight_grad = finish(output_rows, output_got)
+    side_z = line.hold(side_z)
 
     def up_columns(at):
         columns = slice(at, at + ff_part)
@@ -1257,8 +1302,10 @@
             axis=1,
         )
 
-    gate_weight_grad = line.passed(up_columns(0))
-    up_weight_grad = up_columns(ff_part)
+    gate_weight_grad = up_columns(0)
+    up_weight_grad = line.passed(up_columns(ff_part))
+    heads_grad_own = finish(heads_own, heads_got)
+    out_back = line.passed(line.hold(out_back))
     heads_grad_other = finish(heads_other, heads_got_other)
 
     def head_grad(start, width):
@@ -1270,12 +1317,11 @@
     key_weight_grad = head_grad(query_part, key_part)
     value_weight_grad = head_grad(query_part + key_part, key_part)
 
-    back = back.reshape(count, -1, features).astype(F32)
-    share = half // count
-    grad_back = back[:, :share].reshape(half, features)
-    out_back = back[:, share : 2 * share].reshape(half, features)
-    totals = jnp.sum(back[:, 2 * share :], axis=0)
-    gains = jnp.concatenate([totals[i] + totals[i + 1] for i in (0, 2, 4)])[None]
+    back = grad_back.reshape(count, -1, features).astype(F32)
+    grad_back = back[:, :-EXTRA].reshape(half, features)
+    totals = jnp.sum(back[:, -EXTRA:], axis=0)
+    out_back = out_back.astype(F32)
+    gains = jnp.concatenate([totals[i] + totals[i + 4] for i in range(3)])[None]
     gains = gains + swap_col(gains)
     gain_low, gain_high = (part[0] for part in by_half(row, gains, swap_row(gains)))
     attention_total = jnp.concatenate([gain_low[:features], gain_high[:features]])

time: 524 us -> 477 us (0.910)
  waiting for transfers between devices: 202 us -> 162 us
  local copies, waits for them, and re-layouts: 65.7 us -> 58 us
    ppermute x31 -> x28, waiting for transfers between devices: 130 us -> 99.5 us  [swap_dp(): return lax.ppermute(value, 'dp', [(i, i ^ bit) for i in range(count)])]
    ppermute x24 -> x21, waiting for transfers between devices: 60.7 us -> 43 us  [swap_row(): return lax.ppermute(value, 'row', [(0, 1), (1, 0)])]
    all_to_all x3 -> x4, waiting for transfers between devices: 8.63 us -> 16.5 us  [exchange(): return lax.all_to_all(value, 'dp', split_axis=0, concat_axis=0, tiled=True)]
    unnamed x310 -> x262, local copies, waits for them, and re-layouts: 52.1 us -> 46.2 us
    pallas_call x23, Pallas kernels: 21.2 us -> 26.7 us  [local_call(): pl.pallas_call(kernel, out_shape=[jax.ShapeDtypeStruct(shape, dtype) for...]
    ppermute x31 -> x28, starting transfers between devices: 36.3 us -> 31.9 us  [swap_dp(): return lax.ppermute(value, 'dp', [(i, i ^ bit) for i in range(count)])]
    ppermute x24 -> x21, starting transfers between devices: 28.8 us -> 24.5 us  [swap_row(): return lax.ppermute(value, 'row', [(0, 1), (1, 0)])]
    all_to_all x3 -> x4, starting transfers between devices: 15.3 us -> 19.3 us  [exchange(): return lax.all_to_all(value, 'dp', split_axis=0, concat_axis=0, tiled=True)]
  transfers between devices with their start and end apart: 72 -> 69, of which waited for: 34 -> 31; matrix products, arithmetic and copies ran while one was open for 4% -> 5% of each run, Pallas kernels for 21% -> 28%
where the time goes in v3:
time: 477 us; the launch traced here: 472 us
  waiting for transfers between devices  162 us (34%)
  Pallas kernels  157 us (33%)
  starting transfers between devices  76.9 us (16%)
  local copies, waits for them, and re-layouts  58 us (12%)
  other arithmetic  15.9 us (3%)
    pallas_call x40, Pallas kernels, grid_call(): pl.pallas_call(kernel, grid_spec=pltpu.PrefetchScalarGridSpec(num_scalar_...  111 us
    ppermute x28, waiting for transfers between devices, swap_dp(): return lax.ppermute(value, 'dp', [(i, i ^ bit) for i in range(count)])  99.5 us
    unnamed x262, local copies, waits for them, and re-layouts  46.2 us
    ppermute x21, waiting for transfers between devices, swap_row(): return lax.ppermute(value, 'row', [(0, 1), (1, 0)])  43 us
    ppermute x28, starting transfers between devices, swap_dp(): return lax.ppermute(value, 'dp', [(i, i ^ bit) for i in range(count)])  31.9 us
    pallas_call x23, Pallas kernels, local_call(): pl.pallas_call(kernel, out_shape=[jax.ShapeDtypeStruct(shape, dtype) for...  26.7 us
    ppermute x21, starting transfers between devices, swap_row(): return lax.ppermute(value, 'row', [(0, 1), (1, 0)])  24.5 us
    all_to_all x4, starting transfers between devices, exchange(): return lax.all_to_all(value, 'dp', split_axis=0, concat_axis=0, tiled=True)  19.3 us
  transfers between devices with their start and end apart: 69, of which 31 were waited for; matrix products, arithmetic and copies ran while one was open for 5% of the time, Pallas kernels for 28%

profile of v3, /device:TPU:0, one launch (start us, length us, event | category | flops | bytes accessed | tf_op | source)
XLA Modules:
  0.0 472.3 jit_solution(7947084116932348461)
XLA Ops:
  7.1 6.3 %all-to-all-start = ((bf16[8,32,1024]{2,1,0:T(8,128)(2,1)}), bf16[8,32,1024]{2,1,0:T(8,128)(2,1)S(1)}, u32[]{:S(2)}, u32[]{:S(2)}) async-start(bf16[8,32,1024]{2,1,0:T(8,128)(2,1)} %bitcast.1), calls=%async_computation | async-start | bytes 1048576 | tf_op jit(solution)/shard_map/all_to_all | solution.py:75
  16.7 6.2 %collective-permute-done.1.refs_4_ = bf16[256,768]{1,0:T(8,128)(2,1)S(1)} collective-permute-done((bf16[256,768]{1,0:T(8,128)(2,1)S(1)}, bf16[256,768]{1,0:T(8,128)(2,1)S(1)}, u32[]{:S(2)}, u32[]{:S(2)}) %collective-permute-start.1) | collective-permute-done | bytes 393248 | tf_op jit(solution)/shard_map/ppermute | solution.py:34
  28.0 4.7 all-to-all-start.1
  43.3 4.8 %all-to-all-done.1 = bf16[8,32,1024]{2,1,0:T(8,128)(2,1)} async-done(((bf16[8,32,1024]{2,1,0:T(8,128)(2,1)}), bf16[8,32,1024]{2,1,0:T(8,128)(2,1)}, u32[]{:S(2)}, u32[]{:S(2)}) %all-to-all-start.1) | async-done | bytes 524320 | tf_op jit(solution)/shard_map/all_to_all | solution.py:75
  59.1 5.4 %collective-permute-done.4 = f32[8,512]{1,0:T(8,128)S(1)} collective-permute-done((f32[8,512]{1,0:T(8,128)}, f32[8,512]{1,0:T(8,128)S(1)}, u32[]{:S(2)}, u32[]{:S(2)}) %collective-permute-start.4) | collective-permute-done | bytes 16416 | tf_op jit(solution)/shard_map/ppermute | solution.py:34
  73.5 7.2 %attend.1.left_ref.refs_0_ = bf16[512,512]{1,0:T(8,128)(2,1)S(1)} custom-call(f32[512,1024]{1,0:T(8,128)S(1)} %heads_kept.1.query_own.key_own.value_own, bf16[512,1024]{1,0:T(8,128)(2,1)S(1)} %collective-permute-done.3.query_got.key_got.value_got, f32[512,1024]{1,0:T(8,128)S(1)} %heads_kept.1.query_own.key_own.value_own, ...), custom_call_target="tpu_custom_call" | custom-call | flops 230000000 | bytes 738000 | tf_op jit(solution)/shard_map/attend/pallas_call | solution.py:845
  98.7 7.0 %collective-permute-done.15.refs_6_ = bf16[256,768]{1,0:T(8,128)(2,1)} collective-permute-done((bf16[256,768]{1,0:T(8,128)(2,1)S(1)}, bf16[256,768]{1,0:T(8,128)(2,1)}, u32[]{:S(2)}, u32[]{:S(2)}) %collective-permute-start.15) | collective-permute-done | bytes 393248 | tf_op jit(solution)/shard_map/ppermute | solution.py:43
  136.2 4.9 %collective-permute-done.21.refs_3_ = bf16[128,1024]{1,0:T(8,128)(2,1)} collective-permute-done((bf16[128,1024]{1,0:T(8,128)(2,1)S(1)}, bf16[128,1024]{1,0:T(8,128)(2,1)}, u32[]{:S(2)}, u32[]{:S(2)}) %collective-permute-start.21) | collective-permute-done | bytes 262176 | tf_op jit(solution)/shard_map/ppermute | solution.py:34
  151.2 6.3 %collective-permute-done.28.refs_10_ = bf16[256,768]{1,0:T(8,128)(2,1)} collective-permute-done((bf16[256,768]{1,0:T(8,128)(2,1)}, bf16[256,768]{1,0:T(8,128)(2,1)}, u32[]{:S(2)}, u32[]{:S(2)}) %collective-permute-start.28) | collective-permute-done | bytes 393248 | tf_op jit(solution)/shard_map/ppermute | solution.py:34
  157.7 12.6 %gate_and_up.1 = (bf16[1024,768]{1,0:T(8,128)(2,1)S(1)}, bf16[1024,768]{1,0:T(8,128)(2,1)S(1)}, bf16[1024,768]{1,0:T(8,128)(2,1)}) custom-call(s32[5]{0:T(128)S(1)} %copy-done.110, bf16[1024,2048]{1,0:T(8,128)(2,1)} %copy-done, bf16[1024,3072]{1,0:T(8,128)(2,1)} %gate_ref.5, bf16[1024,3072]{1,0:T(8,128)(2,1)} %up_ref.5, ...), custom_call_target="tpu_custom_call" | custom-call | flops 345000000 | bytes 1107000 | tf_op jit(solution)/shard_map/gate_and_up/pallas_call | solution.py:155
  171.9 7.4 %mid_sent.1 = (bf16[512,1024]{1,0:T(8,128)(2,1)}, bf16[512,1024]{1,0:T(8,128)(2,1)}) custom-call(s32[5]{0:T(128)S(1)} %copy-done.110, bf16[1024,768]{1,0:T(8,128)(2,1)S(1)} %get-tuple-element.239.gate_grad_ref.right_ref, bf16[1024,768]{1,0:T(8,128)(2,1)S(1)} %get-tuple-element.251.up_grad_ref.right_ref, bf16[1024,3072]{1,0:T(8,128)(2,1)} %gate_ref.5, ...), custom_call_target="tpu_custom_call" | custom-call | flops 345000000 | bytes 1107000 | tf_op jit(solution)/shard_map/mid_sent/pallas_call | solution.py:155
  191.9 6.1 %mid_kept.1 = (f32[512,1024]{1,0:T(8,128)S(1)}, f32[512,1024]{1,0:T(8,128)S(1)}) custom-call(s32[5]{0:T(128)S(1)} %copy-done.111, bf16[1024,768]{1,0:T(8,128)(2,1)S(1)} %copy-done.22, bf16[1024,768]{1,0:T(8,128)(2,1)S(1)} %copy-done.19, bf16[1024,3072]{1,0:T(8,128)(2,1)} %gate_ref.5, bf16[1024,3072]{1,0:T(8,128)(2,1)} %up_ref.5, ...), custom_call_target="tpu_custom_call" | custom-call | flops 172500000 | bytes 553500 | tf_op jit(solution)/shard_map/mid_kept/pallas_call | solution.py:155
  198.1 8.6 %collective-permute-done.32.refs_1_ = bf16[1024,768]{1,0:T(8,128)(2,1)} collective-permute-done((bf16[1024,768]{1,0:T(8,128)(2,1)}, bf16[1024,768]{1,0:T(8,128)(2,1)}, u32[]{:S(2)}, u32[]{:S(2)}) %collective-permute-start.32) | collective-permute-done | bytes 1572896 | tf_op jit(solution)/shard_map/ppermute | solution.py:34
  221.9 4.6 down_first.1
  256.1 5.8 %down_proj.1 = (f32[512,1024]{1,0:T(8,128)S(1)}, bf16[256,1024]{1,0:T(8,128)(2,1)S(1)}, bf16[256,1024]{1,0:T(8,128)(2,1)S(1)}) custom-call(s32[2]{0:T(128)S(1)} %pad_add_fusion.4.picks, bf16[1024,1536]{1,0:T(8,128)(2,1)S(1)} %copy-done.12, bf16[3072,1024]{1,0:T(8,128)(2,1)} %other_ref.1, bf16[3072,1024]{1,0:T(8,128)(2,1)} %other_ref.1), custom_call_target="tpu_custom_call" | custom-call | flops 5750000 | bytes 18450 | tf_op jit(solution)/shard_map/down_proj/pallas_call | solution.py:155
  263.3 20.0 %collective-permute-done.42.refs_2_ = bf16[2,2,128,768]{3,2,1,0:T(8,128)(2,1)} collective-permute-done((bf16[2,2,128,768]{3,2,1,0:T(8,128)(2,1)}, bf16[2,2,128,768]{3,2,1,0:T(8,128)(2,1)}, u32[]{:S(2)}, u32[]{:S(2)}) %collective-permute-start.42) | collective-permute-done | bytes 786464 | tf_op jit(solution)/shard_map/ppermute | solution.py:43
  284.6 11.9 %attend_back.1 = (bf16[512,1024]{1,0:T(8,128)(2,1)S(1)}, f32[2,128]{1,0:T(2,128)S(1)}) custom-call(f32[512,1024]{1,0:T(8,128)S(1)} %heads_kept.1.query_own.key_own.value_own, bf16[512,1024]{1,0:T(8,128)(2,1)S(1)} %collective-permute-done.3.query_got.key_got.value_got, f32[512,1024]{1,0:T(8,128)S(1)} %heads_kept.1.query_own.key_own.value_own, ...), custom_call_target="tpu_custom_call" | custom-call | flops 230000000 | bytes 738000 | tf_op jit(solution)/shard_map/attend_back/pallas_call | solution.py:860
  311.8 8.3 %collective-permute-done.47.keep_got.send_got = bf16[2,384,1024]{2,1,0:T(8,128)(2,1)S(1)} collective-permute-done((bf16[2,384,1024]{2,1,0:T(8,128)(2,1)S(1)}, bf16[2,384,1024]{2,1,0:T(8,128)(2,1)S(1)}, u32[]{:S(2)}, u32[]{:S(2)}) %collective-permute-start.47) | collective-permute-done | bytes 1572896 | tf_op jit(solution)/shard_map/ppermute | solution.py:43
  333.8 10.4 %collective-permute-done.50.refs_3_ = bf16[2,2,128,768]{3,2,1,0:T(8,128)(2,1)S(1)} collective-permute-done((bf16[2,2,128,768]{3,2,1,0:T(8,128)(2,1)S(1)}, bf16[2,2,128,768]{3,2,1,0:T(8,128)(2,1)S(1)}, u32[]{:S(2)}, u32[]{:S(2)}) %collective-permute-start.50) | collective-permute-done | bytes 786464 | tf_op jit(solution)/shard_map/ppermute | solution.py:43
  368.4 10.0 %collective-permute-done.55.got_ref = bf16[256,1024]{1,0:T(8,128)(2,1)} collective-permute-done((bf16[256,1024]{1,0:T(8,128)(2,1)}, bf16[256,1024]{1,0:T(8,128)(2,1)}, u32[]{:S(2)}, u32[]{:S(2)}) %collective-permute-start.55) | collective-permute-done | bytes 524320 | tf_op jit(solution)/shard_map/ppermute | solution.py:43
  382.8 6.4 %collective-permute-done.54.keep_got.send_got = bf16[2,128,1024]{2,1,0:T(8,128)(2,1)} collective-permute-done((bf16[2,128,1024]{2,1,0:T(8,128)(2,1)}, bf16[2,128,1024]{2,1,0:T(8,128)(2,1)}, u32[]{:S(2)}, u32[]{:S(2)}) %collective-permute-start.54) | collective-permute-done | bytes 524320 | tf_op jit(solution)/shard_map/ppermute | solution.py:43
  410.4 19.6 %collective-permute-done.59.keep_got.send_got = bf16[2,2,128,1024]{3,2,1,0:T(8,128)(2,1)} collective-permute-done((bf16[2,2,128,1024]{3,2,1,0:T(8,128)(2,1)}, bf16[2,2,128,1024]{3,2,1,0:T(8,128)(2,1)}, u32[]{:S(2)}, u32[]{:S(2)}) %collective-permute-start.59) | collective-permute-done | bytes 1048608 | tf_op jit(solution)/shard_map/ppermute | solution.py:43
  455.4 7.3 %all-to-all-done.3 = bf16[8,32,1024]{2,1,0:T(8,128)(2,1)} async-done(((bf16[8,32,1024]{2,1,0:T(8,128)(2,1)}), bf16[8,32,1024]{2,1,0:T(8,128)(2,1)}, u32[]{:S(2)}, u32[]{:S(2)}) %all-to-all-start.3) | async-done | bytes 524320 | tf_op jit(solution)/shard_map/all_to_all | solution.py:75
  462.7 4.8 %collective-permute-done.64.got_ref = bf16[128,1024]{1,0:T(8,128)(2,1)S(1)} collective-permute-done((bf16[128,1024]{1,0:T(8,128)(2,1)S(1)}, bf16[128,1024]{1,0:T(8,128)(2,1)S(1)}, u32[]{:S(2)}, u32[]{:S(2)}) %collective-permute-start.64) | collective-permute-done | bytes 262176 | tf_op jit(solution)/shard_map/ppermute | solution.py:43
  (497 shorter events, 273.1 us)
Async XLA Ops:
  38.3 32.8 %collective-permute-start.3 = (bf16[512,1024]{1,0:T(8,128)(2,1)}, bf16[512,1024]{1,0:T(8,128)(2,1)S(1)}, u32[]{:S(2)}, u32[]{:S(2)}) collective-permute-start(bf16[512,1024]{1,0:T(8,128)(2,1)} %heads_sent.1), channel_id=1, source_target_pairs={{0,2},{2,0},{1,3},{3,1},{4,6},{6,4},{5,7},{7,5},{8,10},{10,8},{9,1... | collective-permute-start | bytes 3145736 | tf_op jit(solution)/shard_map/ppermute | solution.py:34
  170.3 36.4 %collective-permute-start.32 = (bf16[1024,768]{1,0:T(8,128)(2,1)}, bf16[1024,768]{1,0:T(8,128)(2,1)}, u32[]{:S(2)}, u32[]{:S(2)}) collective-permute-start(bf16[1024,768]{1,0:T(8,128)(2,1)} %get-tuple-element.241.refs_0_), channel_id=1, source_target_pairs={{0,2},{2,0},{1,3},{3,1},{4,6},{6,4},{5,7},{7,5},{8,10},{10,8},{9,1... | collective-permute-start | bytes 4718600 | tf_op jit(solution)/shard_map/ppermute | solution.py:34
  190.3 42.2 %collective-permute-start.38 = (bf16[2,2,2,128,768]{4,3,2,1,0:T(8,128)(2,1)}, bf16[2,2,2,128,768]{4,3,2,1,0:T(8,128)(2,1)S(1)}, u32[]{:S(2)}, u32[]{:S(2)}) collective-permute-start(bf16[2,2,2,128,768]{4,3,2,1,0:T(8,128)(2,1)} %take.6), channel_id=1, source_target_pairs={{0,4},{4,0},{8,12},{12,8},{16,20},{20,16},{24,28},{28,24},{1,5},{5... | collective-permute-start | bytes 4718600 | tf_op jit(solution)/shard_map/ppermute | solution.py:43
  238.4 58.1 %collective-permute-start.41 = (bf16[2,2,2,128,768]{4,3,2,1,0:T(8,128)(2,1)}, bf16[2,2,2,128,768]{4,3,2,1,0:T(8,128)(2,1)}, u32[]{:S(2)}, u32[]{:S(2)}) collective-permute-start(bf16[2,2,2,128,768]{4,3,2,1,0:T(8,128)(2,1)} %take.7), channel_id=1, source_target_pairs={{0,4},{4,0},{8,12},{12,8},{16,20},{20,16},{24,28},{28,24},{1,5},{5... | collective-permute-start | bytes 4718600 | tf_op jit(solution)/shard_map/ppermute | solution.py:43
  245.4 37.9 %collective-permute-start.42 = (bf16[2,2,128,768]{3,2,1,0:T(8,128)(2,1)}, bf16[2,2,128,768]{3,2,1,0:T(8,128)(2,1)}, u32[]{:S(2)}, u32[]{:S(2)}) collective-permute-start(bf16[2,2,128,768]{3,2,1,0:T(8,128)(2,1)} %get-tuple-element.267), channel_id=1, source_target_pairs={{0,16},{4,20},{8,24},{12,28},{16,0},{20,4},{24,8},{28,12},{1,17},{... | collective-permute-start | bytes 2359304 | tf_op jit(solution)/shard_map/ppermute | solution.py:43
  254.3 42.3 %collective-permute-start.43 = (bf16[2,2,128,1024]{3,2,1,0:T(8,128)(2,1)S(1)}, bf16[2,2,128,1024]{3,2,1,0:T(8,128)(2,1)S(1)}, u32[]{:S(2)}, u32[]{:S(2)}) collective-permute-start(bf16[2,2,128,1024]{3,2,1,0:T(8,128)(2,1)S(1)} %take.9), channel_id=1, source_target_pairs={{0,8},{4,12},{8,0},{12,4},{16,24},{20,28},{24,16},{28,20},{1,9},{5... | collective-permute-start | bytes 3145736 | tf_op jit(solution)/shard_map/ppermute | solution.py:43
  255.6 27.7 %collective-permute-start.40 = (bf16[512,512]{1,0:T(8,128)(2,1)S(1)}, bf16[512,512]{1,0:T(8,128)(2,1)S(1)}, u32[]{:S(2)}, u32[]{:S(2)}) collective-permute-start(bf16[512,512]{1,0:T(8,128)(2,1)S(1)} %product_nt.1), channel_id=1, source_target_pairs={{0,2},{2,0},{1,3},{3,1},{4,6},{6,4},{5,7},{7,5},{8,10},{10,8},{9,1... | collective-permute-start | bytes 1572872 | tf_op jit(solution)/shard_map/ppermute | solution.py:34
  263.3 33.3 %collective-permute-start.44 = (bf16[256,1024]{1,0:T(8,128)(2,1)S(1)}, bf16[256,1024]{1,0:T(8,128)(2,1)S(1)}, u32[]{:S(2)}, u32[]{:S(2)}) collective-permute-start(bf16[256,1024]{1,0:T(8,128)(2,1)S(1)} %get-tuple-element.276), channel_id=1, source_target_pairs={{0,1},{1,0},{2,3},{3,2},{4,5},{5,4},{6,7},{7,6},{8,9},{9,8},{10,11... | collective-permute-start | bytes 1572872 | tf_op jit(solution)/shard_map/ppermute | solution.py:38
  283.3 36.8 %collective-permute-start.47 = (bf16[2,384,1024]{2,1,0:T(8,128)(2,1)S(1)}, bf16[2,384,1024]{2,1,0:T(8,128)(2,1)S(1)}, u32[]{:S(2)}, u32[]{:S(2)}) collective-permute-start(bf16[2,384,1024]{2,1,0:T(8,128)(2,1)S(1)} %copy-done.71), channel_id=1, source_target_pairs={{0,4},{4,0},{8,12},{12,8},{16,20},{20,16},{24,28},{28,24},{1,5},{5... | collective-permute-start | bytes 4718600 | tf_op jit(solution)/shard_map/ppermute | solution.py:43
  296.6 25.3 %collective-permute-start.46 = (bf16[512,1024]{1,0:T(8,128)(2,1)S(1)}, bf16[512,1024]{1,0:T(8,128)(2,1)S(1)}, u32[]{:S(2)}, u32[]{:S(2)}) collective-permute-start(bf16[512,1024]{1,0:T(8,128)(2,1)S(1)} %get-tuple-element.285.right_ref.grads_ref), channel_id=1, source_target_pairs={{0,2},{2,0},{1,3},{3,1},{4,6},{6,4},{5,7},{7,5},{8,10},{10,8},{9,1... | collective-permute-start | bytes 3145736 | tf_op jit(solution)/shard_map/ppermute | solution.py:34
  304.6 41.8 %collective-permute-start.51 = (bf16[2,2,128,1024]{3,2,1,0:T(8,128)(2,1)S(1)}, bf16[2,2,128,1024]{3,2,1,0:T(8,128)(2,1)S(1)}, u32[]{:S(2)}, u32[]{:S(2)}) collective-permute-start(bf16[2,2,128,1024]{3,2,1,0:T(8,128)(2,1)S(1)} %take.10), channel_id=1, source_target_pairs={{0,8},{4,12},{8,0},{12,4},{16,24},{20,28},{24,16},{28,20},{1,9},{5... | collective-permute-start | bytes 3145736 | tf_op jit(solution)/shard_map/ppermute | solution.py:43
  304.6 39.6 %collective-permute-start.50 = (bf16[2,2,128,768]{3,2,1,0:T(8,128)(2,1)S(1)}, bf16[2,2,128,768]{3,2,1,0:T(8,128)(2,1)S(1)}, u32[]{:S(2)}, u32[]{:S(2)}) collective-permute-start(bf16[2,2,128,768]{3,2,1,0:T(8,128)(2,1)S(1)} %get-tuple-element.282), channel_id=1, source_target_pairs={{0,16},{4,20},{8,24},{12,28},{16,0},{20,4},{24,8},{28,12},{1,17},{... | collective-permute-start | bytes 2359304 | tf_op jit(solution)/shard_map/ppermute | solution.py:43
  352.3 37.0 %collective-permute-start.53 = (bf16[2,128,1536]{2,1,0:T(8,128)(2,1)}, bf16[2,128,1536]{2,1,0:T(8,128)(2,1)}, u32[]{:S(2)}, u32[]{:S(2)}) collective-permute-start(bf16[2,128,1536]{2,1,0:T(8,128)(2,1)} %get-tuple-element.318), channel_id=1, source_target_pairs={{0,2},{2,0},{1,3},{3,1},{4,6},{6,4},{5,7},{7,5},{8,10},{10,8},{9,1... | collective-permute-start | bytes 2359304 | tf_op jit(solution)/shard_map/ppermute | solution.py:34
  353.3 25.1 %collective-permute-start.55 = (bf16[256,1024]{1,0:T(8,128)(2,1)}, bf16[256,1024]{1,0:T(8,128)(2,1)}, u32[]{:S(2)}, u32[]{:S(2)}) collective-permute-start(bf16[256,1024]{1,0:T(8,128)(2,1)} %get-tuple-element.292), channel_id=1, source_target_pairs={{0,8},{4,12},{8,0},{12,4},{16,24},{20,28},{24,16},{28,20},{1,9},{5... | collective-permute-start | bytes 1572872 | tf_op jit(solution)/shard_map/ppermute | solution.py:43
  354.0 37.2 %all-to-all-start.2 = ((bf16[8,40,1024]{2,1,0:T(8,128)(2,1)}), bf16[8,40,1024]{2,1,0:T(8,128)(2,1)}, u32[]{:S(2)}, u32[]{:S(2)}) async-start(bf16[8,40,1024]{2,1,0:T(8,128)(2,1)} %pack_back.1), calls=%async_computation.2 | async-start | bytes 1310720 | tf_op jit(solution)/shard_map/all_to_all | solution.py:75
  358.2 24.6 %collective-permute-start.52 = (bf16[2,128,1024]{2,1,0:T(8,128)(2,1)}, bf16[2,128,1024]{2,1,0:T(8,128)(2,1)}, u32[]{:S(2)}, u32[]{:S(2)}) collective-permute-start(bf16[2,128,1024]{2,1,0:T(8,128)(2,1)} %get-tuple-element.305), channel_id=1, source_target_pairs={{0,4},{4,0},{8,12},{12,8},{16,20},{20,16},{24,28},{28,24},{1,5},{5... | collective-permute-start | bytes 1572872 | tf_op jit(solution)/shard_map/ppermute | solution.py:43
  365.4 23.9 %collective-permute-start.54 = (bf16[2,128,1024]{2,1,0:T(8,128)(2,1)}, bf16[2,128,1024]{2,1,0:T(8,128)(2,1)}, u32[]{:S(2)}, u32[]{:S(2)}) collective-permute-start(bf16[2,128,1024]{2,1,0:T(8,128)(2,1)} %get-tuple-element.321), channel_id=1, source_target_pairs={{0,4},{4,0},{8,12},{12,8},{16,20},{20,16},{24,28},{28,24},{1,5},{5... | collective-permute-start | bytes 1572872 | tf_op jit(solution)/shard_map/ppermute | solution.py:43
  365.7 44.8 %collective-permute-start.60 = (bf16[384,1024]{1,0:T(8,128)(2,1)}, bf16[384,1024]{1,0:T(8,128)(2,1)}, u32[]{:S(2)}, u32[]{:S(2)}) collective-permute-start(bf16[384,1024]{1,0:T(8,128)(2,1)} %copy-done.120), channel_id=1, source_target_pairs={{0,16},{4,20},{8,24},{12,28},{16,0},{20,4},{24,8},{28,12},{1,17},{... | collective-permute-start | bytes 2359304 | tf_op jit(solution)/shard_map/ppermute | solution.py:43
  378.4 51.6 %collective-permute-start.59 = (bf16[2,2,128,1024]{3,2,1,0:T(8,128)(2,1)}, bf16[2,2,128,1024]{3,2,1,0:T(8,128)(2,1)}, u32[]{:S(2)}, u32[]{:S(2)}) collective-permute-start(bf16[2,2,128,1024]{3,2,1,0:T(8,128)(2,1)} %copy-done.82), channel_id=1, source_target_pairs={{0,8},{4,12},{8,0},{12,4},{16,24},{20,28},{24,16},{28,20},{1,9},{5... | collective-permute-start | bytes 3145736 | tf_op jit(solution)/shard_map/ppermute | solution.py:43
  394.2 56.0 %collective-permute-start.57 = (bf16[2,128,1536]{2,1,0:T(8,128)(2,1)}, bf16[2,128,1536]{2,1,0:T(8,128)(2,1)}, u32[]{:S(2)}, u32[]{:S(2)}) collective-permute-start(bf16[2,128,1536]{2,1,0:T(8,128)(2,1)} %pad_maximum_fusion.2), channel_id=1, source_target_pairs={{0,8},{4,12},{8,0},{12,4},{16,24},{20,28},{24,16},{28,20},{1,9},{5... | collective-permute-start | bytes 2359304 | tf_op jit(solution)/shard_map/ppermute | solution.py:43
  395.7 46.5 %collective-permute-start.63 = (f32[1,3072]{1,0:T(1,128)S(1)}, f32[1,3072]{1,0:T(1,128)S(1)}, u32[]{:S(2)}, u32[]{:S(2)}) collective-permute-start(f32[1,3072]{1,0:T(1,128)S(1)} %add.134), channel_id=1, source_target_pairs={{0,2},{2,0},{1,3},{3,1},{4,6},{6,4},{5,7},{7,5},{8,10},{10,8},{9,1... | collective-permute-start | bytes 36872 | tf_op jit(solution)/shard_map/ppermute | solution.py:34
  401.3 46.9 %collective-permute-start.58 = (bf16[128,1024]{1,0:T(8,128)(2,1)}, bf16[128,1024]{1,0:T(8,128)(2,1)}, u32[]{:S(2)}, u32[]{:S(2)}) collective-permute-start(bf16[128,1024]{1,0:T(8,128)(2,1)} %get-tuple-element.333), channel_id=1, source_target_pairs={{0,16},{4,20},{8,24},{12,28},{16,0},{20,4},{24,8},{28,12},{1,17},{... | collective-permute-start | bytes 786440 | tf_op jit(solution)/shard_map/ppermute | solution.py:43
  410.4 42.5 %collective-permute-start.56 = (bf16[128,1024]{1,0:T(8,128)(2,1)}, bf16[128,1024]{1,0:T(8,128)(2,1)}, u32[]{:S(2)}, u32[]{:S(2)}) collective-permute-start(bf16[128,1024]{1,0:T(8,128)(2,1)} %get-tuple-element.336), channel_id=1, source_target_pairs={{0,16},{4,20},{8,24},{12,28},{16,0},{20,4},{24,8},{28,12},{1,17},{... | collective-permute-start | bytes 786440 | tf_op jit(solution)/shard_map/ppermute | solution.py:43
  435.5 27.1 %all-to-all-start.3 = ((bf16[8,32,1024]{2,1,0:T(8,128)(2,1)}), bf16[8,32,1024]{2,1,0:T(8,128)(2,1)}, u32[]{:S(2)}, u32[]{:S(2)}) async-start(bf16[8,32,1024]{2,1,0:T(8,128)(2,1)} %bitcast.37), calls=%async_computation.3 | async-start | bytes 1048576 | tf_op jit(solution)/shard_map/all_to_all | solution.py:75
  (176 other events, 1501.5 us)

commit v4 on v3

--- a/solution.py
+++ b/solution.py
@@ -13,7 +13,7 @@
 ROPE_BASE = 1000000.0
 NEGATIVE = -1e30
 EXTRA = 8
-VMEM_LIMIT = 40 << 20
+VMEM_LIMIT = 28 << 20
 BF16 = jnp.bfloat16
 F32 = jnp.float32
 
@@ -347,7 +347,7 @@
 
 
 def up_kernel(picks, mid_ref, gate_ref, up_ref, *refs):
-    parts = 4
+    parts = 2
     gate_parts, up_parts = refs[:parts], refs[parts : 2 * parts]
     kept_ref, *got_refs = refs[2 * parts : -3]
     gate_grad_ref, up_grad_ref, act_ref = refs[-3:]
@@ -404,8 +404,8 @@
     features = gate_ref.shape[0]
     share = pieces[0].shape[0]
     gate_grad, up_grad = gate_grad_ref[...], up_grad_ref[...]
-    for i in range(features // (2 * share)):
-        at = slice(i * 2 * share, (i + 1) * 2 * share)
+    for i in range(features // share):
+        at = slice(i * share, (i + 1) * share)
         total = dot_nt(gate_grad, gate_ref[at, :]) + dot_nt(up_grad, up_ref[at, :])
         near_ref[:, at] = total.astype(near_ref.dtype)
     for i in range(count):
@@ -895,7 +895,7 @@
     levels = count.bit_length() - 1
     row = lax.axis_index("row")
     col = lax.axis_index("col")
-    xbit, zbit, wbit = my_bit(1), my_bit(2), my_bit(4)
+    xbit, zbit = my_bit(1), my_bit(2)
     half = tokens.shape[0]
     quarter = half // 2
     group = 2 * half
@@ -926,11 +926,11 @@
         return jnp.concatenate(pieces, axis=axis), 0
 
     moved_in = exchange(tokens)
-    share = features // 4
+    share = features // 2
     gate_far, far_base = ff_block(gate_weight, 1 - row, 1)
     up_far, _ = ff_block(up_weight, 1 - row, 1)
     gate_sent, up_sent = (
-        block_of(weight, wbit * 2 + xbit, far_base, (share, ff_part))
+        block_of(weight, xbit, far_base, (share, ff_part))
         for weight in (gate_far, up_far)
     )
     got_gate, got_up = swap_row(gate_sent), swap_row(up_sent)
@@ -950,8 +950,8 @@
     cosine, sine = rotary_tables(slot - start)
     slot_lanes = jnp.broadcast_to(slot.astype(F32)[None], (8, group))
     start_lanes = jnp.broadcast_to(start.astype(F32)[None], (8, group))
-    moved_in, cosine, sine, slot_lanes, start_lanes, got_gate, got_up = together(
-        moved_in, cosine, sine, slot_lanes, start_lanes, got_gate, got_up
+    moved_in, cosine, sine, slot_lanes, start_lanes, got_gate, up_sent = together(
+        moved_in, cosine, sine, slot_lanes, start_lanes, got_gate, up_sent
     )
 
     gain_in = attention_gain.astype(F32)[None]
@@ -971,7 +971,6 @@
     )
     got_gate, got_up = together(got_gate, got_up, heads_sent)[:2]
     got_gate_x, got_up_x = swap_dp(got_gate, 1), swap_dp(got_up, 1)
-    got_gate_w, got_up_w = swap_dp(got_gate, 4), swap_dp(got_up, 4)
 
     down_own, own_at = ff_block(down_weight, row, 0)
     down_other, other_at = ff_block(down_weight, 1 - row, 0)
@@ -985,8 +984,8 @@
     act_sent = [
         act_back(rows_of, down_other, other_at, BF16) for rows_of in (moved_grad, grad_near)
     ]
-    got_heads, kept_heads, got_square, got_gate_x, got_gate_w, grad_z, *act_sent = together(
-        got_heads, kept_heads, got_square, got_gate_x, got_gate_w, grad_z, *act_sent
+    got_heads, kept_heads, got_square, grad_z, *act_sent = together(
+        got_heads, kept_heads, got_square, grad_z, *act_sent
     )
     inverse_in = lax.rsqrt((square + got_square) / D + EPSILON)
     shared = (
@@ -1000,7 +999,6 @@
         key_norm_gain.astype(F32)[None],
     )
     got_act = [swap_row(act_sent[0])]
-    got_gate_wx = swap_dp(got_gate_w, 1)
     grad_far = swap_col(grad_z)
     attention = attend(kept_heads, got_heads, shared, kv_heads, repeat)
     attention, got_act[0], grad_far = together(attention, got_act[0], grad_far)
@@ -1013,10 +1011,9 @@
         act_back(after(rows_of, out_own), down_other, other_at, BF16)
         for rows_of in (grad_z, grad_far)
     ]
-    attention_other, got_act[1], got_gate_wx, got_up_x, got_up_w, out_own, *far_sent = together(
-        attention_other, got_act[1], got_gate_wx, got_up_x, got_up_w, out_own, *far_sent
-    )
-    got_up_wx = swap_dp(got_up_w, 1)
+    attention_other, got_act[1], got_gate_x, out_own, *far_sent = together(
+        attention_other, got_act[1], got_gate_x, out_own, *far_sent
+    )
     out_kept, out_sent = product_onto(
         attention_other, output_weight, 1 - row, query_part, out_own, features // 2, "out_proj"
     )
@@ -1048,7 +1045,7 @@
     by_row = swap_row(normed_mid)
     by_z = swap_z(normed_mid)
     act_kept = act_back(after(grad_all, normed_mid), down_own, own_at, F32, "act_kept")
-    by_row, by_z, act_kept, got_up_wx = together(by_row, by_z, act_kept, got_up_wx)
+    by_row, by_z, act_kept, got_up_x = together(by_row, by_z, act_kept, got_up_x)
     corner_a = swap_row(by_z[:quarter])
     corner_b = swap_z(by_row[quarter:])
     got_act.extend(swap_row(after(sent, by_row)) for sent in far_sent)
@@ -1064,16 +1061,8 @@
 
     gate_own, own_base = ff_block(gate_weight, row, 1)
     up_own, _ = ff_block(up_weight, row, 1)
-    places = (
-        wbit * 2 + xbit,
-        wbit * 2 + 1 - xbit,
-        (1 - wbit) * 2 + xbit,
-        (1 - wbit) * 2 + 1 - xbit,
-    )
-    pieces = (
-        (got_gate, got_gate_x, got_gate_w, got_gate_wx),
-        (got_up, got_up_x, got_up_w, got_up_wx),
-    )
+    places = (xbit, 1 - xbit)
+    pieces = ((got_gate, got_gate_x), (got_up, got_up_x))
     up_weights = (gate_own, up_own, own_base, pieces, places)
     gate_grad, up_grad, activated = gate_and_up(
         mid_all, *up_weights, act_kept, (got_act[0], got_act[2], got_act[1], got_act[3])

time: 477 us -> 470 us (0.985)
  waiting for transfers between devices: 162 us -> 176 us
  local copies, waits for them, and re-layouts: 58 us -> 48.8 us
  Pallas kernels: 157 us -> 149 us
    ppermute x21, waiting for transfers between devices: 43 us -> 75.1 us  [swap_row(): return lax.ppermute(value, 'row', [(0, 1), (1, 0)])]
    ppermute x28 -> x24, waiting for transfers between devices: 99.5 us -> 88.3 us  [swap_dp(): return lax.ppermute(value, 'dp', [(i, i ^ bit) for i in range(count)])]
    unnamed x262 -> x166, local copies, waits for them, and re-layouts: 46.2 us -> 38.2 us
    all_to_all x4, waiting for transfers between devices: 16.5 us -> 9.58 us  [exchange(): return lax.all_to_all(value, 'dp', split_axis=0, concat_axis=0, tiled=True)]
    ppermute x28 -> x24, starting transfers between devices: 31.9 us -> 31.1 us  [swap_dp(): return lax.ppermute(value, 'dp', [(i, i ^ bit) for i in range(count)])]
  transfers between devices with their start and end apart: 69 -> 65, of which waited for: 31 -> 32; matrix products, arithmetic and copies ran while one was open for 5% -> 5% of each run, Pallas kernels for 28% -> 28%
where the time goes in v4:
time: 470 us; the launch traced here: 466 us
  waiting for transfers between devices  176 us (37%)
  Pallas kernels  149 us (32%)
  starting transfers between devices  75 us (16%)
  local copies, waits for them, and re-layouts  48.8 us (10%)
  other arithmetic  15.3 us (3%)
    pallas_call x40, Pallas kernels, grid_call(): pl.pallas_call(kernel, grid_spec=pltpu.PrefetchScalarGridSpec(num_scalar_...  108 us
    ppermute x24, waiting for transfers between devices, swap_dp(): return lax.ppermute(value, 'dp', [(i, i ^ bit) for i in range(count)])  88.3 us
    ppermute x21, waiting for transfers between devices, swap_row(): return lax.ppermute(value, 'row', [(0, 1), (1, 0)])  75.1 us
    unnamed x166, local copies, waits for them, and re-layouts  38.2 us
    ppermute x24, starting transfers between devices, swap_dp(): return lax.ppermute(value, 'dp', [(i, i ^ bit) for i in range(count)])  31.1 us
    ppermute x21, starting transfers between devices, swap_row(): return lax.ppermute(value, 'row', [(0, 1), (1, 0)])  22.1 us
    pallas_call x23, Pallas kernels, local_call(): pl.pallas_call(kernel, out_shape=[jax.ShapeDtypeStruct(shape, dtype) for...  22 us
    all_to_all x4, starting transfers between devices, exchange(): return lax.all_to_all(value, 'dp', split_axis=0, concat_axis=0, tiled=True)  20.2 us
  transfers between devices with their start and end apart: 65, of which 32 were waited for; matrix products, arithmetic and copies ran while one was open for 5% of the time, Pallas kernels for 28%

profile of v4, /device:TPU:0, one launch (start us, length us, event | category | flops | bytes accessed | tf_op | source)
XLA Modules:
  0.0 465.5 jit_solution(1411796808069687320)
XLA Ops:
  5.5 5.8 %all-to-all-start = ((bf16[8,32,1024]{2,1,0:T(8,128)(2,1)}), bf16[8,32,1024]{2,1,0:T(8,128)(2,1)S(1)}, u32[]{:S(2)}, u32[]{:S(2)}) async-start(bf16[8,32,1024]{2,1,0:T(8,128)(2,1)} %bitcast.1), calls=%async_computation | async-start | bytes 1048576 | tf_op jit(solution)/shard_map/all_to_all | solution.py:75
  16.3 7.6 %collective-permute-done.refs_0_ = bf16[512,768]{1,0:T(8,128)(2,1)S(1)} collective-permute-done((bf16[512,768]{1,0:T(8,128)(2,1)S(1)}, bf16[512,768]{1,0:T(8,128)(2,1)S(1)}, u32[]{:S(2)}, u32[]{:S(2)}) %collective-permute-start) | collective-permute-done | bytes 786464 | tf_op jit(solution)/shard_map/ppermute | solution.py:34
  25.7 5.3 %all-to-all-start.1 = ((bf16[8,32,1024]{2,1,0:T(8,128)(2,1)}), bf16[8,32,1024]{2,1,0:T(8,128)(2,1)}, u32[]{:S(2)}, u32[]{:S(2)}) async-start(bf16[8,32,1024]{2,1,0:T(8,128)(2,1)} %bitcast.101), calls=%async_computation.1 | async-start | bytes 1048576 | tf_op jit(solution)/shard_map/all_to_all | solution.py:75
  34.2 5.8 %collective-permute-done.2.refs_2_ = bf16[512,768]{1,0:T(8,128)(2,1)} collective-permute-done((bf16[512,768]{1,0:T(8,128)(2,1)S(1)}, bf16[512,768]{1,0:T(8,128)(2,1)}, u32[]{:S(2)}, u32[]{:S(2)}) %collective-permute-start.2) | collective-permute-done | bytes 786464 | tf_op jit(solution)/shard_map/ppermute | solution.py:34
  57.7 11.4 %collective-permute-done.4 = f32[8,512]{1,0:T(8,128)S(1)} collective-permute-done((f32[8,512]{1,0:T(8,128)S(1)}, f32[8,512]{1,0:T(8,128)S(1)}, u32[]{:S(2)}, u32[]{:S(2)}) %collective-permute-start.4) | collective-permute-done | bytes 16416 | tf_op jit(solution)/shard_map/ppermute | solution.py:34
  72.3 7.2 %attend.1.left_ref.refs_0_ = bf16[512,512]{1,0:T(8,128)(2,1)S(1)} custom-call(f32[512,1024]{1,0:T(8,128)S(1)} %heads_kept.1.query_own.key_own.value_own, bf16[512,1024]{1,0:T(8,128)(2,1)S(1)} %collective-permute-done.3.query_got.key_got.value_got, f32[512,1024]{1,0:T(8,128)S(1)} %heads_kept.1.query_own.key_own.value_own, ...), custom_call_target="tpu_custom_call" | custom-call | flops 230000000 | bytes 738000 | tf_op jit(solution)/shard_map/attend/pallas_call | solution.py:845
  94.7 9.5 %collective-permute-done.10.refs_7_ = bf16[256,768]{1,0:T(8,128)(2,1)S(1)} collective-permute-done((bf16[256,768]{1,0:T(8,128)(2,1)S(1)}, bf16[256,768]{1,0:T(8,128)(2,1)S(1)}, u32[]{:S(2)}, u32[]{:S(2)}) %collective-permute-start.10) | collective-permute-done | bytes 393248 | tf_op jit(solution)/shard_map/ppermute | solution.py:34
  148.7 8.0 %collective-permute-done.24.refs_6_ = bf16[256,768]{1,0:T(8,128)(2,1)} collective-permute-done((bf16[256,768]{1,0:T(8,128)(2,1)}, bf16[256,768]{1,0:T(8,128)(2,1)}, u32[]{:S(2)}, u32[]{:S(2)}) %collective-permute-start.24) | collective-permute-done | bytes 393248 | tf_op jit(solution)/shard_map/ppermute | solution.py:34
  156.8 10.6 %gate_and_up.1 = (bf16[1024,768]{1,0:T(8,128)(2,1)S(1)}, bf16[1024,768]{1,0:T(8,128)(2,1)S(1)}, bf16[1024,768]{1,0:T(8,128)(2,1)S(1)}) custom-call(s32[3]{0:T(128)S(1)} %add_add_fusion.picks, bf16[1024,2048]{1,0:T(8,128)(2,1)S(1)} %mid_all.1.mid_ref.left_ref, bf16[1024,3072]{1,0:T(8,128)(2,1)} %gate_ref.5, bf16[1024,3072]{1,0:T(8,128)(2,1)} %up_ref.5, ...), custom_call_target="tpu_custom_call" | custom-call | flops 345000000 | bytes 1107000 | tf_op jit(solution)/shard_map/gate_and_up/pallas_call | solution.py:155
  168.0 6.3 %mid_sent.1 = (bf16[512,1024]{1,0:T(8,128)(2,1)S(1)}, bf16[512,1024]{1,0:T(8,128)(2,1)S(1)}) custom-call(s32[3]{0:T(128)S(1)} %add_add_fusion.picks, bf16[1024,768]{1,0:T(8,128)(2,1)S(1)} %get-tuple-element.229.gate_grad_ref.right_ref, bf16[1024,768]{1,0:T(8,128)(2,1)S(1)} %get-tuple-element.241.up_grad_ref.right_ref, bf16[1024,3072]{1,0:T(8,128)(2,1)} %gate_ref.5, ...), custom_call_target="tpu_custom_call" | custom-call | flops 345000000 | bytes 1107000 | tf_op jit(solution)/shard_map/mid_sent/pallas_call | solution.py:155
  181.7 6.3 %mid_kept.1 = (f32[512,1024]{1,0:T(8,128)S(1)}, f32[512,1024]{1,0:T(8,128)S(1)}) custom-call(s32[3]{0:T(128)S(1)} %add_add_fusion.picks, bf16[1024,768]{1,0:T(8,128)(2,1)S(1)} %get-tuple-element.229.gate_grad_ref.right_ref, bf16[1024,768]{1,0:T(8,128)(2,1)S(1)} %get-tuple-element.241.up_grad_ref.right_ref, bf16[1024,3072]{1,0:T(8,128)(2,1)} %gate_ref.5, ...), custom_call_target="tpu_custom_call" | custom-call | flops 172500000 | bytes 553500 | tf_op jit(solution)/shard_map/mid_kept/pallas_call | solution.py:155
  188.0 15.5 %collective-permute-done.28.refs_1_ = bf16[1024,768]{1,0:T(8,128)(2,1)S(1)} collective-permute-done((bf16[1024,768]{1,0:T(8,128)(2,1)S(1)}, bf16[1024,768]{1,0:T(8,128)(2,1)S(1)}, u32[]{:S(2)}, u32[]{:S(2)}) %collective-permute-start.28) | collective-permute-done | bytes 1572896 | tf_op jit(solution)/shard_map/ppermute | solution.py:34
  216.0 4.6 down_first.1
  252.0 5.7 %down_proj.1 = (f32[512,1024]{1,0:T(8,128)S(1)}, bf16[256,1024]{1,0:T(8,128)(2,1)S(1)}, bf16[256,1024]{1,0:T(8,128)(2,1)S(1)}) custom-call(s32[2]{0:T(128)S(1)} %pad_add_fusion.4.picks, bf16[1024,1536]{1,0:T(8,128)(2,1)S(1)} %copy-done.9, bf16[3072,1024]{1,0:T(8,128)(2,1)} %other_ref.1, bf16[3072,1024]{1,0:T(8,128)(2,1)} %other_ref.1), custom_call_target="tpu_custom_call" | custom-call | flops 5750000 | bytes 18450 | tf_op jit(solution)/shard_map/down_proj/pallas_call | solution.py:155
  257.8 20.4 %collective-permute-done.38.refs_2_ = bf16[2,2,128,768]{3,2,1,0:T(8,128)(2,1)} collective-permute-done((bf16[2,2,128,768]{3,2,1,0:T(8,128)(2,1)}, bf16[2,2,128,768]{3,2,1,0:T(8,128)(2,1)}, u32[]{:S(2)}, u32[]{:S(2)}) %collective-permute-start.38) | collective-permute-done | bytes 786464 | tf_op jit(solution)/shard_map/ppermute | solution.py:43
  279.8 11.8 %attend_back.1 = (bf16[512,1024]{1,0:T(8,128)(2,1)S(1)}, f32[2,128]{1,0:T(2,128)S(1)}) custom-call(f32[512,1024]{1,0:T(8,128)S(1)} %heads_kept.1.query_own.key_own.value_own, bf16[512,1024]{1,0:T(8,128)(2,1)S(1)} %collective-permute-done.3.query_got.key_got.value_got, f32[512,1024]{1,0:T(8,128)S(1)} %heads_kept.1.query_own.key_own.value_own, ...), custom_call_target="tpu_custom_call" | custom-call | flops 230000000 | bytes 738000 | tf_op jit(solution)/shard_map/attend_back/pallas_call | solution.py:860
  306.2 8.9 %collective-permute-done.43.keep_got.send_got = bf16[2,384,1024]{2,1,0:T(8,128)(2,1)S(1)} collective-permute-done((bf16[2,384,1024]{2,1,0:T(8,128)(2,1)S(1)}, bf16[2,384,1024]{2,1,0:T(8,128)(2,1)S(1)}, u32[]{:S(2)}, u32[]{:S(2)}) %collective-permute-start.43) | collective-permute-done | bytes 1572896 | tf_op jit(solution)/shard_map/ppermute | solution.py:43
  327.8 9.7 %collective-permute-done.46.refs_3_ = bf16[2,2,128,768]{3,2,1,0:T(8,128)(2,1)S(1)} collective-permute-done((bf16[2,2,128,768]{3,2,1,0:T(8,128)(2,1)S(1)}, bf16[2,2,128,768]{3,2,1,0:T(8,128)(2,1)S(1)}, u32[]{:S(2)}, u32[]{:S(2)}) %collective-permute-start.46) | collective-permute-done | bytes 786464 | tf_op jit(solution)/shard_map/ppermute | solution.py:43
  362.4 8.6 %collective-permute-done.51.got_ref = bf16[256,1024]{1,0:T(8,128)(2,1)} collective-permute-done((bf16[256,1024]{1,0:T(8,128)(2,1)}, bf16[256,1024]{1,0:T(8,128)(2,1)}, u32[]{:S(2)}, u32[]{:S(2)}) %collective-permute-start.51) | collective-permute-done | bytes 524320 | tf_op jit(solution)/shard_map/ppermute | solution.py:43
  375.3 7.9 %collective-permute-done.50.keep_got.send_got = bf16[2,128,1024]{2,1,0:T(8,128)(2,1)} collective-permute-done((bf16[2,128,1024]{2,1,0:T(8,128)(2,1)}, bf16[2,128,1024]{2,1,0:T(8,128)(2,1)}, u32[]{:S(2)}, u32[]{:S(2)}) %collective-permute-start.50) | collective-permute-done | bytes 524320 | tf_op jit(solution)/shard_map/ppermute | solution.py:43
  404.0 19.3 %collective-permute-done.55.keep_got.send_got = bf16[2,2,128,1024]{3,2,1,0:T(8,128)(2,1)} collective-permute-done((bf16[2,2,128,1024]{3,2,1,0:T(8,128)(2,1)}, bf16[2,2,128,1024]{3,2,1,0:T(8,128)(2,1)}, u32[]{:S(2)}, u32[]{:S(2)}) %collective-permute-start.55) | collective-permute-done | bytes 1048608 | tf_op jit(solution)/shard_map/ppermute | solution.py:43
  428.5 4.9 %all-to-all-start.3 = ((bf16[8,32,1024]{2,1,0:T(8,128)(2,1)}), bf16[8,32,1024]{2,1,0:T(8,128)(2,1)}, u32[]{:S(2)}, u32[]{:S(2)}) async-start(bf16[8,32,1024]{2,1,0:T(8,128)(2,1)} %bitcast.33), calls=%async_computation.3 | async-start | bytes 1048576 | tf_op jit(solution)/shard_map/all_to_all | solution.py:75
  448.2 7.9 %all-to-all-done.3 = bf16[8,32,1024]{2,1,0:T(8,128)(2,1)} async-done(((bf16[8,32,1024]{2,1,0:T(8,128)(2,1)}), bf16[8,32,1024]{2,1,0:T(8,128)(2,1)}, u32[]{:S(2)}, u32[]{:S(2)}) %all-to-all-start.3) | async-done | bytes 524320 | tf_op jit(solution)/shard_map/all_to_all | solution.py:75
  456.0 4.7 %collective-permute-done.60.got_ref = bf16[128,1024]{1,0:T(8,128)(2,1)S(1)} collective-permute-done((bf16[128,1024]{1,0:T(8,128)(2,1)S(1)}, bf16[128,1024]{1,0:T(8,128)(2,1)S(1)}, u32[]{:S(2)}, u32[]{:S(2)}) %collective-permute-start.60) | collective-permute-done | bytes 262176 | tf_op jit(solution)/shard_map/ppermute | solution.py:43
  (393 shorter events, 249.7 us)
Async XLA Ops:
  13.1 26.9 %collective-permute-start.2 = (bf16[512,768]{1,0:T(8,128)(2,1)S(1)}, bf16[512,768]{1,0:T(8,128)(2,1)}, u32[]{:S(2)}, u32[]{:S(2)}) collective-permute-start(bf16[512,768]{1,0:T(8,128)(2,1)S(1)} %block_of.3), channel_id=1, source_target_pairs={{0,2},{2,0},{1,3},{3,1},{4,6},{6,4},{5,7},{7,5},{8,10},{10,8},{9,1... | collective-permute-start | bytes 2359304 | tf_op jit(solution)/shard_map/ppermute | solution.py:34
  44.2 25.0 %collective-permute-start.3 = (bf16[512,1024]{1,0:T(8,128)(2,1)}, bf16[512,1024]{1,0:T(8,128)(2,1)S(1)}, u32[]{:S(2)}, u32[]{:S(2)}) collective-permute-start(bf16[512,1024]{1,0:T(8,128)(2,1)} %heads_sent.1), channel_id=1, source_target_pairs={{0,2},{2,0},{1,3},{3,1},{4,6},{6,4},{5,7},{7,5},{8,10},{10,8},{9,1... | collective-permute-start | bytes 3145736 | tf_op jit(solution)/shard_map/ppermute | solution.py:34
  69.2 24.6 %collective-permute-start.11 = (bf16[512,768]{1,0:T(8,128)(2,1)S(1)}, bf16[512,768]{1,0:T(8,128)(2,1)S(1)}, u32[]{:S(2)}, u32[]{:S(2)}) collective-permute-start(bf16[512,768]{1,0:T(8,128)(2,1)S(1)} %copy-done.21), channel_id=1, source_target_pairs={{0,4},{4,0},{8,12},{12,8},{16,20},{20,16},{24,28},{28,24},{1,5},{5... | collective-permute-start | bytes 2359304 | tf_op jit(solution)/shard_map/ppermute | solution.py:43
  167.4 36.1 %collective-permute-start.28 = (bf16[1024,768]{1,0:T(8,128)(2,1)S(1)}, bf16[1024,768]{1,0:T(8,128)(2,1)S(1)}, u32[]{:S(2)}, u32[]{:S(2)}) collective-permute-start(bf16[1024,768]{1,0:T(8,128)(2,1)S(1)} %get-tuple-element.231.refs_0_), channel_id=1, source_target_pairs={{0,2},{2,0},{1,3},{3,1},{4,6},{6,4},{5,7},{7,5},{8,10},{10,8},{9,1... | collective-permute-start | bytes 4718600 | tf_op jit(solution)/shard_map/ppermute | solution.py:34
  181.1 46.2 %collective-permute-start.34 = (bf16[2,2,2,128,768]{4,3,2,1,0:T(8,128)(2,1)S(1)}, bf16[2,2,2,128,768]{4,3,2,1,0:T(8,128)(2,1)S(1)}, u32[]{:S(2)}, u32[]{:S(2)}) collective-permute-start(bf16[2,2,2,128,768]{4,3,2,1,0:T(8,128)(2,1)S(1)} %take.6), channel_id=1, source_target_pairs={{0,4},{4,0},{8,12},{12,8},{16,20},{20,16},{24,28},{28,24},{1,5},{5... | collective-permute-start | bytes 4718600 | tf_op jit(solution)/shard_map/ppermute | solution.py:43
  233.7 57.9 %collective-permute-start.37 = (bf16[2,2,2,128,768]{4,3,2,1,0:T(8,128)(2,1)}, bf16[2,2,2,128,768]{4,3,2,1,0:T(8,128)(2,1)}, u32[]{:S(2)}, u32[]{:S(2)}) collective-permute-start(bf16[2,2,2,128,768]{4,3,2,1,0:T(8,128)(2,1)} %take.7), channel_id=1, source_target_pairs={{0,4},{4,0},{8,12},{12,8},{16,20},{20,16},{24,28},{28,24},{1,5},{5... | collective-permute-start | bytes 4718600 | tf_op jit(solution)/shard_map/ppermute | solution.py:43
  240.5 37.8 %collective-permute-start.38 = (bf16[2,2,128,768]{3,2,1,0:T(8,128)(2,1)}, bf16[2,2,128,768]{3,2,1,0:T(8,128)(2,1)}, u32[]{:S(2)}, u32[]{:S(2)}) collective-permute-start(bf16[2,2,128,768]{3,2,1,0:T(8,128)(2,1)} %get-tuple-element.257), channel_id=1, source_target_pairs={{0,16},{4,20},{8,24},{12,28},{16,0},{20,4},{24,8},{28,12},{1,17},{... | collective-permute-start | bytes 2359304 | tf_op jit(solution)/shard_map/ppermute | solution.py:43
  250.2 41.8 %collective-permute-start.39 = (bf16[2,2,128,1024]{3,2,1,0:T(8,128)(2,1)S(1)}, bf16[2,2,128,1024]{3,2,1,0:T(8,128)(2,1)S(1)}, u32[]{:S(2)}, u32[]{:S(2)}) collective-permute-start(bf16[2,2,128,1024]{3,2,1,0:T(8,128)(2,1)S(1)} %take.9), channel_id=1, source_target_pairs={{0,8},{4,12},{8,0},{12,4},{16,24},{20,28},{24,16},{28,20},{1,9},{5... | collective-permute-start | bytes 3145736 | tf_op jit(solution)/shard_map/ppermute | solution.py:43
  250.7 27.5 %collective-permute-start.36 = (bf16[512,512]{1,0:T(8,128)(2,1)S(1)}, bf16[512,512]{1,0:T(8,128)(2,1)S(1)}, u32[]{:S(2)}, u32[]{:S(2)}) collective-permute-start(bf16[512,512]{1,0:T(8,128)(2,1)S(1)} %product_nt.1), channel_id=1, source_target_pairs={{0,2},{2,0},{1,3},{3,1},{4,6},{6,4},{5,7},{7,5},{8,10},{10,8},{9,1... | collective-permute-start | bytes 1572872 | tf_op jit(solution)/shard_map/ppermute | solution.py:34
  257.7 33.9 %collective-permute-start.40 = (bf16[256,1024]{1,0:T(8,128)(2,1)S(1)}, bf16[256,1024]{1,0:T(8,128)(2,1)S(1)}, u32[]{:S(2)}, u32[]{:S(2)}) collective-permute-start(bf16[256,1024]{1,0:T(8,128)(2,1)S(1)} %get-tuple-element.266), channel_id=1, source_target_pairs={{0,1},{1,0},{2,3},{3,2},{4,5},{5,4},{6,7},{7,6},{8,9},{9,8},{10,11... | collective-permute-start | bytes 1572872 | tf_op jit(solution)/shard_map/ppermute | solution.py:38
  278.2 36.8 %collective-permute-start.43 = (bf16[2,384,1024]{2,1,0:T(8,128)(2,1)S(1)}, bf16[2,384,1024]{2,1,0:T(8,128)(2,1)S(1)}, u32[]{:S(2)}, u32[]{:S(2)}) collective-permute-start(bf16[2,384,1024]{2,1,0:T(8,128)(2,1)S(1)} %copy-done.48), channel_id=1, source_target_pairs={{0,4},{4,0},{8,12},{12,8},{16,20},{20,16},{24,28},{28,24},{1,5},{5... | collective-permute-start | bytes 4718600 | tf_op jit(solution)/shard_map/ppermute | solution.py:43
  292.0 25.0 %collective-permute-start.42 = (bf16[512,1024]{1,0:T(8,128)(2,1)S(1)}, bf16[512,1024]{1,0:T(8,128)(2,1)S(1)}, u32[]{:S(2)}, u32[]{:S(2)}) collective-permute-start(bf16[512,1024]{1,0:T(8,128)(2,1)S(1)} %get-tuple-element.275.right_ref.grads_ref), channel_id=1, source_target_pairs={{0,2},{2,0},{1,3},{3,1},{4,6},{6,4},{5,7},{7,5},{8,10},{10,8},{9,1... | collective-permute-start | bytes 3145736 | tf_op jit(solution)/shard_map/ppermute | solution.py:34
  298.2 41.6 %collective-permute-start.47 = (bf16[2,2,128,1024]{3,2,1,0:T(8,128)(2,1)S(1)}, bf16[2,2,128,1024]{3,2,1,0:T(8,128)(2,1)S(1)}, u32[]{:S(2)}, u32[]{:S(2)}) collective-permute-start(bf16[2,2,128,1024]{3,2,1,0:T(8,128)(2,1)S(1)} %take.10), channel_id=1, source_target_pairs={{0,8},{4,12},{8,0},{12,4},{16,24},{20,28},{24,16},{28,20},{1,9},{5... | collective-permute-start | bytes 3145736 | tf_op jit(solution)/shard_map/ppermute | solution.py:43
  298.2 39.4 %collective-permute-start.46 = (bf16[2,2,128,768]{3,2,1,0:T(8,128)(2,1)S(1)}, bf16[2,2,128,768]{3,2,1,0:T(8,128)(2,1)S(1)}, u32[]{:S(2)}, u32[]{:S(2)}) collective-permute-start(bf16[2,2,128,768]{3,2,1,0:T(8,128)(2,1)S(1)} %get-tuple-element.272), channel_id=1, source_target_pairs={{0,16},{4,20},{8,24},{12,28},{16,0},{20,4},{24,8},{28,12},{1,17},{... | collective-permute-start | bytes 2359304 | tf_op jit(solution)/shard_map/ppermute | solution.py:43
  345.0 38.2 %collective-permute-start.49 = (bf16[2,128,1536]{2,1,0:T(8,128)(2,1)}, bf16[2,128,1536]{2,1,0:T(8,128)(2,1)}, u32[]{:S(2)}, u32[]{:S(2)}) collective-permute-start(bf16[2,128,1536]{2,1,0:T(8,128)(2,1)} %get-tuple-element.308), channel_id=1, source_target_pairs={{0,2},{2,0},{1,3},{3,1},{4,6},{6,4},{5,7},{7,5},{8,10},{10,8},{9,1... | collective-permute-start | bytes 2359304 | tf_op jit(solution)/shard_map/ppermute | solution.py:34
  346.5 24.4 %collective-permute-start.51 = (bf16[256,1024]{1,0:T(8,128)(2,1)}, bf16[256,1024]{1,0:T(8,128)(2,1)}, u32[]{:S(2)}, u32[]{:S(2)}) collective-permute-start(bf16[256,1024]{1,0:T(8,128)(2,1)} %get-tuple-element.282), channel_id=1, source_target_pairs={{0,8},{4,12},{8,0},{12,4},{16,24},{20,28},{24,16},{28,20},{1,9},{5... | collective-permute-start | bytes 1572872 | tf_op jit(solution)/shard_map/ppermute | solution.py:43
  348.0 37.2 %all-to-all-start.2 = ((bf16[8,40,1024]{2,1,0:T(8,128)(2,1)}), bf16[8,40,1024]{2,1,0:T(8,128)(2,1)}, u32[]{:S(2)}, u32[]{:S(2)}) async-start(bf16[8,40,1024]{2,1,0:T(8,128)(2,1)} %pack_back.1), calls=%async_computation.2 | async-start | bytes 1310720 | tf_op jit(solution)/shard_map/all_to_all | solution.py:75
  359.6 44.3 %collective-permute-start.56 = (bf16[384,1024]{1,0:T(8,128)(2,1)}, bf16[384,1024]{1,0:T(8,128)(2,1)}, u32[]{:S(2)}, u32[]{:S(2)}) collective-permute-start(bf16[384,1024]{1,0:T(8,128)(2,1)} %copy-done.72), channel_id=1, source_target_pairs={{0,16},{4,20},{8,24},{12,28},{16,0},{20,4},{24,8},{28,12},{1,17},{... | collective-permute-start | bytes 2359304 | tf_op jit(solution)/shard_map/ppermute | solution.py:43
  371.0 52.3 %collective-permute-start.55 = (bf16[2,2,128,1024]{3,2,1,0:T(8,128)(2,1)}, bf16[2,2,128,1024]{3,2,1,0:T(8,128)(2,1)}, u32[]{:S(2)}, u32[]{:S(2)}) collective-permute-start(bf16[2,2,128,1024]{3,2,1,0:T(8,128)(2,1)} %copy-done.57), channel_id=1, source_target_pairs={{0,8},{4,12},{8,0},{12,4},{16,24},{20,28},{24,16},{28,20},{1,9},{5... | collective-permute-start | bytes 3145736 | tf_op jit(solution)/shard_map/ppermute | solution.py:43
  388.1 55.1 %collective-permute-start.53 = (bf16[2,128,1536]{2,1,0:T(8,128)(2,1)}, bf16[2,128,1536]{2,1,0:T(8,128)(2,1)}, u32[]{:S(2)}, u32[]{:S(2)}) collective-permute-start(bf16[2,128,1536]{2,1,0:T(8,128)(2,1)} %pad_maximum_fusion.2), channel_id=1, source_target_pairs={{0,8},{4,12},{8,0},{12,4},{16,24},{20,28},{24,16},{28,20},{1,9},{5... | collective-permute-start | bytes 2359304 | tf_op jit(solution)/shard_map/ppermute | solution.py:43
  389.6 46.2 %collective-permute-start.59 = (f32[1,3072]{1,0:T(1,128)S(1)}, f32[1,3072]{1,0:T(1,128)S(1)}, u32[]{:S(2)}, u32[]{:S(2)}) collective-permute-start(f32[1,3072]{1,0:T(1,128)S(1)} %add.115), channel_id=1, source_target_pairs={{0,2},{2,0},{1,3},{3,1},{4,6},{6,4},{5,7},{7,5},{8,10},{10,8},{9,1... | collective-permute-start | bytes 36872 | tf_op jit(solution)/shard_map/ppermute | solution.py:34
  395.0 46.3 %collective-permute-start.54 = (bf16[128,1024]{1,0:T(8,128)(2,1)}, bf16[128,1024]{1,0:T(8,128)(2,1)}, u32[]{:S(2)}, u32[]{:S(2)}) collective-permute-start(bf16[128,1024]{1,0:T(8,128)(2,1)} %get-tuple-element.323), channel_id=1, source_target_pairs={{0,16},{4,20},{8,24},{12,28},{16,0},{20,4},{24,8},{28,12},{1,17},{... | collective-permute-start | bytes 786440 | tf_op jit(solution)/shard_map/ppermute | solution.py:43
  404.0 42.0 %collective-permute-start.52 = (bf16[128,1024]{1,0:T(8,128)(2,1)}, bf16[128,1024]{1,0:T(8,128)(2,1)S(1)}, u32[]{:S(2)}, u32[]{:S(2)}) collective-permute-start(bf16[128,1024]{1,0:T(8,128)(2,1)} %get-tuple-element.326), channel_id=1, source_target_pairs={{0,16},{4,20},{8,24},{12,28},{16,0},{20,4},{24,8},{28,12},{1,17},{... | collective-permute-start | bytes 786440 | tf_op jit(solution)/shard_map/ppermute | solution.py:43
  428.5 27.5 %all-to-all-start.3 = ((bf16[8,32,1024]{2,1,0:T(8,128)(2,1)}), bf16[8,32,1024]{2,1,0:T(8,128)(2,1)}, u32[]{:S(2)}, u32[]{:S(2)}) async-start(bf16[8,32,1024]{2,1,0:T(8,128)(2,1)} %bitcast.33), calls=%async_computation.3 | async-start | bytes 1048576 | tf_op jit(solution)/shard_map/all_to_all | solution.py:75
  (124 other events, 976.3 us)

commit v5 on v4

--- a/solution.py
+++ b/solution.py
@@ -119,7 +119,7 @@
 
 
 def light(name):
-    amount = WINDOWS.get(name, 0.05) * 0.1
+    amount = WINDOWS.get(name, 0.05) * 1.0
     return pl.CostEstimate(
         flops=int(amount * 1.15e9), bytes_accessed=int(amount * 3.69e6), transcendentals=0
     )
@@ -1011,8 +1011,8 @@
         act_back(after(rows_of, out_own), down_other, other_at, BF16)
         for rows_of in (grad_z, grad_far)
     ]
-    attention_other, got_act[1], got_gate_x, out_own, *far_sent = together(
-        attention_other, got_act[1], got_gate_x, out_own, *far_sent
+    attention_other, got_gate_x, out_own, *far_sent = together(
+        attention_other, got_gate_x, out_own, *far_sent
     )
     out_kept, out_sent = product_onto(
         attention_other, output_weight, 1 - row, query_part, out_own, features // 2, "out_proj"
@@ -1035,6 +1035,7 @@
         ],
         "grad_all",
     )
+    got_square, got_act[1] = together(got_square, got_act[1])
     normed_mid, inverse_mid = local_call(
         normed_kernel,
         (stream_mid, square_mid, got_square, gain_mid),

time: 470 us -> 456 us (0.970)
  local copies, waits for them, and re-layouts: 48.8 us -> 38.3 us
  Pallas kernels: 149 us -> 143 us
    unnamed x166 -> x156, local copies, waits for them, and re-layouts: 38.2 us -> 28.8 us
  transfers between devices with their start and end apart: 65 -> 65, of which waited for: 32 -> 33; matrix products, arithmetic and copies ran while one was open for 5% -> 4% of each run, Pallas kernels for 28% -> 28%
where the time goes in v5:
time: 456 us; the launch traced here: 451 us
  waiting for transfers between devices  179 us (39%)
  Pallas kernels  143 us (31%)
  starting transfers between devices  73.8 us (16%)
  local copies, waits for them, and re-layouts  38.3 us (8%)
  other arithmetic  15.2 us (3%)
    pallas_call x40, Pallas kernels, grid_call(): pl.pallas_call(kernel, grid_spec=pltpu.PrefetchScalarGridSpec(num_scalar_...  104 us
    ppermute x24, waiting for transfers between devices, swap_dp(): return lax.ppermute(value, 'dp', [(i, i ^ bit) for i in range(count)])  90.2 us
    ppermute x21, waiting for transfers between devices, swap_row(): return lax.ppermute(value, 'row', [(0, 1), (1, 0)])  75.4 us
    ppermute x24, starting transfers between devices, swap_dp(): return lax.ppermute(value, 'dp', [(i, i ^ bit) for i in range(count)])  29.8 us
    unnamed x156, local copies, waits for them, and re-layouts  28.8 us
    ppermute x21, starting transfers between devices, swap_row(): return lax.ppermute(value, 'row', [(0, 1), (1, 0)])  22.9 us
    pallas_call x23, Pallas kernels, local_call(): pl.pallas_call(kernel, out_shape=[jax.ShapeDtypeStruct(shape, dtype) for...  20.1 us
    all_to_all x4, starting transfers between devices, exchange(): return lax.all_to_all(value, 'dp', split_axis=0, concat_axis=0, tiled=True)  19.4 us
  transfers between devices with their start and end apart: 65, of which 33 were waited for; matrix products, arithmetic and copies ran while one was open for 4% of the time, Pallas kernels for 28%

profile of v5, /device:TPU:0, one launch (start us, length us, event | category | flops | bytes accessed | tf_op | source)
XLA Modules:
  0.0 451.2 jit_solution(6563661502684007498)
XLA Ops:
  5.5 5.8 %all-to-all-start = ((bf16[8,32,1024]{2,1,0:T(8,128)(2,1)}), bf16[8,32,1024]{2,1,0:T(8,128)(2,1)S(1)}, u32[]{:S(2)}, u32[]{:S(2)}) async-start(bf16[8,32,1024]{2,1,0:T(8,128)(2,1)} %bitcast.1), calls=%async_computation | async-start | bytes 1048576 | tf_op jit(solution)/shard_map/all_to_all | solution.py:75
  16.3 7.6 %collective-permute-done.refs_0_ = bf16[512,768]{1,0:T(8,128)(2,1)S(1)} collective-permute-done((bf16[512,768]{1,0:T(8,128)(2,1)S(1)}, bf16[512,768]{1,0:T(8,128)(2,1)S(1)}, u32[]{:S(2)}, u32[]{:S(2)}) %collective-permute-start) | collective-permute-done | bytes 786464 | tf_op jit(solution)/shard_map/ppermute | solution.py:34
  25.7 5.3 %all-to-all-start.1 = ((bf16[8,32,1024]{2,1,0:T(8,128)(2,1)}), bf16[8,32,1024]{2,1,0:T(8,128)(2,1)}, u32[]{:S(2)}, u32[]{:S(2)}) async-start(bf16[8,32,1024]{2,1,0:T(8,128)(2,1)} %bitcast.101), calls=%async_computation.1 | async-start | bytes 1048576 | tf_op jit(solution)/shard_map/all_to_all | solution.py:75
  31.4 8.6 %collective-permute-done.2.refs_2_ = bf16[512,768]{1,0:T(8,128)(2,1)} collective-permute-done((bf16[512,768]{1,0:T(8,128)(2,1)S(1)}, bf16[512,768]{1,0:T(8,128)(2,1)}, u32[]{:S(2)}, u32[]{:S(2)}) %collective-permute-start.2) | collective-permute-done | bytes 786464 | tf_op jit(solution)/shard_map/ppermute | solution.py:34
  57.7 11.4 %collective-permute-done.4 = f32[8,512]{1,0:T(8,128)S(1)} collective-permute-done((f32[8,512]{1,0:T(8,128)S(1)}, f32[8,512]{1,0:T(8,128)S(1)}, u32[]{:S(2)}, u32[]{:S(2)}) %collective-permute-start.4) | collective-permute-done | bytes 16416 | tf_op jit(solution)/shard_map/ppermute | solution.py:34
  72.3 7.2 %attend.1.left_ref.refs_0_ = bf16[512,512]{1,0:T(8,128)(2,1)S(1)} custom-call(f32[512,1024]{1,0:T(8,128)S(1)} %heads_kept.1.query_own.key_own.value_own, bf16[512,1024]{1,0:T(8,128)(2,1)S(1)} %collective-permute-done.3.query_got.key_got.value_got, f32[512,1024]{1,0:T(8,128)S(1)} %heads_kept.1.query_own.key_own.value_own, ...), custom_call_target="tpu_custom_call" | custom-call | flops 2300000000 | bytes 7380000 | tf_op jit(solution)/shard_map/attend/pallas_call | solution.py:845
  101.4 7.9 %collective-permute-done.13.refs_7_ = bf16[256,768]{1,0:T(8,128)(2,1)S(1)} collective-permute-done((bf16[256,768]{1,0:T(8,128)(2,1)S(1)}, bf16[256,768]{1,0:T(8,128)(2,1)S(1)}, u32[]{:S(2)}, u32[]{:S(2)}) %collective-permute-start.13) | collective-permute-done | bytes 393248 | tf_op jit(solution)/shard_map/ppermute | solution.py:34
  145.8 8.0 %collective-permute-done.24.refs_6_ = bf16[256,768]{1,0:T(8,128)(2,1)} collective-permute-done((bf16[256,768]{1,0:T(8,128)(2,1)}, bf16[256,768]{1,0:T(8,128)(2,1)}, u32[]{:S(2)}, u32[]{:S(2)}) %collective-permute-start.24) | collective-permute-done | bytes 393248 | tf_op jit(solution)/shard_map/ppermute | solution.py:34
  153.8 10.6 %gate_and_up.1 = (bf16[1024,768]{1,0:T(8,128)(2,1)S(1)}, bf16[1024,768]{1,0:T(8,128)(2,1)S(1)}, bf16[1024,768]{1,0:T(8,128)(2,1)S(1)}) custom-call(s32[3]{0:T(128)S(1)} %add_add_fusion.picks, bf16[1024,2048]{1,0:T(8,128)(2,1)S(1)} %mid_all.1.mid_ref.left_ref, bf16[1024,3072]{1,0:T(8,128)(2,1)} %gate_ref.5, bf16[1024,3072]{1,0:T(8,128)(2,1)} %up_ref.5, ...), custom_call_target="tpu_custom_call" | custom-call | flops 3449999872 | bytes 11070000 | tf_op jit(solution)/shard_map/gate_and_up/pallas_call | solution.py:155
  165.0 6.3 %mid_sent.1 = (bf16[512,1024]{1,0:T(8,128)(2,1)S(1)}, bf16[512,1024]{1,0:T(8,128)(2,1)S(1)}) custom-call(s32[3]{0:T(128)S(1)} %add_add_fusion.picks, bf16[1024,768]{1,0:T(8,128)(2,1)S(1)} %get-tuple-element.231.gate_grad_ref.right_ref, bf16[1024,768]{1,0:T(8,128)(2,1)S(1)} %get-tuple-element.243.up_grad_ref.right_ref, bf16[1024,3072]{1,0:T(8,128)(2,1)} %gate_ref.5, ...), custom_call_target="tpu_custom_call" | custom-call | flops 3449999872 | bytes 11070000 | tf_op jit(solution)/shard_map/mid_sent/pallas_call | solution.py:155
  178.6 6.3 %mid_kept.1 = (f32[512,1024]{1,0:T(8,128)S(1)}, f32[512,1024]{1,0:T(8,128)S(1)}) custom-call(s32[3]{0:T(128)S(1)} %add_add_fusion.picks, bf16[1024,768]{1,0:T(8,128)(2,1)S(1)} %get-tuple-element.231.gate_grad_ref.right_ref, bf16[1024,768]{1,0:T(8,128)(2,1)S(1)} %get-tuple-element.243.up_grad_ref.right_ref, bf16[1024,3072]{1,0:T(8,128)(2,1)} %gate_ref.5, ...), custom_call_target="tpu_custom_call" | custom-call | flops 1724999936 | bytes 5535000 | tf_op jit(solution)/shard_map/mid_kept/pallas_call | solution.py:155
  185.0 15.6 %collective-permute-done.28.refs_1_ = bf16[1024,768]{1,0:T(8,128)(2,1)S(1)} collective-permute-done((bf16[1024,768]{1,0:T(8,128)(2,1)S(1)}, bf16[1024,768]{1,0:T(8,128)(2,1)S(1)}, u32[]{:S(2)}, u32[]{:S(2)}) %collective-permute-start.28) | collective-permute-done | bytes 1572896 | tf_op jit(solution)/shard_map/ppermute | solution.py:34
  213.1 4.6 %down_first.1 = bf16[1536,1024]{1,0:T(8,128)(2,1)S(1)} custom-call(s32[1]{0:T(128)} %constant.157.clone.1.picks, bf16[1024,1536]{1,0:T(8,128)(2,1)S(1)} %act_all.1.left_ref.act_ref, bf16[1024,1024]{1,0:T(8,128)(2,1)S(1)} %copy-done.41), custom_call_target="tpu_custom_call" | custom-call | flops 3449999872 | bytes 11070000 | tf_op jit(solution)/shard_map/down_first/pallas_call | solution.py:155
  247.2 5.7 %down_proj.1 = (f32[512,1024]{1,0:T(8,128)S(1)}, bf16[256,1024]{1,0:T(8,128)(2,1)S(1)}, bf16[256,1024]{1,0:T(8,128)(2,1)S(1)}) custom-call(s32[2]{0:T(128)S(1)} %pad_add_fusion.4.picks, bf16[1024,1536]{1,0:T(8,128)(2,1)S(1)} %copy-done.15, bf16[3072,1024]{1,0:T(8,128)(2,1)} %other_ref.1, bf16[3072,1024]{1,0:T(8,128)(2,1)} %other_ref.1), custom_call_target="tpu_custom_call" | custom-call | flops 57500000 | bytes 184500 | tf_op jit(solution)/shard_map/down_proj/pallas_call | solution.py:155
  253.0 20.1 %collective-permute-done.38.refs_2_ = bf16[2,2,128,768]{3,2,1,0:T(8,128)(2,1)S(1)} collective-permute-done((bf16[2,2,128,768]{3,2,1,0:T(8,128)(2,1)S(1)}, bf16[2,2,128,768]{3,2,1,0:T(8,128)(2,1)S(1)}, u32[]{:S(2)}, u32[]{:S(2)}) %collective-permute-start.38) | collective-permute-done | bytes 786464 | tf_op jit(solution)/shard_map/ppermute | solution.py:43
  274.6 11.8 %attend_back.1 = (bf16[512,1024]{1,0:T(8,128)(2,1)S(1)}, f32[2,128]{1,0:T(2,128)S(1)}) custom-call(f32[512,1024]{1,0:T(8,128)S(1)} %heads_kept.1.query_own.key_own.value_own, bf16[512,1024]{1,0:T(8,128)(2,1)S(1)} %collective-permute-done.3.query_got.key_got.value_got, f32[512,1024]{1,0:T(8,128)S(1)} %heads_kept.1.query_own.key_own.value_own, ...), custom_call_target="tpu_custom_call" | custom-call | flops 2300000000 | bytes 7380000 | tf_op jit(solution)/shard_map/attend_back/pallas_call | solution.py:860
  299.5 10.3 %collective-permute-done.43.keep_got.send_got = bf16[2,384,1024]{2,1,0:T(8,128)(2,1)S(1)} collective-permute-done((bf16[2,384,1024]{2,1,0:T(8,128)(2,1)S(1)}, bf16[2,384,1024]{2,1,0:T(8,128)(2,1)S(1)}, u32[]{:S(2)}, u32[]{:S(2)}) %collective-permute-start.43) | collective-permute-done | bytes 1572896 | tf_op jit(solution)/shard_map/ppermute | solution.py:43
  322.3 10.4 %collective-permute-done.46.refs_3_ = bf16[2,2,128,768]{3,2,1,0:T(8,128)(2,1)S(1)} collective-permute-done((bf16[2,2,128,768]{3,2,1,0:T(8,128)(2,1)S(1)}, bf16[2,2,128,768]{3,2,1,0:T(8,128)(2,1)S(1)}, u32[]{:S(2)}, u32[]{:S(2)}) %collective-permute-start.46) | collective-permute-done | bytes 786464 | tf_op jit(solution)/shard_map/ppermute | solution.py:43
  355.8 9.1 %collective-permute-done.48.keep_got.send_got = bf16[2,128,1024]{2,1,0:T(8,128)(2,1)S(1)} collective-permute-done((bf16[2,128,1024]{2,1,0:T(8,128)(2,1)}, bf16[2,128,1024]{2,1,0:T(8,128)(2,1)S(1)}, u32[]{:S(2)}, u32[]{:S(2)}) %collective-permute-start.48) | collective-permute-done | bytes 524320 | tf_op jit(solution)/shard_map/ppermute | solution.py:43
  365.7 8.9 %collective-permute-done.50.keep_got.send_got = bf16[2,128,1024]{2,1,0:T(8,128)(2,1)S(1)} collective-permute-done((bf16[2,128,1024]{2,1,0:T(8,128)(2,1)S(1)}, bf16[2,128,1024]{2,1,0:T(8,128)(2,1)S(1)}, u32[]{:S(2)}, u32[]{:S(2)}) %collective-permute-start.50) | collective-permute-done | bytes 524320 | tf_op jit(solution)/shard_map/ppermute | solution.py:43
  386.6 9.2 %collective-permute-done.56.got_ref = bf16[384,1024]{1,0:T(8,128)(2,1)} collective-permute-done((bf16[384,1024]{1,0:T(8,128)(2,1)}, bf16[384,1024]{1,0:T(8,128)(2,1)}, u32[]{:S(2)}, u32[]{:S(2)}) %collective-permute-start.56) | collective-permute-done | bytes 786464 | tf_op jit(solution)/shard_map/ppermute | solution.py:43
  395.8 12.0 %collective-permute-done.55.keep_got.send_got = bf16[2,2,128,1024]{3,2,1,0:T(8,128)(2,1)S(1)} collective-permute-done((bf16[2,2,128,1024]{3,2,1,0:T(8,128)(2,1)}, bf16[2,2,128,1024]{3,2,1,0:T(8,128)(2,1)S(1)}, u32[]{:S(2)}, u32[]{:S(2)}) %collective-permute-start.55) | collective-permute-done | bytes 1048608 | tf_op jit(solution)/shard_map/ppermute | solution.py:43
  433.7 8.0 %all-to-all-done.3 = bf16[8,32,1024]{2,1,0:T(8,128)(2,1)} async-done(((bf16[8,32,1024]{2,1,0:T(8,128)(2,1)}), bf16[8,32,1024]{2,1,0:T(8,128)(2,1)}, u32[]{:S(2)}, u32[]{:S(2)}) %all-to-all-start.3) | async-done | bytes 524320 | tf_op jit(solution)/shard_map/all_to_all | solution.py:75
  441.6 4.7 %collective-permute-done.60.got_ref = bf16[128,1024]{1,0:T(8,128)(2,1)S(1)} collective-permute-done((bf16[128,1024]{1,0:T(8,128)(2,1)}, bf16[128,1024]{1,0:T(8,128)(2,1)S(1)}, u32[]{:S(2)}, u32[]{:S(2)}) %collective-permute-start.60) | collective-permute-done | bytes 262176 | tf_op jit(solution)/shard_map/ppermute | solution.py:43
  (383 shorter events, 233.6 us)
Async XLA Ops:
  13.1 26.9 %collective-permute-start.2 = (bf16[512,768]{1,0:T(8,128)(2,1)S(1)}, bf16[512,768]{1,0:T(8,128)(2,1)}, u32[]{:S(2)}, u32[]{:S(2)}) collective-permute-start(bf16[512,768]{1,0:T(8,128)(2,1)S(1)} %block_of.3), channel_id=1, source_target_pairs={{0,2},{2,0},{1,3},{3,1},{4,6},{6,4},{5,7},{7,5},{8,10},{10,8},{9,1... | collective-permute-start | bytes 2359304 | tf_op jit(solution)/shard_map/ppermute | solution.py:34
  44.2 25.0 %collective-permute-start.3 = (bf16[512,1024]{1,0:T(8,128)(2,1)}, bf16[512,1024]{1,0:T(8,128)(2,1)S(1)}, u32[]{:S(2)}, u32[]{:S(2)}) collective-permute-start(bf16[512,1024]{1,0:T(8,128)(2,1)} %heads_sent.1), channel_id=1, source_target_pairs={{0,2},{2,0},{1,3},{3,1},{4,6},{6,4},{5,7},{7,5},{8,10},{10,8},{9,1... | collective-permute-start | bytes 3145736 | tf_op jit(solution)/shard_map/ppermute | solution.py:34
  99.2 26.2 %collective-permute-start.16 = (bf16[512,768]{1,0:T(8,128)(2,1)}, bf16[512,768]{1,0:T(8,128)(2,1)}, u32[]{:S(2)}, u32[]{:S(2)}) collective-permute-start(bf16[512,768]{1,0:T(8,128)(2,1)} %collective-permute-done.2.refs_2_), channel_id=1, source_target_pairs={{0,4},{4,0},{8,12},{12,8},{16,20},{20,16},{24,28},{28,24},{1,5},{5... | collective-permute-start | bytes 2359304 | tf_op jit(solution)/shard_map/ppermute | solution.py:43
  164.5 36.1 %collective-permute-start.28 = (bf16[1024,768]{1,0:T(8,128)(2,1)S(1)}, bf16[1024,768]{1,0:T(8,128)(2,1)S(1)}, u32[]{:S(2)}, u32[]{:S(2)}) collective-permute-start(bf16[1024,768]{1,0:T(8,128)(2,1)S(1)} %get-tuple-element.233.refs_0_), channel_id=1, source_target_pairs={{0,2},{2,0},{1,3},{3,1},{4,6},{6,4},{5,7},{7,5},{8,10},{10,8},{9,1... | collective-permute-start | bytes 4718600 | tf_op jit(solution)/shard_map/ppermute | solution.py:34
  178.1 46.3 %collective-permute-start.34 = (bf16[2,2,2,128,768]{4,3,2,1,0:T(8,128)(2,1)S(1)}, bf16[2,2,2,128,768]{4,3,2,1,0:T(8,128)(2,1)S(1)}, u32[]{:S(2)}, u32[]{:S(2)}) collective-permute-start(bf16[2,2,2,128,768]{4,3,2,1,0:T(8,128)(2,1)S(1)} %take.6), channel_id=1, source_target_pairs={{0,4},{4,0},{8,12},{12,8},{16,20},{20,16},{24,28},{28,24},{1,5},{5... | collective-permute-start | bytes 4718600 | tf_op jit(solution)/shard_map/ppermute | solution.py:43
  230.8 55.7 %collective-permute-start.37 = (bf16[2,2,2,128,768]{4,3,2,1,0:T(8,128)(2,1)}, bf16[2,2,2,128,768]{4,3,2,1,0:T(8,128)(2,1)}, u32[]{:S(2)}, u32[]{:S(2)}) collective-permute-start(bf16[2,2,2,128,768]{4,3,2,1,0:T(8,128)(2,1)} %take.7), channel_id=1, source_target_pairs={{0,4},{4,0},{8,12},{12,8},{16,20},{20,16},{24,28},{28,24},{1,5},{5... | collective-permute-start | bytes 4718600 | tf_op jit(solution)/shard_map/ppermute | solution.py:43
  235.5 37.5 %collective-permute-start.38 = (bf16[2,2,128,768]{3,2,1,0:T(8,128)(2,1)S(1)}, bf16[2,2,128,768]{3,2,1,0:T(8,128)(2,1)S(1)}, u32[]{:S(2)}, u32[]{:S(2)}) collective-permute-start(bf16[2,2,128,768]{3,2,1,0:T(8,128)(2,1)S(1)} %get-tuple-element.259), channel_id=1, source_target_pairs={{0,16},{4,20},{8,24},{12,28},{16,0},{20,4},{24,8},{28,12},{1,17},{... | collective-permute-start | bytes 2359304 | tf_op jit(solution)/shard_map/ppermute | solution.py:43
  245.4 41.8 %collective-permute-start.39 = (bf16[2,2,128,1024]{3,2,1,0:T(8,128)(2,1)S(1)}, bf16[2,2,128,1024]{3,2,1,0:T(8,128)(2,1)S(1)}, u32[]{:S(2)}, u32[]{:S(2)}) collective-permute-start(bf16[2,2,128,1024]{3,2,1,0:T(8,128)(2,1)S(1)} %take.9), channel_id=1, source_target_pairs={{0,8},{4,12},{8,0},{12,4},{16,24},{20,28},{24,16},{28,20},{1,9},{5... | collective-permute-start | bytes 3145736 | tf_op jit(solution)/shard_map/ppermute | solution.py:43
  245.9 27.2 %collective-permute-start.36 = (bf16[512,512]{1,0:T(8,128)(2,1)S(1)}, bf16[512,512]{1,0:T(8,128)(2,1)S(1)}, u32[]{:S(2)}, u32[]{:S(2)}) collective-permute-start(bf16[512,512]{1,0:T(8,128)(2,1)S(1)} %product_nt.1), channel_id=1, source_target_pairs={{0,2},{2,0},{1,3},{3,1},{4,6},{6,4},{5,7},{7,5},{8,10},{10,8},{9,1... | collective-permute-start | bytes 1572872 | tf_op jit(solution)/shard_map/ppermute | solution.py:34
  252.9 33.6 %collective-permute-start.40 = (bf16[256,1024]{1,0:T(8,128)(2,1)S(1)}, bf16[256,1024]{1,0:T(8,128)(2,1)S(1)}, u32[]{:S(2)}, u32[]{:S(2)}) collective-permute-start(bf16[256,1024]{1,0:T(8,128)(2,1)S(1)} %get-tuple-element.268), channel_id=1, source_target_pairs={{0,1},{1,0},{2,3},{3,2},{4,5},{5,4},{6,7},{7,6},{8,9},{9,8},{10,11... | collective-permute-start | bytes 1572872 | tf_op jit(solution)/shard_map/ppermute | solution.py:38
  273.1 36.8 %collective-permute-start.43 = (bf16[2,384,1024]{2,1,0:T(8,128)(2,1)S(1)}, bf16[2,384,1024]{2,1,0:T(8,128)(2,1)S(1)}, u32[]{:S(2)}, u32[]{:S(2)}) collective-permute-start(bf16[2,384,1024]{2,1,0:T(8,128)(2,1)S(1)} %copy-done.49), channel_id=1, source_target_pairs={{0,4},{4,0},{8,12},{12,8},{16,20},{20,16},{24,28},{28,24},{1,5},{5... | collective-permute-start | bytes 4718600 | tf_op jit(solution)/shard_map/ppermute | solution.py:43
  287.2 24.6 %collective-permute-start.42 = (bf16[512,1024]{1,0:T(8,128)(2,1)S(1)}, bf16[512,1024]{1,0:T(8,128)(2,1)S(1)}, u32[]{:S(2)}, u32[]{:S(2)}) collective-permute-start(bf16[512,1024]{1,0:T(8,128)(2,1)S(1)} %get-tuple-element.277.right_ref.grads_ref), channel_id=1, source_target_pairs={{0,2},{2,0},{1,3},{3,1},{4,6},{6,4},{5,7},{7,5},{8,10},{10,8},{9,1... | collective-permute-start | bytes 3145736 | tf_op jit(solution)/shard_map/ppermute | solution.py:34
  292.1 42.6 %collective-permute-start.47 = (bf16[2,2,128,1024]{3,2,1,0:T(8,128)(2,1)S(1)}, bf16[2,2,128,1024]{3,2,1,0:T(8,128)(2,1)S(1)}, u32[]{:S(2)}, u32[]{:S(2)}) collective-permute-start(bf16[2,2,128,1024]{3,2,1,0:T(8,128)(2,1)S(1)} %take.10), channel_id=1, source_target_pairs={{0,8},{4,12},{8,0},{12,4},{16,24},{20,28},{24,16},{28,20},{1,9},{5... | collective-permute-start | bytes 3145736 | tf_op jit(solution)/shard_map/ppermute | solution.py:43
  292.2 40.5 %collective-permute-start.46 = (bf16[2,2,128,768]{3,2,1,0:T(8,128)(2,1)S(1)}, bf16[2,2,128,768]{3,2,1,0:T(8,128)(2,1)S(1)}, u32[]{:S(2)}, u32[]{:S(2)}) collective-permute-start(bf16[2,2,128,768]{3,2,1,0:T(8,128)(2,1)S(1)} %get-tuple-element.274), channel_id=1, source_target_pairs={{0,16},{4,20},{8,24},{12,28},{16,0},{20,4},{24,8},{28,12},{1,17},{... | collective-permute-start | bytes 2359304 | tf_op jit(solution)/shard_map/ppermute | solution.py:43
  315.2 35.6 %collective-permute-start.51 = (bf16[256,1024]{1,0:T(8,128)(2,1)}, bf16[256,1024]{1,0:T(8,128)(2,1)}, u32[]{:S(2)}, u32[]{:S(2)}) collective-permute-start(bf16[256,1024]{1,0:T(8,128)(2,1)} %get-tuple-element.284), channel_id=1, source_target_pairs={{0,8},{4,12},{8,0},{12,4},{16,24},{20,28},{24,16},{28,20},{1,9},{5... | collective-permute-start | bytes 1572872 | tf_op jit(solution)/shard_map/ppermute | solution.py:43
  338.4 36.2 %collective-permute-start.49 = (bf16[2,128,1536]{2,1,0:T(8,128)(2,1)}, bf16[2,128,1536]{2,1,0:T(8,128)(2,1)}, u32[]{:S(2)}, u32[]{:S(2)}) collective-permute-start(bf16[2,128,1536]{2,1,0:T(8,128)(2,1)} %get-tuple-element.310), channel_id=1, source_target_pairs={{0,2},{2,0},{1,3},{3,1},{4,6},{6,4},{5,7},{7,5},{8,10},{10,8},{9,1... | collective-permute-start | bytes 2359304 | tf_op jit(solution)/shard_map/ppermute | solution.py:34
  339.9 39.1 %all-to-all-start.2 = ((bf16[8,40,1024]{2,1,0:T(8,128)(2,1)}), bf16[8,40,1024]{2,1,0:T(8,128)(2,1)}, u32[]{:S(2)}, u32[]{:S(2)}) async-start(bf16[8,40,1024]{2,1,0:T(8,128)(2,1)} %copy-done.29), calls=%async_computation.2 | async-start | bytes 1310720 | tf_op jit(solution)/shard_map/all_to_all | solution.py:75
  344.2 51.6 %collective-permute-start.56 = (bf16[384,1024]{1,0:T(8,128)(2,1)}, bf16[384,1024]{1,0:T(8,128)(2,1)}, u32[]{:S(2)}, u32[]{:S(2)}) collective-permute-start(bf16[384,1024]{1,0:T(8,128)(2,1)} %copy-done.66), channel_id=1, source_target_pairs={{0,16},{4,20},{8,24},{12,28},{16,0},{20,4},{24,8},{28,12},{1,17},{... | collective-permute-start | bytes 2359304 | tf_op jit(solution)/shard_map/ppermute | solution.py:43
  350.8 57.0 %collective-permute-start.55 = (bf16[2,2,128,1024]{3,2,1,0:T(8,128)(2,1)}, bf16[2,2,128,1024]{3,2,1,0:T(8,128)(2,1)S(1)}, u32[]{:S(2)}, u32[]{:S(2)}) collective-permute-start(bf16[2,2,128,1024]{3,2,1,0:T(8,128)(2,1)} %take.11), channel_id=1, source_target_pairs={{0,8},{4,12},{8,0},{12,4},{16,24},{20,28},{24,16},{28,20},{1,9},{5... | collective-permute-start | bytes 3145736 | tf_op jit(solution)/shard_map/ppermute | solution.py:43
  376.5 52.3 %collective-permute-start.53 = (bf16[2,128,1536]{2,1,0:T(8,128)(2,1)}, bf16[2,128,1536]{2,1,0:T(8,128)(2,1)}, u32[]{:S(2)}, u32[]{:S(2)}) collective-permute-start(bf16[2,128,1536]{2,1,0:T(8,128)(2,1)} %pad_maximum_fusion.2), channel_id=1, source_target_pairs={{0,8},{4,12},{8,0},{12,4},{16,24},{20,28},{24,16},{28,20},{1,9},{5... | collective-permute-start | bytes 2359304 | tf_op jit(solution)/shard_map/ppermute | solution.py:43
  384.3 42.6 %collective-permute-start.54 = (bf16[128,1024]{1,0:T(8,128)(2,1)}, bf16[128,1024]{1,0:T(8,128)(2,1)}, u32[]{:S(2)}, u32[]{:S(2)}) collective-permute-start(bf16[128,1024]{1,0:T(8,128)(2,1)} %get-tuple-element.325), channel_id=1, source_target_pairs={{0,16},{4,20},{8,24},{12,28},{16,0},{20,4},{24,8},{28,12},{1,17},{... | collective-permute-start | bytes 786440 | tf_op jit(solution)/shard_map/ppermute | solution.py:43
  384.7 36.3 %collective-permute-start.59 = (f32[1,3072]{1,0:T(1,128)S(1)}, f32[1,3072]{1,0:T(1,128)S(1)}, u32[]{:S(2)}, u32[]{:S(2)}) collective-permute-start(f32[1,3072]{1,0:T(1,128)S(1)} %add.115), channel_id=1, source_target_pairs={{0,2},{2,0},{1,3},{3,1},{4,6},{6,4},{5,7},{7,5},{8,10},{10,8},{9,1... | collective-permute-start | bytes 36872 | tf_op jit(solution)/shard_map/ppermute | solution.py:34
  395.8 35.8 %collective-permute-start.52 = (bf16[128,1024]{1,0:T(8,128)(2,1)}, bf16[128,1024]{1,0:T(8,128)(2,1)S(1)}, u32[]{:S(2)}, u32[]{:S(2)}) collective-permute-start(bf16[128,1024]{1,0:T(8,128)(2,1)} %get-tuple-element.328), channel_id=1, source_target_pairs={{0,16},{4,20},{8,24},{12,28},{16,0},{20,4},{24,8},{28,12},{1,17},{... | collective-permute-start | bytes 786440 | tf_op jit(solution)/shard_map/ppermute | solution.py:43
  413.0 28.6 %all-to-all-start.3 = ((bf16[8,32,1024]{2,1,0:T(8,128)(2,1)}), bf16[8,32,1024]{2,1,0:T(8,128)(2,1)}, u32[]{:S(2)}, u32[]{:S(2)}) async-start(bf16[8,32,1024]{2,1,0:T(8,128)(2,1)} %bitcast.33), calls=%async_computation.3 | async-start | bytes 1048576 | tf_op jit(solution)/shard_map/all_to_all | solution.py:75
  (119 other events, 964.3 us)
